TPU v7x, 128 devices: a whole 4x4x4 slice. The times are simulated.
128 devices in a mesh: stream: 32 (over x_hi, y, z), span: 4 (over x_lo, core).
Axes of the slice: x: 4 (x_hi: 2, x_lo: 2; x = x_hi * 2 + x_lo), y: 4, z: 4, core: 2. Of those that a mesh axis runs over, the one named last changes fastest.
Arguments:
- velocity: float32 [3, 256, 128, 512], P(None, 'stream', None, 'span'), may hold values from -3 to 3
- fraction: float32 [256, 128, 512], P('stream', None, 'span'), may hold values from 0 to 1
- pressure_now: float32 [256, 128, 512], P('stream', None, 'span'), may hold values from -6 to 6
- pressure_old: float32 [256, 128, 512], P('stream', None, 'span'), may hold values from -6 to 6
- inflow: float32 [2, 128], replicated, may hold values from 0 to 1
Outputs:
- velocity_out: float32 [3, 256, 128, 512], P(None, 'stream', None, 'span')
- fraction_out: float32 [256, 128, 512], P('stream', None, 'span')
- pressure_out: float32 [256, 128, 512], P('stream', None, 'span')
- pressure_prev: float32 [256, 128, 512], P('stream', None, 'span')
All inputs are finite; a program needn't handle non-finite values.
Results may differ from a plain program's by a relative error of at most 0.0001.
Values sent between devices are 32-bit elements; how exact they have to be, the bound alone decides.
No kernel may reach another device: no remote copies, remote signals or barrier semaphores. Data moves between devices by JAX's collectives and lax.ppermute only.
A program may use at most 128 MiB of HBM per device.

v0:
```python
import math

import jax
import jax.numpy as jnp
from jax import lax
from jax.sharding import PartitionSpec as P

NZ = 512
SWEEPS = 7
STEPS = 2


TIME_STEP = 0.1
RHO_LIQUID = 1.0
RHO_GAS = 0.5
MU_LIQUID = 0.05
MU_GAS = 0.02
TENSION = 0.5
WALL_SPEED = 1.0
SLOPE_FLOOR = 0.5
DIRECTIONS = ((1, 0, 0), (0, 1, 0), (0, 0, 1))


def with_halo(block, sides, width, periodic):
    for axis, dim in sides:
        count = lax.axis_size(axis)
        forward = [(i, i + 1) for i in range(count - 1)]
        if periodic:
            forward.append((count - 1, 0))
        backward = [(target, source) for source, target in forward]
        low = lax.ppermute(
            lax.slice_in_dim(block, block.shape[dim] - width, None, axis=dim), axis, forward
        )
        high = lax.ppermute(lax.slice_in_dim(block, 0, width, axis=dim), axis, backward)
        block = jnp.concatenate([low, block, high], axis=dim)
    return block


def shifted(field, first_off, gap_off, span_off):
    return field[
        1 + first_off : field.shape[0] - 1 + first_off,
        1 + gap_off : field.shape[1] - 1 + gap_off,
        1 + span_off : field.shape[2] - 1 + span_off,
    ]


def central(field, axis):
    direction = DIRECTIONS[axis]
    ahead = shifted(field, direction[0], direction[1], direction[2])
    behind = shifted(field, -direction[0], -direction[1], -direction[2])
    return (ahead - behind) * 0.5


def second(field, axis):
    direction = DIRECTIONS[axis]
    ahead = shifted(field, direction[0], direction[1], direction[2])
    behind = shifted(field, -direction[0], -direction[1], -direction[2])
    return ahead - 2.0 * shifted(field, 0, 0, 0) + behind


def mixed(field, one_axis, other_axis):
    first_dir = DIRECTIONS[one_axis]
    other_dir = DIRECTIONS[other_axis]
    total = jnp.zeros_like(shifted(field, 0, 0, 0))
    for sign_one in (1, -1):
        for sign_two in (1, -1):
            offsets = [sign_one * first_dir[k] + sign_two * other_dir[k] for k in range(3)]
            total = total + sign_one * sign_two * shifted(field, offsets[0], offsets[1], offsets[2])
    return total * 0.25


def close_ends(padded, inflow, first, last):
    zero_row = jnp.zeros_like(inflow[0])
    profile = jnp.stack([inflow[0], zero_row, zero_row, inflow[1], zero_row, zero_row])
    target = (6, 2, padded.shape[2], padded.shape[3])
    lower = jnp.broadcast_to(profile[:, None, :, None], target)
    keeping = jnp.asarray([1.0, 1.0, 1.0, 1.0, 0.0, 0.0], jnp.float32).reshape(6, 1, 1, 1)
    upper = jnp.broadcast_to(padded[:, -3:-2] * keeping, target)
    return jnp.concatenate(
        [
            jnp.where(first, lower, padded[:, :2]),
            padded[:, 2:-2],
            jnp.where(last, upper, padded[:, -2:]),
        ],
        axis=1,
    )


def pad_gap(padded):
    signs = jnp.asarray([-1.0, -1.0, -1.0, 1.0, 1.0, 1.0], jnp.float32).reshape(6, 1, 1, 1)
    offsets = jnp.asarray([2.0 * WALL_SPEED, 0.0, 0.0, 0.0, 0.0, 0.0], jnp.float32).reshape(
        6, 1, 1, 1
    )
    bottom = signs * padded[:, :, :1] + offsets
    top = signs * padded[:, :, -1:]
    return jnp.concatenate([bottom, padded, top], axis=2)


def predict(padded):
    speeds = [padded[0], padded[1], padded[2]]
    volume = padded[3]
    guess = 2.0 * padded[4] - padded[5]
    centre = [shifted(field, 0, 0, 0) for field in speeds]
    volume_centre = shifted(volume, 0, 0, 0)
    density = RHO_GAS + (RHO_LIQUID - RHO_GAS) * volume_centre
    kinematic = (MU_GAS + (MU_LIQUID - MU_GAS) * volume_centre) / density
    slopes = [central(volume, axis) for axis in range(3)]
    magnitude = jnp.maximum(
        jnp.sqrt(slopes[0] * slopes[0] + slopes[1] * slopes[1] + slopes[2] * slopes[2]), SLOPE_FLOOR
    )
    normals = [slope / magnitude for slope in slopes]
    laplace_volume = second(volume, 0) + second(volume, 1) + second(volume, 2)
    bending = jnp.zeros_like(volume_centre)
    for one_axis in range(3):
        for other_axis in range(3):
            if one_axis == other_axis:
                hessian = second(volume, one_axis)
            else:
                hessian = mixed(volume, one_axis, other_axis)
            bending = bending + normals[one_axis] * normals[other_axis] * hessian
    curvature = -(laplace_volume - bending) / magnitude
    provisional = []
    for comp in range(3):
        field = speeds[comp]
        transport = jnp.zeros_like(volume_centre)
        diffusion = jnp.zeros_like(volume_centre)
        for axis in range(3):
            curve = second(field, axis)
            transport = (
                transport
                + centre[axis] * central(field, axis)
                - 0.5 * jnp.abs(centre[axis]) * curve
            )
            diffusion = diffusion + curve
        tension = TENSION * curvature * slopes[comp] / density
        provisional.append(
            centre[comp] + TIME_STEP * (-transport + kinematic * diffusion + tension)
        )
    guess_slopes = [central(guess, axis) for axis in range(3)]
    fluxes = [
        RHO_GAS / TIME_STEP * provisional[axis] + (1.0 - RHO_GAS / density) * guess_slopes[axis]
        for axis in range(3)
    ]
    net = jnp.zeros_like(volume_centre)
    for axis in range(3):
        direction = DIRECTIONS[axis]
        speed_ahead = shifted(speeds[axis], direction[0], direction[1], direction[2])
        speed_behind = shifted(speeds[axis], -direction[0], -direction[1], -direction[2])
        volume_ahead = shifted(volume, direction[0], direction[1], direction[2])
        volume_behind = shifted(volume, -direction[0], -direction[1], -direction[2])
        face_ahead = (centre[axis] + speed_ahead) * 0.5
        face_behind = (speed_behind + centre[axis]) * 0.5
        leaving = (
            jnp.maximum(face_ahead, 0.0) * volume_centre
            + jnp.minimum(face_ahead, 0.0) * volume_ahead
        )
        entering = (
            jnp.maximum(face_behind, 0.0) * volume_behind
            + jnp.minimum(face_behind, 0.0) * volume_centre
        )
        net = net + (leaving - entering)
    fraction_new = volume_centre - TIME_STEP * net
    return (provisional, fluxes, fraction_new, density, guess_slopes)


def interior(frame):
    return frame[1:-1, :, 1:-1]


def divergence(fluxes):
    first_part = (fluxes[0][2:, :, 1:-1] - fluxes[0][:-2, :, 1:-1]) * 0.5
    gap_flux = fluxes[1][1:-1, :, 1:-1]
    zero_row = jnp.zeros_like(gap_flux[:, :1])
    gap_part = (
        jnp.concatenate([gap_flux[:, 1:], zero_row], axis=1)
        - jnp.concatenate([zero_row, gap_flux[:, :-1]], axis=1)
    ) * 0.5
    span_part = (fluxes[2][1:-1, :, 2:] - fluxes[2][1:-1, :, :-2]) * 0.5
    return first_part + gap_part + span_part


def transform_tables():
    index = jnp.arange(NZ, dtype=jnp.int32)
    wave = jnp.where(index <= NZ // 2, index, index - NZ // 2)
    phase = index[:, None] * wave[None, :] % NZ
    angle = phase.astype(jnp.float32) * (2.0 * math.pi / NZ)
    forward = jnp.where(index[None, :] <= NZ // 2, jnp.cos(angle), jnp.sin(angle))
    weight = jnp.where((index == 0) | (index == NZ // 2), 1.0 / NZ, 2.0 / NZ).astype(jnp.float32)
    inverse = jnp.transpose(forward) * weight[:, None]
    eigen = 2.0 - 2.0 * jnp.cos(wave.astype(jnp.float32) * (2.0 * math.pi / NZ))
    return (forward, inverse, eigen)


def gap_pair(field):
    above = jnp.concatenate([field[..., 1:], field[..., -1:]], axis=-1)
    below = jnp.concatenate([field[..., :1], field[..., :-1]], axis=-1)
    return above + below


def pressure_slopes(cycle):
    cycle = jnp.concatenate([cycle[:, :1], cycle, cycle[:, -1:]], axis=1)
    return [central(cycle, axis) for axis in range(3)]


def correct(provisional, density, guess_slopes, slopes):
    inner_density = interior(density)
    speeds = []
    for axis in range(3):
        change = slopes[axis] / RHO_GAS + (1.0 / inner_density - 1.0 / RHO_GAS) * interior(
            guess_slopes[axis]
        )
        speeds.append(interior(provisional[axis]) - TIME_STEP * change)
    return jnp.stack(speeds)


def to_modes(source, forward, offset):
    own_rows = lax.dynamic_slice_in_dim(forward, offset, source.shape[2], 0)
    return lax.psum_scatter(
        jnp.einsum("xyz,zc->cxy", source, own_rows, precision=lax.Precision.HIGHEST),
        "span",
        scatter_dimension=0,
        tiled=True,
    )


def from_modes(modal, inverse, offset):
    width_z = modal.shape[0]
    own_columns = lax.dynamic_slice_in_dim(inverse, offset, width_z, 1)
    return jnp.einsum(
        "cxy,cz->xyz",
        lax.all_gather(modal, "span", axis=0, tiled=True),
        own_columns,
        precision=lax.Precision.HIGHEST,
    )


def relax(spectrum, diagonal):
    modal = -spectrum / diagonal
    for sweep in range(SWEEPS - 1):
        padded = with_halo(modal, (("stream", 1),), 1, False)
        beside_all = padded[:, 2:] + padded[:, :-2] + gap_pair(modal)
        modal = (beside_all - spectrum) / diagonal
    return modal


def per_device(velocity, fraction, pressure_now, pressure_old, inflow):
    stream_index = lax.axis_index("stream")
    stream_count = lax.axis_size("stream")
    first = stream_index == 0
    last = stream_index == stream_count - 1
    width_z = fraction.shape[2]
    offset = lax.axis_index("span") * width_z
    forward, inverse, eigen = transform_tables()
    local_eigen = lax.dynamic_slice_in_dim(eigen, offset, width_z, 0)
    diagonal = (4.0 + local_eigen)[:, None, None]
    state = jnp.concatenate(
        [velocity, fraction[None], pressure_now[None], pressure_old[None]], axis=0
    )
    for step in range(STEPS):
        padded = with_halo(state, (("stream", 1), ("span", 3)), 2, True)
        padded = pad_gap(close_ends(padded, inflow, first, last))
        provisional, fluxes, fraction_new, density, guess_slopes = predict(padded)
        source = divergence(fluxes)
        spectrum = to_modes(source, forward, offset)
        modal = relax(spectrum, diagonal)
        pressure = from_modes(modal, inverse, offset)
        cycle = with_halo(pressure, (("stream", 0), ("span", 2)), 1, True)
        cycle = jnp.concatenate(
            [jnp.where(first, 0.0, cycle[:1]), cycle[1:-1], jnp.where(last, 0.0, cycle[-1:])],
            axis=0,
        )
        speeds = correct(provisional, density, guess_slopes, pressure_slopes(cycle))
        state = jnp.concatenate(
            [speeds, interior(fraction_new)[None], pressure[None], state[4:5]], axis=0
        )
    return (state[:3], state[3], state[4], state[5])


def solution(mesh):
    return jax.shard_map(
        per_device,
        mesh=mesh,
        in_specs=(
            P(None, "stream", None, "span"),
            P("stream", None, "span"),
            P("stream", None, "span"),
            P("stream", None, "span"),
            P(),
        ),
        out_specs=(
            P(None, "stream", None, "span"),
            P("stream", None, "span"),
            P("stream", None, "span"),
            P("stream", None, "span"),
        ),
        check_vma=False,
    )
```

profile of v0, /device:TPU:7, one launch (start us, length us, event | category | flops | bytes accessed | tf_op | source)
XLA Modules:
  0.0 509.8 jit_solution(8274067826438726985)
XLA Ops:
  24.6 13.2 %collective-permute-done = f32[6,2,128,128]{2,3,1,0:T(8,128)} collective-permute-done((f32[6,2,128,128]{2,3,1,0:T(8,128)}, f32[6,2,128,128]{2,3,1,0:T(8,128)}, u32[]{:S(2)}, u32[]{:S(2)}) %collective-permute-start) | collective-permute-done | bytes 786464 | tf_op jit(solution)/shard_map/ppermute | solution.py:31
  54.2 9.9 %pad_maximum_fusion = f32[6,12,130,132]{2,3,1,0:T(8,128)} fusion(f32[6,12,1,132]{2,3,1,0:T(8,128)} %get-tuple-element.41, f32[6,2,128,132]{2,3,1,0:T(8,128)S(1)} %get-tuple-element.43, f32[6,8,128,132]{2,3,1,0:T(8,128)S(1)} %slice.1307, f32[6,2,128,132]{2,3,1,0:T(8,128)S(1)} %get-tuple-element.42, f32[6,12,1,132]{2,3,1,0:T(8,128)S(1)} %get-tuple-element.40), kind=kLoop, calls=%fused_computation | loop fusion | flops 4942080 | bytes 9884160 | tf_op jit(solution)/shard_map/concatenate | solution.py:96
  88.6 29.8 %reduce-scatter.3.cloned.1.call-done = f32[128,8,128]{2,0,1:T(8,128)} async-done(((f32[512,8,128]{2,0,1:T(8,128)}), f32[128,8,128]{2,0,1:T(8,128)}) %reduce-scatter.3.cloned.1.call-update) | async-done | bytes 524304 | tf_op jit(solution)/shard_map/reduce_scatter | solution.py:218
  119.8 7.3 %collective-permute-start.4 = (f32[128,1,128]{2,0,1:T(8,128)S(1)}, f32[128,1,128]{2,0,1:T(8,128)S(1)}, u32[]{:S(2)}, u32[]{:S(2)}) collective-permute-start(f32[128,1,128]{2,0,1:T(8,128)S(1)} %get-tuple-element.178), channel_id=1, source_target_pairs={{4,0},{8,4},{12,8},{16,12},{20,16},{24,20},{28,24},{32,28},{36,32}... | collective-permute-start | bytes 196616 | tf_op jit(solution)/shard_map/ppermute | solution.py:34
  129.3 8.6 %collective-permute-done.5 = f32[128,1,128]{2,0,1:T(8,128)S(1)} collective-permute-done((f32[128,1,128]{2,0,1:T(8,128)S(1)}, f32[128,1,128]{2,0,1:T(8,128)S(1)}, u32[]{:S(2)}, u32[]{:S(2)}) %collective-permute-start.5) | collective-permute-done | bytes 65568 | tf_op jit(solution)/shard_map/ppermute | solution.py:31
  144.0 7.2 %collective-permute-done.7 = f32[128,1,128]{2,0,1:T(8,128)S(1)} collective-permute-done((f32[128,1,128]{2,0,1:T(8,128)S(1)}, f32[128,1,128]{2,0,1:T(8,128)S(1)}, u32[]{:S(2)}, u32[]{:S(2)}) %collective-permute-start.7) | collective-permute-done | bytes 65568 | tf_op jit(solution)/shard_map/ppermute | solution.py:31
  157.3 7.2 %collective-permute-done.9 = f32[128,1,128]{2,0,1:T(8,128)S(1)} collective-permute-done((f32[128,1,128]{2,0,1:T(8,128)S(1)}, f32[128,1,128]{2,0,1:T(8,128)S(1)}, u32[]{:S(2)}, u32[]{:S(2)}) %collective-permute-start.9) | collective-permute-done | bytes 65568 | tf_op jit(solution)/shard_map/ppermute | solution.py:31
  170.5 7.2 %collective-permute-done.11 = f32[128,1,128]{2,0,1:T(8,128)S(1)} collective-permute-done((f32[128,1,128]{2,0,1:T(8,128)S(1)}, f32[128,1,128]{2,0,1:T(8,128)S(1)}, u32[]{:S(2)}, u32[]{:S(2)}) %collective-permute-start.11) | collective-permute-done | bytes 65568 | tf_op jit(solution)/shard_map/ppermute | solution.py:31
  183.8 7.2 %collective-permute-done.13 = f32[128,1,128]{2,0,1:T(8,128)S(1)} collective-permute-done((f32[128,1,128]{2,0,1:T(8,128)S(1)}, f32[128,1,128]{2,0,1:T(8,128)S(1)}, u32[]{:S(2)}, u32[]{:S(2)}) %collective-permute-start.13) | collective-permute-done | bytes 65568 | tf_op jit(solution)/shard_map/ppermute | solution.py:31
  197.0 7.2 %collective-permute-done.15 = f32[128,1,128]{2,0,1:T(8,128)S(1)} collective-permute-done((f32[128,1,128]{2,0,1:T(8,128)S(1)}, f32[128,1,128]{2,0,1:T(8,128)S(1)}, u32[]{:S(2)}, u32[]{:S(2)}) %collective-permute-start.15) | collective-permute-done | bytes 65568 | tf_op jit(solution)/shard_map/ppermute | solution.py:31
  212.0 25.5 %all-gather.3.cloned.1.call-done = f32[512,8,128]{2,0,1:T(8,128)} async-done(((f32[128,8,128]{2,0,1:T(8,128)}), f32[512,8,128]{2,0,1:T(8,128)}) %all-gather.3.cloned.1.call-update) | async-done | bytes 2097168 | tf_op jit(solution)/shard_map/all_gather | solution.py:231
  261.7 8.0 %collective-permute-start.21 = (f32[6,2,128,128]{2,3,1,0:T(8,128)S(1)}, f32[6,2,128,128]{2,3,1,0:T(8,128)S(1)}, u32[]{:S(2)}, u32[]{:S(2)}) collective-permute-start(f32[6,2,128,128]{2,3,1,0:T(8,128)S(1)} %get-tuple-element.67), channel_id=1, source_target_pairs={{4,0},{8,4},{12,8},{16,12},{20,16},{24,20},{28,24},{32,28},{36,32}... | collective-permute-start | bytes 2359304 | tf_op jit(solution)/shard_map/ppermute | solution.py:34
  269.7 16.7 %collective-permute-done.20 = f32[6,2,128,128]{2,3,1,0:T(8,128)S(1)} collective-permute-done((f32[6,2,128,128]{2,3,1,0:T(8,128)S(1)}, f32[6,2,128,128]{2,3,1,0:T(8,128)S(1)}, u32[]{:S(2)}, u32[]{:S(2)}) %collective-permute-start.20) | collective-permute-done | bytes 786464 | tf_op jit(solution)/shard_map/ppermute | solution.py:31
  297.2 9.9 %pad_maximum_fusion.1 = f32[6,12,130,132]{2,3,1,0:T(8,128)} fusion(f32[6,12,1,132]{2,3,1,0:T(8,128)} %get-tuple-element.39, f32[6,2,128,132]{2,3,1,0:T(8,128)S(1)} %get-tuple-element.45, f32[6,8,128,132]{2,3,1,0:T(8,128)S(1)} %slice.1435, f32[6,2,128,132]{2,3,1,0:T(8,128)S(1)} %get-tuple-element.44, f32[6,12,1,132]{2,3,1,0:T(8,128)S(1)} %get-tuple-element.38), kind=kLoop, calls=%fused_computation.1 | loop fusion | flops 4942080 | bytes 9884160 | tf_op jit(solution)/shard_map/concatenate | solution.py:96
  311.7 6.4 %multiply_add_fusion.2 = (f32[10,128,130]{1,2,0:T(8,128)S(1)}, f32[10,128,130]{1,2,0:T(8,128)}, f32[10,128,130]{1,2,0:T(8,128)}, f32[10,128,130]{1,2,0:T(8,128)S(1)}) fusion(f32[12,130,132]{1,2,0:T(8,128)S(1)} %get-tuple-element.29, f32[12,130,132]{1,2,0:T(8,128)S(1)} %get-tuple-element.31, f32[12,130,132]{1,2,0:T(8,128)S(1)} %get-tuple-element.30, ...), kind=kLoop, calls=%fused_computation.88 | loop fusion | flops 22131200 | bytes 22630400 | tf_op jit(solution)/shard_map/add | solution.py:141
  331.5 28.8 %reduce-scatter.5.cloned.1.call-done = f32[128,8,128]{2,0,1:T(8,128)} async-done(((f32[512,8,128]{2,0,1:T(8,128)}), f32[128,8,128]{2,0,1:T(8,128)}) %reduce-scatter.5.cloned.1.call-update) | async-done | bytes 524304 | tf_op jit(solution)/shard_map/reduce_scatter | solution.py:218
  361.7 7.3 %collective-permute-start.24 = (f32[128,1,128]{2,0,1:T(8,128)S(1)}, f32[128,1,128]{2,0,1:T(8,128)S(1)}, u32[]{:S(2)}, u32[]{:S(2)}) collective-permute-start(f32[128,1,128]{2,0,1:T(8,128)S(1)} %get-tuple-element.140), channel_id=1, source_target_pairs={{4,0},{8,4},{12,8},{16,12},{20,16},{24,20},{28,24},{32,28},{36,32}... | collective-permute-start | bytes 196616 | tf_op jit(solution)/shard_map/ppermute | solution.py:34
  371.2 8.6 %collective-permute-done.25 = f32[128,1,128]{2,0,1:T(8,128)S(1)} collective-permute-done((f32[128,1,128]{2,0,1:T(8,128)S(1)}, f32[128,1,128]{2,0,1:T(8,128)S(1)}, u32[]{:S(2)}, u32[]{:S(2)}) %collective-permute-start.25) | collective-permute-done | bytes 65568 | tf_op jit(solution)/shard_map/ppermute | solution.py:31
  385.9 7.2 %collective-permute-done.27 = f32[128,1,128]{2,0,1:T(8,128)S(1)} collective-permute-done((f32[128,1,128]{2,0,1:T(8,128)S(1)}, f32[128,1,128]{2,0,1:T(8,128)S(1)}, u32[]{:S(2)}, u32[]{:S(2)}) %collective-permute-start.27) | collective-permute-done | bytes 65568 | tf_op jit(solution)/shard_map/ppermute | solution.py:31
  399.2 7.2 %collective-permute-done.29 = f32[128,1,128]{2,0,1:T(8,128)S(1)} collective-permute-done((f32[128,1,128]{2,0,1:T(8,128)S(1)}, f32[128,1,128]{2,0,1:T(8,128)S(1)}, u32[]{:S(2)}, u32[]{:S(2)}) %collective-permute-start.29) | collective-permute-done | bytes 65568 | tf_op jit(solution)/shard_map/ppermute | solution.py:31
  412.4 7.2 %collective-permute-done.31 = f32[128,1,128]{2,0,1:T(8,128)S(1)} collective-permute-done((f32[128,1,128]{2,0,1:T(8,128)S(1)}, f32[128,1,128]{2,0,1:T(8,128)S(1)}, u32[]{:S(2)}, u32[]{:S(2)}) %collective-permute-start.31) | collective-permute-done | bytes 65568 | tf_op jit(solution)/shard_map/ppermute | solution.py:31
  425.7 7.2 %collective-permute-done.33 = f32[128,1,128]{2,0,1:T(8,128)S(1)} collective-permute-done((f32[128,1,128]{2,0,1:T(8,128)S(1)}, f32[128,1,128]{2,0,1:T(8,128)S(1)}, u32[]{:S(2)}, u32[]{:S(2)}) %collective-permute-start.33) | collective-permute-done | bytes 65568 | tf_op jit(solution)/shard_map/ppermute | solution.py:31
  439.2 6.9 %collective-permute-done.35 = f32[128,1,128]{2,0,1:T(8,128)S(1)} collective-permute-done((f32[128,1,128]{2,0,1:T(8,128)S(1)}, f32[128,1,128]{2,0,1:T(8,128)S(1)}, u32[]{:S(2)}, u32[]{:S(2)}) %collective-permute-start.35) | collective-permute-done | bytes 65568 | tf_op jit(solution)/shard_map/ppermute | solution.py:31
  457.7 21.7 %all-gather.5.cloned.1.call-done = f32[512,8,128]{2,0,1:T(8,128)} async-done(((f32[128,8,128]{2,0,1:T(8,128)}), f32[512,8,128]{2,0,1:T(8,128)}) %all-gather.5.cloned.1.call-update) | async-done | bytes 2097168 | tf_op jit(solution)/shard_map/all_gather | solution.py:231
  (294 shorter events, 221.5 us)
Async XLA Ops:
  7.2 111.2 %reduce-scatter.3.cloned.1.call-start = ((), (), s32[]{:S(2)}) async-start(), calls=%async_computation.2 | async-start | bytes 2621440 | tf_op jit(solution)/shard_map/reduce_scatter | solution.py:218
  13.3 24.4 %collective-permute-start = (f32[6,2,128,128]{2,3,1,0:T(8,128)}, f32[6,2,128,128]{2,3,1,0:T(8,128)}, u32[]{:S(2)}, u32[]{:S(2)}) collective-permute-start(f32[6,2,128,128]{2,3,1,0:T(8,128)} %get-tuple-element.68), channel_id=1, source_target_pairs={{0,4},{4,8},{8,12},{12,16},{16,20},{20,24},{24,28},{28,32},{32,36}... | collective-permute-start | bytes 2359304 | tf_op jit(solution)/shard_map/ppermute | solution.py:31
  15.0 22.8 %collective-permute-start.1 = (f32[6,2,128,128]{2,3,1,0:T(8,128)}, f32[6,2,128,128]{2,3,1,0:T(8,128)}, u32[]{:S(2)}, u32[]{:S(2)}) collective-permute-start(f32[6,2,128,128]{2,3,1,0:T(8,128)} %get-tuple-element.69), channel_id=1, source_target_pairs={{4,0},{8,4},{12,8},{16,12},{20,16},{24,20},{28,24},{32,28},{36,32}... | collective-permute-start | bytes 2359304 | tf_op jit(solution)/shard_map/ppermute | solution.py:34
  88.4 149.2 %all-gather.3.cloned.1.call-start = ((), (), s32[]{:S(2)}) async-start(), calls=%async_computation.3 | async-start | bytes 2621440 | tf_op jit(solution)/shard_map/all_gather | solution.py:231
  119.8 9.5 %collective-permute-start.4 = (f32[128,1,128]{2,0,1:T(8,128)S(1)}, f32[128,1,128]{2,0,1:T(8,128)S(1)}, u32[]{:S(2)}, u32[]{:S(2)}) collective-permute-start(f32[128,1,128]{2,0,1:T(8,128)S(1)} %get-tuple-element.178), channel_id=1, source_target_pairs={{4,0},{8,4},{12,8},{16,12},{20,16},{24,20},{28,24},{32,28},{36,32}... | collective-permute-start | bytes 196616 | tf_op jit(solution)/shard_map/ppermute | solution.py:34
  127.2 10.7 %collective-permute-start.5 = (f32[128,1,128]{2,0,1:T(8,128)S(1)}, f32[128,1,128]{2,0,1:T(8,128)S(1)}, u32[]{:S(2)}, u32[]{:S(2)}) collective-permute-start(f32[128,1,128]{2,0,1:T(8,128)S(1)} %get-tuple-element.179), channel_id=1, source_target_pairs={{0,4},{4,8},{8,12},{12,16},{16,20},{20,24},{24,28},{28,32},{32,36}... | collective-permute-start | bytes 196616 | tf_op jit(solution)/shard_map/ppermute | solution.py:31
  140.4 10.7 %collective-permute-start.7 = (f32[128,1,128]{2,0,1:T(8,128)S(1)}, f32[128,1,128]{2,0,1:T(8,128)S(1)}, u32[]{:S(2)}, u32[]{:S(2)}) collective-permute-start(f32[128,1,128]{2,0,1:T(8,128)S(1)} %get-tuple-element.173), channel_id=1, source_target_pairs={{0,4},{4,8},{8,12},{12,16},{16,20},{20,24},{24,28},{28,32},{32,36}... | collective-permute-start | bytes 196616 | tf_op jit(solution)/shard_map/ppermute | solution.py:31
  153.7 10.7 %collective-permute-start.9 = (f32[128,1,128]{2,0,1:T(8,128)S(1)}, f32[128,1,128]{2,0,1:T(8,128)S(1)}, u32[]{:S(2)}, u32[]{:S(2)}) collective-permute-start(f32[128,1,128]{2,0,1:T(8,128)S(1)} %get-tuple-element.167), channel_id=1, source_target_pairs={{0,4},{4,8},{8,12},{12,16},{16,20},{20,24},{24,28},{28,32},{32,36}... | collective-permute-start | bytes 196616 | tf_op jit(solution)/shard_map/ppermute | solution.py:31
  166.9 10.7 %collective-permute-start.11 = (f32[128,1,128]{2,0,1:T(8,128)S(1)}, f32[128,1,128]{2,0,1:T(8,128)S(1)}, u32[]{:S(2)}, u32[]{:S(2)}) collective-permute-start(f32[128,1,128]{2,0,1:T(8,128)S(1)} %get-tuple-element.161), channel_id=1, source_target_pairs={{0,4},{4,8},{8,12},{12,16},{16,20},{20,24},{24,28},{28,32},{32,36}... | collective-permute-start | bytes 196616 | tf_op jit(solution)/shard_map/ppermute | solution.py:31
  180.2 10.7 %collective-permute-start.13 = (f32[128,1,128]{2,0,1:T(8,128)S(1)}, f32[128,1,128]{2,0,1:T(8,128)S(1)}, u32[]{:S(2)}, u32[]{:S(2)}) collective-permute-start(f32[128,1,128]{2,0,1:T(8,128)S(1)} %get-tuple-element.155), channel_id=1, source_target_pairs={{0,4},{4,8},{8,12},{12,16},{16,20},{20,24},{24,28},{28,32},{32,36}... | collective-permute-start | bytes 196616 | tf_op jit(solution)/shard_map/ppermute | solution.py:31
  193.4 10.7 %collective-permute-start.15 = (f32[128,1,128]{2,0,1:T(8,128)S(1)}, f32[128,1,128]{2,0,1:T(8,128)S(1)}, u32[]{:S(2)}, u32[]{:S(2)}) collective-permute-start(f32[128,1,128]{2,0,1:T(8,128)S(1)} %get-tuple-element.149), channel_id=1, source_target_pairs={{0,4},{4,8},{8,12},{12,16},{16,20},{20,24},{24,28},{28,32},{32,36}... | collective-permute-start | bytes 196616 | tf_op jit(solution)/shard_map/ppermute | solution.py:31
  205.3 154.9 %reduce-scatter.5.cloned.1.call-start = ((), (), s32[]{:S(2)}) async-start(), calls=%async_computation.4 | async-start | bytes 2621440 | tf_op jit(solution)/shard_map/reduce_scatter | solution.py:218
  241.7 9.5 %collective-permute-start.16 = (f32[1,128,128]{1,2,0:T(8,128)S(1)}, f32[1,128,128]{1,2,0:T(8,128)S(1)}, u32[]{:S(2)}, u32[]{:S(2)}) collective-permute-start(f32[1,128,128]{1,2,0:T(8,128)S(1)} %get-tuple-element.142), channel_id=1, source_target_pairs={{0,4},{4,8},{8,12},{12,16},{16,20},{20,24},{24,28},{28,32},{32,36}... | collective-permute-start | bytes 196616 | tf_op jit(solution)/shard_map/ppermute | solution.py:31
  261.6 24.8 %collective-permute-start.20 = (f32[6,2,128,128]{2,3,1,0:T(8,128)S(1)}, f32[6,2,128,128]{2,3,1,0:T(8,128)S(1)}, u32[]{:S(2)}, u32[]{:S(2)}) collective-permute-start(f32[6,2,128,128]{2,3,1,0:T(8,128)S(1)} %get-tuple-element.66), channel_id=1, source_target_pairs={{0,4},{4,8},{8,12},{12,16},{16,20},{20,24},{24,28},{28,32},{32,36}... | collective-permute-start | bytes 2359304 | tf_op jit(solution)/shard_map/ppermute | solution.py:31
  261.7 24.7 %collective-permute-start.21 = (f32[6,2,128,128]{2,3,1,0:T(8,128)S(1)}, f32[6,2,128,128]{2,3,1,0:T(8,128)S(1)}, u32[]{:S(2)}, u32[]{:S(2)}) collective-permute-start(f32[6,2,128,128]{2,3,1,0:T(8,128)S(1)} %get-tuple-element.67), channel_id=1, source_target_pairs={{4,0},{8,4},{12,8},{16,12},{20,16},{24,20},{28,24},{32,28},{36,32}... | collective-permute-start | bytes 2359304 | tf_op jit(solution)/shard_map/ppermute | solution.py:34
  331.5 148.0 %all-gather.5.cloned.1.call-start = ((), (), s32[]{:S(2)}) async-start(), calls=%async_computation.5 | async-start | bytes 2621440 | tf_op jit(solution)/shard_map/all_gather | solution.py:231
  361.7 9.5 %collective-permute-start.24 = (f32[128,1,128]{2,0,1:T(8,128)S(1)}, f32[128,1,128]{2,0,1:T(8,128)S(1)}, u32[]{:S(2)}, u32[]{:S(2)}) collective-permute-start(f32[128,1,128]{2,0,1:T(8,128)S(1)} %get-tuple-element.140), channel_id=1, source_target_pairs={{4,0},{8,4},{12,8},{16,12},{20,16},{24,20},{28,24},{32,28},{36,32}... | collective-permute-start | bytes 196616 | tf_op jit(solution)/shard_map/ppermute | solution.py:34
  369.1 10.7 %collective-permute-start.25 = (f32[128,1,128]{2,0,1:T(8,128)S(1)}, f32[128,1,128]{2,0,1:T(8,128)S(1)}, u32[]{:S(2)}, u32[]{:S(2)}) collective-permute-start(f32[128,1,128]{2,0,1:T(8,128)S(1)} %get-tuple-element.141), channel_id=1, source_target_pairs={{0,4},{4,8},{8,12},{12,16},{16,20},{20,24},{24,28},{28,32},{32,36}... | collective-permute-start | bytes 196616 | tf_op jit(solution)/shard_map/ppermute | solution.py:31
  382.3 10.7 %collective-permute-start.27 = (f32[128,1,128]{2,0,1:T(8,128)S(1)}, f32[128,1,128]{2,0,1:T(8,128)S(1)}, u32[]{:S(2)}, u32[]{:S(2)}) collective-permute-start(f32[128,1,128]{2,0,1:T(8,128)S(1)} %get-tuple-element.135), channel_id=1, source_target_pairs={{0,4},{4,8},{8,12},{12,16},{16,20},{20,24},{24,28},{28,32},{32,36}... | collective-permute-start | bytes 196616 | tf_op jit(solution)/shard_map/ppermute | solution.py:31
  395.6 10.7 %collective-permute-start.29 = (f32[128,1,128]{2,0,1:T(8,128)S(1)}, f32[128,1,128]{2,0,1:T(8,128)S(1)}, u32[]{:S(2)}, u32[]{:S(2)}) collective-permute-start(f32[128,1,128]{2,0,1:T(8,128)S(1)} %get-tuple-element.129), channel_id=1, source_target_pairs={{0,4},{4,8},{8,12},{12,16},{16,20},{20,24},{24,28},{28,32},{32,36}... | collective-permute-start | bytes 196616 | tf_op jit(solution)/shard_map/ppermute | solution.py:31
  408.8 10.7 %collective-permute-start.31 = (f32[128,1,128]{2,0,1:T(8,128)S(1)}, f32[128,1,128]{2,0,1:T(8,128)S(1)}, u32[]{:S(2)}, u32[]{:S(2)}) collective-permute-start(f32[128,1,128]{2,0,1:T(8,128)S(1)} %get-tuple-element.123), channel_id=1, source_target_pairs={{0,4},{4,8},{8,12},{12,16},{16,20},{20,24},{24,28},{28,32},{32,36}... | collective-permute-start | bytes 196616 | tf_op jit(solution)/shard_map/ppermute | solution.py:31
  422.1 10.7 %collective-permute-start.33 = (f32[128,1,128]{2,0,1:T(8,128)S(1)}, f32[128,1,128]{2,0,1:T(8,128)S(1)}, u32[]{:S(2)}, u32[]{:S(2)}) collective-permute-start(f32[128,1,128]{2,0,1:T(8,128)S(1)} %get-tuple-element.117), channel_id=1, source_target_pairs={{0,4},{4,8},{8,12},{12,16},{16,20},{20,24},{24,28},{28,32},{32,36}... | collective-permute-start | bytes 196616 | tf_op jit(solution)/shard_map/ppermute | solution.py:31
  435.3 10.7 %collective-permute-start.35 = (f32[128,1,128]{2,0,1:T(8,128)S(1)}, f32[128,1,128]{2,0,1:T(8,128)S(1)}, u32[]{:S(2)}, u32[]{:S(2)}) collective-permute-start(f32[128,1,128]{2,0,1:T(8,128)S(1)} %get-tuple-element.111), channel_id=1, source_target_pairs={{0,4},{4,8},{8,12},{12,16},{16,20},{20,24},{24,28},{28,32},{32,36}... | collective-permute-start | bytes 196616 | tf_op jit(solution)/shard_map/ppermute | solution.py:31
  483.7 9.5 %collective-permute-start.36 = (f32[1,128,128]{1,2,0:T(8,128)S(1)}, f32[1,128,128]{1,2,0:T(8,128)S(1)}, u32[]{:S(2)}, u32[]{:S(2)}) collective-permute-start(f32[1,128,128]{1,2,0:T(8,128)S(1)} %get-tuple-element.104), channel_id=1, source_target_pairs={{0,4},{4,8},{8,12},{12,16},{16,20},{20,24},{24,28},{28,32},{32,36}... | collective-permute-start | bytes 196616 | tf_op jit(solution)/shard_map/ppermute | solution.py:31
  (68 other events, 439.2 us)
Sparse Core Ops, SparseCore 0:
  88.5 29.8 reduce-scatter.2
  205.5 32.0 all-gather.2
  331.6 28.6 reduce-scatter.4
  447.4 32.0 all-gather.4
where the time goes:
time: 516 us; the launch traced here: 510 us
  waiting for transfers between devices  237 us (46%)
  starting transfers between devices  109 us (21%)
  other arithmetic  107 us (21%)
  local copies, waits for them, and re-layouts  22.2 us (4%)
  matrix products  18.8 us (4%)
  between operations  15.3 us (3%)
    ppermute x20, waiting for transfers between devices, with_halo(): lax.ppermute(lax.slice_in_dim(block, block.shape[dim] - width, None, axis...  124 us
    ppermute x20, starting transfers between devices, with_halo(): lax.ppermute(lax.slice_in_dim(block, 0, width, axis=dim), axis, backward)  59.6 us
    reduce_scatter x2, waiting for transfers between devices, to_modes(): lax.psum_scatter(jnp.einsum('xyz,zc->cxy', source, own_rows, precision=la...  58.6 us
    ppermute x20, starting transfers between devices, with_halo(): lax.ppermute(lax.slice_in_dim(block, block.shape[dim] - width, None, axis...  49.1 us
    all_gather x2, waiting for transfers between devices, from_modes(): lax.all_gather(modal, 'span', axis=0, tiled=True)  47.2 us
    add x6, other arithmetic, predict(): RHO_GAS / TIME_STEP * provisional[axis]  28.4 us
    concatenate x2, other arithmetic, pad_gap(): return jnp.concatenate([bottom, padded, top], axis=2)  19.8 us
    unnamed x105, local copies, waits for them, and re-layouts  15.5 us
  transfers between devices with their start and end apart: 44, of which 26 were waited for; matrix products, arithmetic and copies ran while one was open for 6% of the time, Pallas kernels for 0%

commit v1 on v0

v1 whole, which is shorter than its diff:
```python
import functools
import math

import jax
import jax.numpy as jnp
import numpy as np
from jax import lax
from jax.experimental import pallas as pl
from jax.experimental.pallas import tpu as pltpu
from jax.sharding import PartitionSpec as P

STEPS = 2
POWERS = 7
NX, NY, NZ = 8, 128, 128
TOP = 8
ROWS = NY + 2 * TOP
BLOCKS = 4
F32 = jnp.float32
BF16 = jnp.bfloat16
HIGHEST = lax.Precision.HIGHEST
VMEM_LIMIT = 60 * 1024 * 1024


def comb(n, k):
    return math.comb(n, k) if 0 <= k <= n else 0


RATIO = 3.0 - 2.0 * math.sqrt(2.0)


def line_kernel(power, n):
    return RATIO ** (power + n) * sum(
        comb(power - 1 + n + k, power - 1) * comb(power - 1 + k, power - 1) * RATIO ** (2 * k)
        for k in range(40)
    )


def far_kernel(power, j, z):
    return RATIO ** (power + 1 + z) * sum(
        comb(power - 1 + k, power - 1) * RATIO ** (2 * k) * comb(power + z + k, power - 1 - j)
        for k in range(40)
    )


@functools.cache
def solve_table():
    near = np.zeros((POWERS, 144, NZ + 2))
    for m in range(POWERS):
        kernel = np.array([line_kernel(m + 1, n) for n in range(NZ + 2)])
        z = np.arange(-1, NZ + 1)
        own = np.arange(NZ)
        near[m, :NZ] = kernel[np.abs(z[None, :] - own[:, None])]
        far = np.array([[far_kernel(m + 1, j, t) for t in z] for j in range(POWERS)])
        near[m, NZ : NZ + POWERS] = far
        near[m, NZ + POWERS : NZ + 2 * POWERS] = far[:, ::-1]
        near[m, NZ + 14] = -2.5 * near[m, 0]
        near[m, NZ + 15] = 2.5 * near[m, NZ - 1]
    value = near[:, :, 1:-1]
    slope = 0.5 * (near[:, :, 2:] - near[:, :, :-2])
    wide = np.concatenate([value, slope]).transpose(1, 0, 2).reshape(144, 2 * POWERS * NZ)
    wide = wide.astype(np.float32)
    head = wide.astype(jnp.bfloat16)
    tail = (wide - head.astype(np.float32)).astype(jnp.bfloat16)
    table = np.zeros((512, wide.shape[1]), jnp.bfloat16)
    table[0:128] = head[:NZ]
    table[128:256] = head[:NZ]
    table[256:384] = tail[:NZ]
    table[384:400] = head[NZ:]
    table[400:416] = head[NZ:]
    table[416:432] = tail[NZ:]
    return table


@functools.cache
def moment_table():
    table = np.zeros((2, NZ, 128), np.float32)
    for z in range(NZ):
        for j in range(POWERS):
            table[0, z, j] = comb(z, j) * RATIO**z
            table[0, z, POWERS + j] = comb(NZ - 1 - z, j) * RATIO ** (NZ - 1 - z)
    table[1, 0, 14] = 1.0
    table[1, NZ - 1, 15] = 1.0
    return table


@functools.cache
def combine_table():
    small = np.zeros((BLOCKS, 16, 16))
    end = [comb(NZ - 1, a) * RATIO ** (NZ - 1) for a in range(POWERS)]
    for o in range(1, 2 * BLOCKS + 1):
        gap = NZ * (o - 1)
        for j in range(POWERS):
            for a in range(j + 1):
                factor = comb(gap, j - a) * RATIO**gap
                left = -o
                small[left % BLOCKS, POWERS + a, j] += factor
                small[(left - 1) % BLOCKS, 15, j] += factor * end[a] * -2.5
                small[(left + 1) % BLOCKS, 14, j] += factor * (2.5 if a == 0 else 0.0)
                right = o
                small[right % BLOCKS, a, POWERS + j] += factor
                small[(right - 1) % BLOCKS, 15, POWERS + j] += factor * (-2.5 if a == 0 else 0.0)
                small[(right + 1) % BLOCKS, 14, POWERS + j] += factor * end[a] * 2.5
    small[-1 % BLOCKS, 15, 14] += 1.0
    small[1 % BLOCKS, 14, 15] += 1.0
    table = np.zeros((BLOCKS, 128, 128), np.float32)
    for x in range(NX):
        table[:, 16 * x : 16 * x + 16, 16 * x : 16 * x + 16] = small
    return table


def lanes(rows):
    return lax.broadcasted_iota(jnp.int32, (rows, 128), 1)


def pack_columns(fields):
    lane = lanes(NY)
    packed = jnp.zeros((NY, 128), F32)
    for k in range(5):
        for x in range(NX):
            pair = 12 * k + x + 2
            keep = (lane == 2 * pair + 1) | (lane == 2 * pair + 2)
            packed = jnp.where(keep, pltpu.roll(fields(k, x), 2 * pair + 2, 1), packed)
    return packed


def pack_body(vel, frac, now, old, right, left, packed, guess):
    for x in range(NX):
        guess[x] = 2.0 * now[x] - old[x]
    emit_faces(vel, frac, guess, right, left, packed)


def emit_faces(vel, frac, guess, right, left, packed):
    right[0:2] = vel[0, 6:8]
    right[2] = vel[1, 7]
    right[3] = vel[2, 7]
    right[4:6] = frac[6:8]
    right[6:8] = guess[6:8]
    left[0:2] = vel[0, 0:2]
    left[2] = vel[1, 0]
    left[3] = vel[2, 0]
    left[4:6] = frac[0:2]
    left[6:8] = guess[0:2]

    def field(k, x):
        return vel[k, x] if k < 3 else (frac[x] if k == 3 else guess[x])

    packed[...] = pack_columns(field)


def predict_body(
    flags, vel, frac, guess, low, high, sides, sides_low, sides_high, profile, moments,
    mid, frac_new, source, pack,
    U, V, W, F, G, FM, FP, Z, end_mid, sem,
):
    own = pl.ds(TOP, NY)
    copies = []

    def fetch(src, dst):
        copy = pltpu.make_async_copy(src, dst, sem.at[len(copies)])
        copy.start()
        copies.append(copy)

    for k, buf in enumerate((U, V, W)):
        fetch(vel.at[k], buf.at[pl.ds(2, NX), own])
    fetch(frac, F.at[pl.ds(2, NX), own])
    fetch(guess, G.at[pl.ds(2, NX), own])
    for msg, far, near in ((low, 0, 1), (high, 10, 10)):
        fetch(msg.at[pl.ds(0, 2)], U.at[pl.ds(far, 2), own])
        fetch(msg.at[2], V.at[near, own])
        fetch(msg.at[3], W.at[near, own])
        fetch(msg.at[pl.ds(4, 2)], F.at[pl.ds(far, 2), own])
        fetch(msg.at[pl.ds(6, 2)], G.at[pl.ds(far, 2), own])

    first = flags[0] == 1
    last = flags[1] == 1
    lane = lanes(NY)
    place = lane // 2
    slot = place % 12
    group = place // 12
    merged = sides[...]
    below = pltpu.roll(sides_low[...], 112, 1)
    above = pltpu.roll(sides_high[...], 16, 1)
    below_wall = jnp.where(group == 0, profile[0], jnp.where(group == 3, profile[1], 0.0))
    above_wall = jnp.where(slot == 10, pltpu.roll(merged, 2, 1), pltpu.roll(merged, 4, 1))
    below = jnp.where(first, below_wall, below)
    above = jnp.where(last, above_wall, above)
    Z[...] = jnp.where(slot < 2, below, jnp.where(slot >= 10, above, merged))

    for copy in copies:
        copy.wait()

    @pl.when(first)
    def _():
        for e in range(2):
            U[e, own] = profile[0]
            F[e, own] = profile[1]

    @pl.when(last)
    def _():
        for e in (10, 11):
            U[e, own] = U[9, own]
            F[e, own] = F[9, own]
        V[10, own] = V[9, own]
        W[10, own] = W[9, own]

    def shift_fraction(e, carry):
        lane = lanes(NY)
        centre = F[e, own]
        ends = pltpu.roll(Z[...], 128 - 2 * (36 + e) - 1, 1)
        FM[e, own] = jnp.where(lane == 0, ends, pltpu.roll(centre, 1, 1))
        FP[e, own] = jnp.where(lane == 127, ends, pltpu.roll(centre, 127, 1))
        for buf in (F, FM, FP):
            buf[e, pl.ds(TOP - 1, 1)] = buf[e, pl.ds(TOP, 1)]
            buf[e, pl.ds(TOP + NY, 1)] = buf[e, pl.ds(TOP + NY - 1, 1)]
        G[e, pl.ds(TOP - 1, 1)] = G[e, pl.ds(TOP, 1)]
        G[e, pl.ds(TOP + NY, 1)] = G[e, pl.ds(TOP + NY - 1, 1)]
        for buf, wall in ((U, 2.0), (V, 0.0), (W, 0.0)):
            buf[e, pl.ds(TOP - 1, 1)] = wall - buf[e, pl.ds(TOP, 1)]
            buf[e, pl.ds(TOP + NY, 1)] = -buf[e, pl.ds(TOP + NY - 1, 1)]
        return carry

    lax.fori_loop(0, 12, shift_fraction, 0)

    def cells(e, y, components):
        lane = lanes(8)
        at_low = lane == 0
        at_high = lane == 127
        here, up, down = pl.ds(y + TOP, 8), pl.ds(y + TOP + 1, 8), pl.ds(y + TOP - 1, 8)
        ends_all = Z[pl.ds(y, 8), :]

        def star(buf, k):
            centre = buf[e, here]
            ends = pltpu.roll(ends_all, 128 - 2 * (12 * k + e) - 1, 1)
            behind = jnp.where(at_low, ends, pltpu.roll(centre, 1, 1))
            ahead = jnp.where(at_high, ends, pltpu.roll(centre, 127, 1))
            return centre, (
                (buf[e + 1, here], buf[e - 1, here]),
                (buf[e, up], buf[e, down]),
                (ahead, behind),
            )

        c = F[e, here]
        around = ((F[e + 1, here], F[e - 1, here]), (F[e, up], F[e, down]), (FP[e, here], FM[e, here]))
        d = [p - m for p, m in around]
        second = [p + m - 2.0 * c for p, m in around]
        mxy = (F[e + 1, up] - F[e + 1, down]) - (F[e - 1, up] - F[e - 1, down])
        mxz = (FP[e + 1, here] - FM[e + 1, here]) - (FP[e - 1, here] - FM[e - 1, here])
        myz = (FP[e, up] - FM[e, up]) - (FP[e, down] - FM[e, down])
        dd = [v * v for v in d]
        inverse = lax.rsqrt(jnp.maximum(dd[0] + dd[1] + dd[2], 1.0))
        bend = (dd[0] * second[0] + dd[1] * second[1] + dd[2] * second[2]) + 0.5 * (
            d[0] * (d[1] * mxy + d[2] * mxz) + d[1] * d[2] * myz
        )
        laplace = second[0] + second[1] + second[2]
        volume = 1.0 / (0.5 + 0.5 * c)
        pull = (bend * (inverse * inverse) - laplace) * (0.5 * inverse) * volume
        nu = (0.02 + 0.03 * c) * volume
        if len(components) == 3:
            stars = [star(buf, k) for k, buf in enumerate((U, V, W))]
            centres = [s[0] for s in stars]
        else:
            stars = [star(U, 0)]
            centres = [stars[0][0], V[e, here], W[e, here]]
        speeds = [jnp.abs(v) for v in centres]
        if len(components) == 3:
            guesses = star(G, 4)[1]
        else:
            guesses = ((G[e + 1, here], G[e - 1, here]),)
        lift = 2.0 - volume
        out = []
        for k in components:
            centre, sides_ = stars[k]
            twice = 2.0 * centre
            transport = 0.0
            diffusion = 0.0
            for a in range(3):
                p, m = sides_[a]
                curve = p + m - twice
                transport = transport + (centres[a] * (p - m) - speeds[a] * curve)
                diffusion = diffusion + curve
            change = nu * diffusion + pull * d[k] - 0.5 * transport
            p, m = guesses[k]
            out.append(centre + 0.1 * (change + 0.5 * (lift * (p - m))))
        if len(components) == 1:
            return out
        net = 0.0
        for a in range(3):
            p, m = stars[a][1][a]
            fp, fm = around[a]
            ahead = centres[a] + p
            behind = centres[a] + m
            net = net + (
                (jnp.maximum(ahead, 0.0) - jnp.minimum(behind, 0.0)) * c
                + (jnp.minimum(ahead, 0.0) * fp - jnp.maximum(behind, 0.0) * fm)
            )
        return out + [c - 0.05 * net]

    def block(i, carry):
        x = i // 16
        y = pl.multiple_of((i % 16) * 8, 8)
        u, v, w, f = cells(x + 2, y, (0, 1, 2))
        rows = pl.ds(y, 8)
        mid[0, x, rows] = u
        mid[1, x, rows] = v
        mid[2, x, rows] = w
        frac_new[x, rows] = f
        return carry

    lax.fori_loop(0, 16 * NX, block, 0)

    def end_block(i, carry):
        side = i // 16
        y = pl.multiple_of((i % 16) * 8, 8)
        (u,) = cells(1 + 9 * side, y, (0,))
        end_mid[side, pl.ds(y, 8)] = u
        return carry

    lax.fori_loop(0, 32, end_block, 0)

    lane = lanes(NY)
    row = lax.broadcasted_iota(jnp.int32, (NY, 128), 0)
    pack[...] = jnp.zeros((NY, 128), F32)
    for x in range(NX):
        before = mid[0, x - 1] if x > 0 else end_mid[0]
        after = mid[0, x + 1] if x < NX - 1 else end_mid[1]
        v = mid[1, x]
        w = mid[2, x]
        v_up = jnp.where(row == NY - 1, 0.0, pltpu.roll(v, NY - 1, 0))
        v_down = jnp.where(row == 0, 0.0, pltpu.roll(v, 1, 0))
        w_up = jnp.where(lane == NZ - 1, 0.0, pltpu.roll(w, NZ - 1, 1))
        w_down = jnp.where(lane == 0, 0.0, pltpu.roll(w, 1, 1))
        s = 2.5 * ((after - before) + (v_up - v_down) + (w_up - w_down))
        source[x] = s
        part = jnp.dot(s, moments[0], precision=HIGHEST, preferred_element_type=F32) + jnp.dot(
            w, moments[1], precision=HIGHEST, preferred_element_type=F32
        )
        pack[...] += pltpu.roll(part, 16 * x, 1) if x else part


def combine_body(a, b, c, d, table, out):
    total = 0.0
    for k, ref in enumerate((a, b, c, d)):
        total = total + jnp.dot(ref[...], table[k], precision=HIGHEST, preferred_element_type=F32)
    out[...] = total


def solve_body(more, *refs):
    (flags, mid, frac, now, source, low, high, far, far_low, far_high, table) = refs[:11]
    vel, pressure = refs[11:13]
    U, Q, lhs = refs[-3:]
    if more:
        right, left, packed, guess = refs[13:17]
    first = flags[0] == 1
    last = flags[1] == 1
    halo = POWERS

    def terms(plane, values, moments, start):
        lane = lanes(NY)
        head = values.astype(BF16)
        tail = (values - head.astype(F32)).astype(BF16)
        m_head = moments.astype(BF16).astype(F32)
        m_tail = moments - m_head
        side = jnp.where(
            lane < 16,
            m_head,
            jnp.where(
                lane < 32,
                pltpu.roll(m_tail, 16, 1),
                jnp.where(lane < 48, pltpu.roll(m_head, 32, 1), 0.0),
            ),
        )
        lhs[:, 0:128] = head
        lhs[:, 128:256] = tail
        lhs[:, 256:384] = head
        lhs[:, 384:512] = side.astype(BF16)
        left_side = lhs[...]
        for kind, out in enumerate((U, Q)):
            base = kind * POWERS * 128
            result = jnp.dot(
                left_side,
                table[:, base + start * 128 : base + POWERS * 128],
                preferred_element_type=F32,
            )
            for m in range(start, POWERS):
                out[m, plane, pl.ds(TOP, NY)] = result[:, (m - start) * 128 : (m - start + 1) * 128]
                ghosts(out, m, plane)

    def ghosts(out, m, plane):
        out[m, plane, pl.ds(TOP - 1, 1)] = out[m, plane, pl.ds(TOP, 1)]
        out[m, plane, pl.ds(TOP + NY, 1)] = out[m, plane, pl.ds(TOP + NY - 1, 1)]

    def own_plane(x, carry):
        moments = pltpu.roll(far[...], (128 - 16 * x) % 128, 1)
        terms(x + halo, source[x], moments, 0)
        return carry

    lax.fori_loop(0, NX, own_plane, 0)
    for k in range(1, halo + 1):
        x = NX - k
        moments = pltpu.roll(far_low[...], (128 - 16 * x) % 128, 1)
        terms(halo - k, low[x], moments, k - 1)
        x = k - 1
        moments = pltpu.roll(far_high[...], (128 - 16 * x) % 128, 1)
        terms(halo + NX - 1 + k, high[x], moments, k - 1)

    for m in range(POWERS - 2, -1, -1):
        for out, extra in ((U, 1), (Q, 0)):
            reach = m + extra

            def sweep(plane, carry, out=out, m=m):
                inside = ((plane >= halo) | jnp.logical_not(first)) & (
                    (plane < halo + NX) | jnp.logical_not(last)
                )
                keep = jnp.where(inside, 1.0, 0.0).astype(F32)
                for y in range(0, NY, 32):
                    here = pl.ds(TOP + y, 32)
                    beside = (out[m + 1, plane - 1, here] + out[m + 1, plane + 1, here]) + (
                        out[m + 1, plane, pl.ds(TOP + y - 1, 32)]
                        + out[m + 1, plane, pl.ds(TOP + y + 1, 32)]
                    )
                    out[m, plane, here] += keep * beside
                ghosts(out, m, plane)
                return carry

            lax.fori_loop(halo - reach, halo + NX + reach, sweep, 0)

    def correct(x, carry):
        plane = x + halo
        for y in range(0, NY, 32):
            here = pl.ds(TOP + y, 32)
            rows = pl.ds(y, 32)
            p = -U[0, plane, here]
            pressure[x, rows] = p
            vel[0, x, rows] = mid[0, x, rows] + 0.1 * (U[0, plane + 1, here] - U[0, plane - 1, here])
            vel[1, x, rows] = mid[1, x, rows] + 0.1 * (
                U[0, plane, pl.ds(TOP + y + 1, 32)] - U[0, plane, pl.ds(TOP + y - 1, 32)]
            )
            vel[2, x, rows] = mid[2, x, rows] + 0.2 * Q[0, plane, here]
            if more:
                guess[x, rows] = 2.0 * p - now[x, rows]
        return carry

    lax.fori_loop(0, NX, correct, 0)
    if more:
        emit_faces(vel, frac, guess, right, left, packed)


def shape(*dims):
    return jax.ShapeDtypeStruct(dims, F32)


IN_VMEM = pl.BlockSpec(memory_space=pltpu.VMEM)
IN_SMEM = pl.BlockSpec(memory_space=pltpu.SMEM)
ANYWHERE = pl.BlockSpec(memory_space=pl.ANY)
PARAMS = pltpu.CompilerParams(vmem_limit_bytes=VMEM_LIMIT)
BLOCK = (NX, NY, NZ)


def pack_call(velocity, fraction, now, old):
    return pl.pallas_call(
        pack_body,
        out_shape=(shape(*BLOCK), shape(*BLOCK), shape(NY, 128), shape(*BLOCK)),
        in_specs=[IN_VMEM] * 4,
        out_specs=(IN_VMEM,) * 4,
        compiler_params=PARAMS,
        name="pack",
    )(velocity, fraction, now, old)


def predict_call(flags, velocity, fraction, guess, low, high, sides, sides_low, sides_high, profile, moments):
    padded = pltpu.VMEM((12, ROWS, NZ), F32)
    return pl.pallas_call(
        predict_body,
        out_shape=(shape(3, *BLOCK), shape(*BLOCK), shape(*BLOCK), shape(NY, 128)),
        in_specs=[IN_SMEM] + [ANYWHERE] * 5 + [IN_VMEM] * 5,
        out_specs=(IN_VMEM,) * 4,
        scratch_shapes=[padded] * 7
        + [
            pltpu.VMEM((NY, 128), F32),
            pltpu.VMEM((2, NY, NZ), F32),
            pltpu.SemaphoreType.DMA((15,)),
        ],
        compiler_params=PARAMS,
        name="predict",
    )(flags, velocity, fraction, guess, low, high, sides, sides_low, sides_high, profile, moments)


def combine_call(packs, table):
    return pl.pallas_call(
        combine_body,
        out_shape=shape(NY, 128),
        in_specs=[IN_VMEM] * 5,
        out_specs=IN_VMEM,
        compiler_params=PARAMS,
        name="combine",
    )(*packs, table)


def solve_call(more, flags, mid, frac, now, source, low, high, far, far_low, far_high, table):
    outs = [shape(3, *BLOCK), shape(*BLOCK)]
    if more:
        outs += [shape(*BLOCK), shape(*BLOCK), shape(NY, 128), shape(*BLOCK)]
    planes = NX + 2 * POWERS
    return pl.pallas_call(
        functools.partial(solve_body, more),
        out_shape=tuple(outs),
        in_specs=[IN_SMEM] + [IN_VMEM] * 10,
        out_specs=(IN_VMEM,) * len(outs),
        scratch_shapes=[
            pltpu.VMEM((POWERS, planes, ROWS, NZ), F32),
            pltpu.VMEM((POWERS, planes, ROWS, NZ), F32),
            pltpu.VMEM((NY, 512), BF16),
        ],
        compiler_params=PARAMS,
        name="solve",
    )(flags, mid, frac, now, source, low, high, far, far_low, far_high, table)


def per_device(velocity, fraction, pressure_now, pressure_old, inflow):
    stream = lax.axis_index("stream")
    count = lax.axis_size("stream")
    flags = jnp.stack([stream == 0, stream == count - 1]).astype(jnp.int32)
    forward = [(i, i + 1) for i in range(count - 1)]
    backward = [(i + 1, i) for i in range(count - 1)]

    def along(block, step):
        return lax.ppermute(block, "stream", forward if step > 0 else backward)

    def around(block, offset):
        return lax.ppermute(
            block, "span", [((i + offset) % BLOCKS, i) for i in range(BLOCKS)]
        )

    profile = jnp.broadcast_to(inflow[:, :, None], (2, NY, NZ))
    odd = lanes(NY) % 2 == 1
    moments = jnp.asarray(moment_table())
    combine = jnp.asarray(combine_table())
    table = jnp.asarray(solve_table())

    right, left, packed, guess = pack_call(velocity, fraction, pressure_now, pressure_old)
    now = pressure_now
    for step in range(STEPS):
        more = step < STEPS - 1
        low = along(right, 1)
        high = along(left, -1)
        sides = jnp.where(odd, around(packed, -1), jnp.roll(around(packed, 1), -2, axis=1))
        sides_low = along(sides, 1)
        sides_high = along(sides, -1)
        mid, fraction, source, pack = predict_call(
            flags, velocity, fraction, guess, low, high, sides, sides_low, sides_high, profile, moments
        )
        source_low = along(source, 1)
        source_high = along(source, -1)
        far = combine_call([pack] + [around(pack, o) for o in (1, 2, 3)], combine)
        far_low = along(far, 1)
        far_high = along(far, -1)
        results = solve_call(
            more, flags, mid, fraction, now, source, source_low, source_high, far, far_low, far_high, table
        )
        velocity, pressure = results[:2]
        old, now = now, pressure
        if more:
            right, left, packed, guess = results[2:]
    return (velocity, fraction, now, old)


def solution(mesh):
    return jax.shard_map(
        per_device,
        mesh=mesh,
        in_specs=(
            P(None, "stream", None, "span"),
            P("stream", None, "span"),
            P("stream", None, "span"),
            P("stream", None, "span"),
            P(),
        ),
        out_specs=(
            P(None, "stream", None, "span"),
            P("stream", None, "span"),
            P("stream", None, "span"),
            P("stream", None, "span"),
        ),
        check_vma=False,
    )
```

time: 516 us -> 246 us (0.48); the launches traced: 510 us -> 246 us
  waiting for transfers between devices: 237 us -> 67.3 us
  other arithmetic: 107 us -> 0.78 us
  Pallas kernels: 0 us -> 85.5 us
  starting transfers between devices: 109 us -> 85.1 us
  matrix products: 18.8 us -> 0 us
  local copies, waits for them, and re-layouts: 22.2 us -> 5.91 us
  between operations: 15.3 us -> 1.01 us
    pallas_call x0 -> x7, Pallas kernels: none -> 85.5 us  [the longest x2 42.3 us: predict_call(): pl.pallas_call(predict_body, out_shape=(shape(3, *BLOCK), shape(*BLOCK),...]
    ppermute x40 -> x26, waiting for transfers between devices: 131 us -> 67.3 us  [the longest x16 34.7 us: along(): return lax.ppermute(block, 'stream', forward if step > 0 else backward)]
    reduce_scatter x2 -> x0, waiting for transfers between devices: 58.6 us -> none  [to_modes(): lax.psum_scatter(jnp.einsum('xyz,zc->cxy', source, own_rows, precision=la...]
    all_gather x2 -> x0, waiting for transfers between devices: 47.2 us -> none  [from_modes(): lax.all_gather(modal, 'span', axis=0, tiled=True)]
    add x10 -> x1, other arithmetic: 38.1 us -> 0.01 us  [per_device(): odd = lanes(NY) % 2 == 1]
    concatenate x11 -> x0, other arithmetic: 25.6 us -> none  [the longest x2 19.8 us: pad_gap(): return jnp.concatenate([bottom, padded, top], axis=2)]
    ppermute x40 -> x26, starting transfers between devices: 109 us -> 85.1 us  [the longest x16 75.2 us: along(): return lax.ppermute(block, 'stream', forward if step > 0 else backward)]
    dot_general x4 -> x0, matrix products: 18.8 us -> none  [the longest x2 10.7 us: to_modes(): jnp.einsum('xyz,zc->cxy', source, own_rows, precision=lax.Precision.HIGHEST)]
  transfers between devices with their start and end apart: 44 -> 26, of which waited for: 26 -> 13; matrix products, arithmetic and copies ran while one was open for 6% -> 0% of each run, Pallas kernels for 0% -> 2%
where the time goes in v1:
time: 246 us
  Pallas kernels  85.5 us (35%)
  starting transfers between devices  85.1 us (35%)
  waiting for transfers between devices  67.3 us (27%)
  local copies, waits for them, and re-layouts  5.91 us (2%)
    ppermute x16, starting transfers between devices, along(): return lax.ppermute(block, 'stream', forward if step > 0 else backward)  75.2 us
    pallas_call x2, Pallas kernels, predict_call(): pl.pallas_call(predict_body, out_shape=(shape(3, *BLOCK), shape(*BLOCK),...  42.3 us
    pallas_call x2, Pallas kernels, solve_call(): pl.pallas_call(functools.partial(solve_body, more), out_shape=tuple(outs)...  35.4 us
    ppermute x16, waiting for transfers between devices, along(): return lax.ppermute(block, 'stream', forward if step > 0 else backward)  34.7 us
    ppermute x10, waiting for transfers between devices, around(): lax.ppermute(block, 'span', [((i + offset) % BLOCKS, i) for i in range(BL...  32.6 us
    ppermute x10, starting transfers between devices, around(): lax.ppermute(block, 'span', [((i + offset) % BLOCKS, i) for i in range(BL...  9.89 us
  transfers between devices with their start and end apart: 26, of which 13 were waited for; matrix products, arithmetic and copies ran while one was open for 0% of the time, Pallas kernels for 2%

profile of v1, /device:TPU:7, one launch (start us, length us, event | category | flops | bytes accessed | tf_op | source)
XLA Modules:
  0.0 245.6 jit_solution(1076865743418495168)
XLA Ops:
  0.6 3.6 %pack.1 = (f32[8,128,128]{2,1,0:T(8,128)}, f32[8,128,128]{2,1,0:T(8,128)}, f32[128,128]{1,0:T(8,128)}, f32[8,128,128]{2,1,0:T(8,128)}) custom-call(f32[3,8,128,128]{3,2,1,0:T(8,128)} %vel.3, f32[8,128,128]{2,1,0:T(8,128)} %frac.3, f32[8,128,128]{2,1,0:T(8,128)} %refs_3_.1, f32[8,128,128]{2,1,0:T(8,128)} %old.1), custom_call_target="tpu_custom_call" | custom-call | tf_op jit(solution)/shard_map/pack/pallas_call | solution.py:460
  6.0 3.5 %collective-permute-start = (f32[8,128,128]{2,1,0:T(8,128)}, f32[8,128,128]{2,1,0:T(8,128)S(1)}, u32[]{:S(2)}, u32[]{:S(2)}) collective-permute-start(f32[8,128,128]{2,1,0:T(8,128)} %get-tuple-element.25), channel_id=1, source_target_pairs={{0,4},{4,8},{8,12},{12,16},{16,20},{20,24},{24,28},{28,32},{32,36}... | collective-permute-start | bytes 1572872 | tf_op jit(solution)/shard_map/ppermute | solution.py:527
  9.5 7.5 %collective-permute-start.1 = (f32[8,128,128]{2,1,0:T(8,128)}, f32[8,128,128]{2,1,0:T(8,128)S(1)}, u32[]{:S(2)}, u32[]{:S(2)}) collective-permute-start(f32[8,128,128]{2,1,0:T(8,128)} %get-tuple-element.26), channel_id=1, source_target_pairs={{4,0},{8,4},{12,8},{16,12},{20,16},{24,20},{28,24},{32,28},{36,32}... | collective-permute-start | bytes 1572872 | tf_op jit(solution)/shard_map/ppermute | solution.py:527
  17.2 3.2 %collective-permute-start.5 = (f32[128,128]{1,0:T(8,128)S(1)}, f32[128,128]{1,0:T(8,128)S(1)}, u32[]{:S(2)}, u32[]{:S(2)}) collective-permute-start(f32[128,128]{1,0:T(8,128)S(1)} %maximum_select_fusion.sides), channel_id=1, source_target_pairs={{4,0},{8,4},{12,8},{16,12},{20,16},{24,20},{28,24},{32,28},{36,32}... | collective-permute-start | bytes 196616 | tf_op jit(solution)/shard_map/ppermute | solution.py:527
  23.1 7.0 %collective-permute-done.5.sides_high = f32[128,128]{1,0:T(8,128)S(1)} collective-permute-done((f32[128,128]{1,0:T(8,128)S(1)}, f32[128,128]{1,0:T(8,128)S(1)}, u32[]{:S(2)}, u32[]{:S(2)}) %collective-permute-start.5) | collective-permute-done | bytes 65568 | tf_op jit(solution)/shard_map/ppermute | solution.py:527
  32.2 21.2 %predict.2 = (f32[3,8,128,128]{3,2,1,0:T(8,128)}, f32[8,128,128]{2,1,0:T(8,128)}, f32[8,128,128]{2,1,0:T(8,128)}, f32[128,128]{1,0:T(8,128)}) custom-call(s32[2]{0:T(128)} %add_convert_fusion.flags.refs_0_, f32[3,8,128,128]{3,2,1,0:T(8,128)} %vel.3, f32[8,128,128]{2,1,0:T(8,128)} %frac.3, f32[8,128,128]{2,1,0:T(8,128)} %get-tuple-element.24.guess, ...), custom_call_target="tpu_custom_call" | custom-call | tf_op jit(solution)/shard_map/predict/pallas_call | solution.py:472
  53.4 8.8 %collective-permute-start.7 = (f32[8,128,128]{2,1,0:T(8,128)}, f32[8,128,128]{2,1,0:T(8,128)S(1)}, u32[]{:S(2)}, u32[]{:S(2)}) collective-permute-start(f32[8,128,128]{2,1,0:T(8,128)} %get-tuple-element.30.refs_4_), channel_id=1, source_target_pairs={{4,0},{8,4},{12,8},{16,12},{20,16},{24,20},{28,24},{32,28},{36,32}... | collective-permute-start | bytes 1572872 | tf_op jit(solution)/shard_map/ppermute | solution.py:527
  66.4 8.2 %collective-permute-done.10.d = f32[128,128]{1,0:T(8,128)S(1)} collective-permute-done((f32[128,128]{1,0:T(8,128)}, f32[128,128]{1,0:T(8,128)S(1)}, u32[]{:S(2)}, u32[]{:S(2)}) %collective-permute-start.10) | collective-permute-done | bytes 65568 | tf_op jit(solution)/shard_map/ppermute | solution.py:530
  74.6 2.3 collective-permute-done.9.c
  80.8 11.3 %collective-permute-start.12 = (f32[128,128]{1,0:T(8,128)}, f32[128,128]{1,0:T(8,128)S(1)}, u32[]{:S(2)}, u32[]{:S(2)}) collective-permute-start(f32[128,128]{1,0:T(8,128)} %combine.2.refs_7_), channel_id=1, source_target_pairs={{4,0},{8,4},{12,8},{16,12},{20,16},{24,20},{28,24},{32,28},{36,32}... | collective-permute-start | bytes 196616 | tf_op jit(solution)/shard_map/ppermute | solution.py:527
  94.1 9.0 %collective-permute-done.11.refs_8_ = f32[128,128]{1,0:T(8,128)S(1)} collective-permute-done((f32[128,128]{1,0:T(8,128)}, f32[128,128]{1,0:T(8,128)S(1)}, u32[]{:S(2)}, u32[]{:S(2)}) %collective-permute-start.11) | collective-permute-done | bytes 65568 | tf_op jit(solution)/shard_map/ppermute | solution.py:527
  104.1 18.1 %solve.2 = (f32[3,8,128,128]{3,2,1,0:T(8,128)}, f32[8,128,128]{2,1,0:T(8,128)}, f32[8,128,128]{2,1,0:T(8,128)}, f32[8,128,128]{2,1,0:T(8,128)}, f32[128,128]{1,0:T(8,128)}, /*index=5*/f32[8,128,128]{2,1,0:T(8,128)}) custom-call(s32[2]{0:T(128)} %add_convert_fusion.flags.refs_0_, f32[3,8,128,128]{3,2,1,0:T(8,128)} %get-tuple-element.28.refs_1_, ...), custom_call_target="tpu_custom_call" | custom-call | tf_op jit(solution)/shard_map/solve/pallas_call | solution.py:504
  124.1 9.1 %collective-permute-start.14 = (f32[8,128,128]{2,1,0:T(8,128)}, f32[8,128,128]{2,1,0:T(8,128)S(1)}, u32[]{:S(2)}, u32[]{:S(2)}) collective-permute-start(f32[8,128,128]{2,1,0:T(8,128)} %get-tuple-element.35), channel_id=1, source_target_pairs={{4,0},{8,4},{12,8},{16,12},{20,16},{24,20},{28,24},{32,28},{36,32}... | collective-permute-start | bytes 1572872 | tf_op jit(solution)/shard_map/ppermute | solution.py:527
  133.2 2.7 %collective-permute-start.16 = (f32[128,128]{1,0:T(8,128)}, f32[128,128]{1,0:T(8,128)S(1)}, u32[]{:S(2)}, u32[]{:S(2)}) collective-permute-start(f32[128,128]{1,0:T(8,128)} %get-tuple-element.36), channel_id=1, source_target_pairs={{1,0},{2,1},{3,2},{0,3},{5,4},{6,5},{7,6},{4,7},{9,8},{10,9},{11,1... | collective-permute-start | bytes 196616 | tf_op jit(solution)/shard_map/ppermute | solution.py:530
  135.9 10.9 %collective-permute-done.16 = f32[128,128]{1,0:T(8,128)S(1)} collective-permute-done((f32[128,128]{1,0:T(8,128)}, f32[128,128]{1,0:T(8,128)S(1)}, u32[]{:S(2)}, u32[]{:S(2)}) %collective-permute-start.16) | collective-permute-done | bytes 65568 | tf_op jit(solution)/shard_map/ppermute | solution.py:530
  148.9 3.4 %collective-permute-start.17 = (f32[128,128]{1,0:T(8,128)S(1)}, f32[128,128]{1,0:T(8,128)S(1)}, u32[]{:S(2)}, u32[]{:S(2)}) collective-permute-start(f32[128,128]{1,0:T(8,128)S(1)} %maximum_select_fusion.1.sides), channel_id=1, source_target_pairs={{0,4},{4,8},{8,12},{12,16},{16,20},{20,24},{24,28},{28,32},{32,36}... | collective-permute-start | bytes 196616 | tf_op jit(solution)/shard_map/ppermute | solution.py:527
  152.4 7.6 %collective-permute-done.17.sides_low = f32[128,128]{1,0:T(8,128)S(1)} collective-permute-done((f32[128,128]{1,0:T(8,128)S(1)}, f32[128,128]{1,0:T(8,128)S(1)}, u32[]{:S(2)}, u32[]{:S(2)}) %collective-permute-start.17) | collective-permute-done | bytes 65568 | tf_op jit(solution)/shard_map/ppermute | solution.py:527
  161.0 21.2 %predict.3 = (f32[3,8,128,128]{3,2,1,0:T(8,128)}, f32[8,128,128]{2,1,0:T(8,128)}, f32[8,128,128]{2,1,0:T(8,128)}, f32[128,128]{1,0:T(8,128)}) custom-call(s32[2]{0:T(128)} %add_convert_fusion.flags.refs_0_, f32[3,8,128,128]{3,2,1,0:T(8,128)} %get-tuple-element.32.vel, f32[8,128,128]{2,1,0:T(8,128)} %get-tuple-element.29.refs_2_.frac, ...), custom_call_target="tpu_custom_call" | custom-call | tf_op jit(solution)/shard_map/predict/pallas_call | solution.py:472
  184.1 3.4 %collective-permute-start.19 = (f32[8,128,128]{2,1,0:T(8,128)}, f32[8,128,128]{2,1,0:T(8,128)S(1)}, u32[]{:S(2)}, u32[]{:S(2)}) collective-permute-start(f32[8,128,128]{2,1,0:T(8,128)} %get-tuple-element.40.refs_4_), channel_id=1, source_target_pairs={{0,4},{4,8},{8,12},{12,16},{16,20},{20,24},{24,28},{28,32},{32,36}... | collective-permute-start | bytes 1572872 | tf_op jit(solution)/shard_map/ppermute | solution.py:527
  190.7 5.6 %collective-permute-done.23.d = f32[128,128]{1,0:T(8,128)S(1)} collective-permute-done((f32[128,128]{1,0:T(8,128)}, f32[128,128]{1,0:T(8,128)S(1)}, u32[]{:S(2)}, u32[]{:S(2)}) %collective-permute-start.23) | collective-permute-done | bytes 65568 | tf_op jit(solution)/shard_map/ppermute | solution.py:530
  196.3 4.3 %collective-permute-done.22.c = f32[128,128]{1,0:T(8,128)S(1)} collective-permute-done((f32[128,128]{1,0:T(8,128)}, f32[128,128]{1,0:T(8,128)S(1)}, u32[]{:S(2)}, u32[]{:S(2)}) %collective-permute-start.22) | collective-permute-done | bytes 65568 | tf_op jit(solution)/shard_map/ppermute | solution.py:530
  204.0 11.5 %collective-permute-start.25 = (f32[128,128]{1,0:T(8,128)}, f32[128,128]{1,0:T(8,128)S(1)}, u32[]{:S(2)}, u32[]{:S(2)}) collective-permute-start(f32[128,128]{1,0:T(8,128)} %combine.3.refs_7_), channel_id=1, source_target_pairs={{4,0},{8,4},{12,8},{16,12},{20,16},{24,20},{28,24},{32,28},{36,32}... | collective-permute-start | bytes 196616 | tf_op jit(solution)/shard_map/ppermute | solution.py:527
  217.5 9.8 %collective-permute-done.24.refs_8_ = f32[128,128]{1,0:T(8,128)S(1)} collective-permute-done((f32[128,128]{1,0:T(8,128)}, f32[128,128]{1,0:T(8,128)S(1)}, u32[]{:S(2)}, u32[]{:S(2)}) %collective-permute-start.24) | collective-permute-done | bytes 65568 | tf_op jit(solution)/shard_map/ppermute | solution.py:527
  228.3 17.3 %solve.3 = (f32[3,8,128,128]{3,2,1,0:T(8,128)}, f32[8,128,128]{2,1,0:T(8,128)}) custom-call(s32[2]{0:T(128)} %add_convert_fusion.flags.refs_0_, f32[3,8,128,128]{3,2,1,0:T(8,128)} %get-tuple-element.37.refs_1_, f32[8,128,128]{2,1,0:T(8,128)} %get-tuple-element.21.refs_2_, f32[8,128,128]{2,1,0:T(8,128)} %get-tuple-element.23.refs_3_, ...), custom_call_target="tpu_custom_call" | custom-call | tf_op jit(solution)/shard_map/solve/pallas_call | solution.py:504
  (94 shorter events, 34.1 us)
Async XLA Ops:
  4.2 12.8 %collective-permute-start.3 = (f32[128,128]{1,0:T(8,128)}, f32[128,128]{1,0:T(8,128)S(1)}, u32[]{:S(2)}, u32[]{:S(2)}) collective-permute-start(f32[128,128]{1,0:T(8,128)} %get-tuple-element.27), channel_id=1, source_target_pairs={{1,0},{2,1},{3,2},{0,3},{5,4},{6,5},{7,6},{4,7},{9,8},{10,9},{11,1... | collective-permute-start | bytes 196616 | tf_op jit(solution)/shard_map/ppermute | solution.py:530
  4.9 12.2 %collective-permute-start.2 = (f32[128,128]{1,0:T(8,128)}, f32[128,128]{1,0:T(8,128)S(1)}, u32[]{:S(2)}, u32[]{:S(2)}) collective-permute-start(f32[128,128]{1,0:T(8,128)} %get-tuple-element.27), channel_id=1, source_target_pairs={{3,0},{0,1},{1,2},{2,3},{7,4},{4,5},{5,6},{6,7},{11,8},{8,9},{9,10... | collective-permute-start | bytes 196616 | tf_op jit(solution)/shard_map/ppermute | solution.py:530
  6.0 25.2 %collective-permute-start = (f32[8,128,128]{2,1,0:T(8,128)}, f32[8,128,128]{2,1,0:T(8,128)S(1)}, u32[]{:S(2)}, u32[]{:S(2)}) collective-permute-start(f32[8,128,128]{2,1,0:T(8,128)} %get-tuple-element.25), channel_id=1, source_target_pairs={{0,4},{4,8},{8,12},{12,16},{16,20},{20,24},{24,28},{28,32},{32,36}... | collective-permute-start | bytes 1572872 | tf_op jit(solution)/shard_map/ppermute | solution.py:527
  9.5 21.7 %collective-permute-start.1 = (f32[8,128,128]{2,1,0:T(8,128)}, f32[8,128,128]{2,1,0:T(8,128)S(1)}, u32[]{:S(2)}, u32[]{:S(2)}) collective-permute-start(f32[8,128,128]{2,1,0:T(8,128)} %get-tuple-element.26), channel_id=1, source_target_pairs={{4,0},{8,4},{12,8},{16,12},{20,16},{24,20},{28,24},{32,28},{36,32}... | collective-permute-start | bytes 1572872 | tf_op jit(solution)/shard_map/ppermute | solution.py:527
  17.2 12.9 %collective-permute-start.5 = (f32[128,128]{1,0:T(8,128)S(1)}, f32[128,128]{1,0:T(8,128)S(1)}, u32[]{:S(2)}, u32[]{:S(2)}) collective-permute-start(f32[128,128]{1,0:T(8,128)S(1)} %maximum_select_fusion.sides), channel_id=1, source_target_pairs={{4,0},{8,4},{12,8},{16,12},{20,16},{24,20},{28,24},{32,28},{36,32}... | collective-permute-start | bytes 196616 | tf_op jit(solution)/shard_map/ppermute | solution.py:527
  20.5 10.7 %collective-permute-start.4 = (f32[128,128]{1,0:T(8,128)S(1)}, f32[128,128]{1,0:T(8,128)S(1)}, u32[]{:S(2)}, u32[]{:S(2)}) collective-permute-start(f32[128,128]{1,0:T(8,128)S(1)} %maximum_select_fusion.sides), channel_id=1, source_target_pairs={{0,4},{4,8},{8,12},{12,16},{16,20},{20,24},{24,28},{28,32},{32,36}... | collective-permute-start | bytes 196616 | tf_op jit(solution)/shard_map/ppermute | solution.py:527
  53.4 49.7 %collective-permute-start.7 = (f32[8,128,128]{2,1,0:T(8,128)}, f32[8,128,128]{2,1,0:T(8,128)S(1)}, u32[]{:S(2)}, u32[]{:S(2)}) collective-permute-start(f32[8,128,128]{2,1,0:T(8,128)} %get-tuple-element.30.refs_4_), channel_id=1, source_target_pairs={{4,0},{8,4},{12,8},{16,12},{20,16},{24,20},{28,24},{32,28},{36,32}... | collective-permute-start | bytes 1572872 | tf_op jit(solution)/shard_map/ppermute | solution.py:527
  62.2 40.9 %collective-permute-start.6 = (f32[8,128,128]{2,1,0:T(8,128)}, f32[8,128,128]{2,1,0:T(8,128)S(1)}, u32[]{:S(2)}, u32[]{:S(2)}) collective-permute-start(f32[8,128,128]{2,1,0:T(8,128)} %get-tuple-element.30.refs_4_), channel_id=1, source_target_pairs={{0,4},{4,8},{8,12},{12,16},{16,20},{20,24},{24,28},{28,32},{32,36}... | collective-permute-start | bytes 1572872 | tf_op jit(solution)/shard_map/ppermute | solution.py:527
  64.1 10.5 %collective-permute-start.10 = (f32[128,128]{1,0:T(8,128)}, f32[128,128]{1,0:T(8,128)S(1)}, u32[]{:S(2)}, u32[]{:S(2)}) collective-permute-start(f32[128,128]{1,0:T(8,128)} %get-tuple-element.31.a), channel_id=1, source_target_pairs={{3,0},{0,1},{1,2},{2,3},{7,4},{4,5},{5,6},{6,7},{11,8},{8,9},{9,10... | collective-permute-start | bytes 196616 | tf_op jit(solution)/shard_map/ppermute | solution.py:530
  65.5 11.4 %collective-permute-start.9 = (f32[128,128]{1,0:T(8,128)}, f32[128,128]{1,0:T(8,128)S(1)}, u32[]{:S(2)}, u32[]{:S(2)}) collective-permute-start(f32[128,128]{1,0:T(8,128)} %get-tuple-element.31.a), channel_id=1, source_target_pairs={{2,0},{3,1},{0,2},{1,3},{6,4},{7,5},{4,6},{5,7},{10,8},{11,9},{8,1... | collective-permute-start | bytes 196616 | tf_op jit(solution)/shard_map/ppermute | solution.py:530
  66.4 11.7 %collective-permute-start.8 = (f32[128,128]{1,0:T(8,128)}, f32[128,128]{1,0:T(8,128)S(1)}, u32[]{:S(2)}, u32[]{:S(2)}) collective-permute-start(f32[128,128]{1,0:T(8,128)} %get-tuple-element.31.a), channel_id=1, source_target_pairs={{1,0},{2,1},{3,2},{0,3},{5,4},{6,5},{7,6},{4,7},{9,8},{10,9},{11,1... | collective-permute-start | bytes 196616 | tf_op jit(solution)/shard_map/ppermute | solution.py:530
  80.8 13.2 %collective-permute-start.12 = (f32[128,128]{1,0:T(8,128)}, f32[128,128]{1,0:T(8,128)S(1)}, u32[]{:S(2)}, u32[]{:S(2)}) collective-permute-start(f32[128,128]{1,0:T(8,128)} %combine.2.refs_7_), channel_id=1, source_target_pairs={{4,0},{8,4},{12,8},{16,12},{20,16},{24,20},{28,24},{32,28},{36,32}... | collective-permute-start | bytes 196616 | tf_op jit(solution)/shard_map/ppermute | solution.py:527
  92.1 10.9 %collective-permute-start.11 = (f32[128,128]{1,0:T(8,128)}, f32[128,128]{1,0:T(8,128)S(1)}, u32[]{:S(2)}, u32[]{:S(2)}) collective-permute-start(f32[128,128]{1,0:T(8,128)} %combine.2.refs_7_), channel_id=1, source_target_pairs={{0,4},{4,8},{8,12},{12,16},{16,20},{20,24},{24,28},{28,32},{32,36}... | collective-permute-start | bytes 196616 | tf_op jit(solution)/shard_map/ppermute | solution.py:527
  122.2 37.8 %collective-permute-start.13 = (f32[8,128,128]{2,1,0:T(8,128)}, f32[8,128,128]{2,1,0:T(8,128)S(1)}, u32[]{:S(2)}, u32[]{:S(2)}) collective-permute-start(f32[8,128,128]{2,1,0:T(8,128)} %get-tuple-element.34), channel_id=1, source_target_pairs={{0,4},{4,8},{8,12},{12,16},{16,20},{20,24},{24,28},{28,32},{32,36}... | collective-permute-start | bytes 1572872 | tf_op jit(solution)/shard_map/ppermute | solution.py:527
  124.1 35.9 %collective-permute-start.14 = (f32[8,128,128]{2,1,0:T(8,128)}, f32[8,128,128]{2,1,0:T(8,128)S(1)}, u32[]{:S(2)}, u32[]{:S(2)}) collective-permute-start(f32[8,128,128]{2,1,0:T(8,128)} %get-tuple-element.35), channel_id=1, source_target_pairs={{4,0},{8,4},{12,8},{16,12},{20,16},{24,20},{28,24},{32,28},{36,32}... | collective-permute-start | bytes 1572872 | tf_op jit(solution)/shard_map/ppermute | solution.py:527
  133.2 13.6 %collective-permute-start.16 = (f32[128,128]{1,0:T(8,128)}, f32[128,128]{1,0:T(8,128)S(1)}, u32[]{:S(2)}, u32[]{:S(2)}) collective-permute-start(f32[128,128]{1,0:T(8,128)} %get-tuple-element.36), channel_id=1, source_target_pairs={{1,0},{2,1},{3,2},{0,3},{5,4},{6,5},{7,6},{4,7},{9,8},{10,9},{11,1... | collective-permute-start | bytes 196616 | tf_op jit(solution)/shard_map/ppermute | solution.py:530
  135.9 11.0 %collective-permute-start.15 = (f32[128,128]{1,0:T(8,128)}, f32[128,128]{1,0:T(8,128)S(1)}, u32[]{:S(2)}, u32[]{:S(2)}) collective-permute-start(f32[128,128]{1,0:T(8,128)} %get-tuple-element.36), channel_id=1, source_target_pairs={{3,0},{0,1},{1,2},{2,3},{7,4},{4,5},{5,6},{6,7},{11,8},{8,9},{9,10... | collective-permute-start | bytes 196616 | tf_op jit(solution)/shard_map/ppermute | solution.py:530
  148.9 11.1 %collective-permute-start.17 = (f32[128,128]{1,0:T(8,128)S(1)}, f32[128,128]{1,0:T(8,128)S(1)}, u32[]{:S(2)}, u32[]{:S(2)}) collective-permute-start(f32[128,128]{1,0:T(8,128)S(1)} %maximum_select_fusion.1.sides), channel_id=1, source_target_pairs={{0,4},{4,8},{8,12},{12,16},{16,20},{20,24},{24,28},{28,32},{32,36}... | collective-permute-start | bytes 196616 | tf_op jit(solution)/shard_map/ppermute | solution.py:527
  182.2 45.1 %collective-permute-start.20 = (f32[8,128,128]{2,1,0:T(8,128)}, f32[8,128,128]{2,1,0:T(8,128)S(1)}, u32[]{:S(2)}, u32[]{:S(2)}) collective-permute-start(f32[8,128,128]{2,1,0:T(8,128)} %get-tuple-element.40.refs_4_), channel_id=1, source_target_pairs={{4,0},{8,4},{12,8},{16,12},{20,16},{24,20},{28,24},{32,28},{36,32}... | collective-permute-start | bytes 1572872 | tf_op jit(solution)/shard_map/ppermute | solution.py:527
  184.1 43.2 %collective-permute-start.19 = (f32[8,128,128]{2,1,0:T(8,128)}, f32[8,128,128]{2,1,0:T(8,128)S(1)}, u32[]{:S(2)}, u32[]{:S(2)}) collective-permute-start(f32[8,128,128]{2,1,0:T(8,128)} %get-tuple-element.40.refs_4_), channel_id=1, source_target_pairs={{0,4},{4,8},{8,12},{12,16},{16,20},{20,24},{24,28},{28,32},{32,36}... | collective-permute-start | bytes 1572872 | tf_op jit(solution)/shard_map/ppermute | solution.py:527
  189.0 11.6 %collective-permute-start.22 = (f32[128,128]{1,0:T(8,128)}, f32[128,128]{1,0:T(8,128)S(1)}, u32[]{:S(2)}, u32[]{:S(2)}) collective-permute-start(f32[128,128]{1,0:T(8,128)} %get-tuple-element.41.a), channel_id=1, source_target_pairs={{2,0},{3,1},{0,2},{1,3},{6,4},{7,5},{4,6},{5,7},{10,8},{11,9},{8,1... | collective-permute-start | bytes 196616 | tf_op jit(solution)/shard_map/ppermute | solution.py:530
  190.7 9.9 %collective-permute-start.21 = (f32[128,128]{1,0:T(8,128)}, f32[128,128]{1,0:T(8,128)S(1)}, u32[]{:S(2)}, u32[]{:S(2)}) collective-permute-start(f32[128,128]{1,0:T(8,128)} %get-tuple-element.41.a), channel_id=1, source_target_pairs={{1,0},{2,1},{3,2},{0,3},{5,4},{6,5},{7,6},{4,7},{9,8},{10,9},{11,1... | collective-permute-start | bytes 196616 | tf_op jit(solution)/shard_map/ppermute | solution.py:530
  204.0 13.5 %collective-permute-start.25 = (f32[128,128]{1,0:T(8,128)}, f32[128,128]{1,0:T(8,128)S(1)}, u32[]{:S(2)}, u32[]{:S(2)}) collective-permute-start(f32[128,128]{1,0:T(8,128)} %combine.3.refs_7_), channel_id=1, source_target_pairs={{4,0},{8,4},{12,8},{16,12},{20,16},{24,20},{28,24},{32,28},{36,32}... | collective-permute-start | bytes 196616 | tf_op jit(solution)/shard_map/ppermute | solution.py:527
  215.5 11.8 %collective-permute-start.24 = (f32[128,128]{1,0:T(8,128)}, f32[128,128]{1,0:T(8,128)S(1)}, u32[]{:S(2)}, u32[]{:S(2)}) collective-permute-start(f32[128,128]{1,0:T(8,128)} %combine.3.refs_7_), channel_id=1, source_target_pairs={{0,4},{4,8},{8,12},{12,16},{16,20},{20,24},{24,28},{28,32},{32,36}... | collective-permute-start | bytes 196616 | tf_op jit(solution)/shard_map/ppermute | solution.py:527
  (27 other events, 122.4 us)

commit v2 on v1

--- a/solution.py
+++ b/solution.py
@@ -18,7 +18,7 @@
 F32 = jnp.float32
 BF16 = jnp.bfloat16
 HIGHEST = lax.Precision.HIGHEST
-VMEM_LIMIT = 60 * 1024 * 1024
+MIB = 1024 * 1024
 
 
 def comb(n, k):
@@ -55,9 +55,11 @@
         near[m, NZ + POWERS : NZ + 2 * POWERS] = far[:, ::-1]
         near[m, NZ + 14] = -2.5 * near[m, 0]
         near[m, NZ + 15] = 2.5 * near[m, NZ - 1]
-    value = near[:, :, 1:-1]
-    slope = 0.5 * (near[:, :, 2:] - near[:, :, :-2])
-    wide = np.concatenate([value, slope]).transpose(1, 0, 2).reshape(144, 2 * POWERS * NZ)
+    wide = np.zeros((144, (POWERS + 1) * NZ))
+    wide[:, : POWERS * NZ] = near[:, :, 1:-1].transpose(1, 0, 2).reshape(144, POWERS * NZ)
+    for m in range(POWERS):
+        wide[:, POWERS * NZ + 2 * m] = near[m, :, -1]
+        wide[:, POWERS * NZ + 2 * m + 1] = near[m, :, 0]
     wide = wide.astype(np.float32)
     head = wide.astype(jnp.bfloat16)
     tail = (wide - head.astype(np.float32)).astype(jnp.bfloat16)
@@ -123,23 +125,23 @@
     return packed
 
 
-def pack_body(vel, frac, now, old, right, left, packed, guess):
+def pack_body(flags, vel, frac, now, old, paired, other, packed, guess):
     for x in range(NX):
         guess[x] = 2.0 * now[x] - old[x]
-    emit_faces(vel, frac, guess, right, left, packed)
-
-
-def emit_faces(vel, frac, guess, right, left, packed):
-    right[0:2] = vel[0, 6:8]
-    right[2] = vel[1, 7]
-    right[3] = vel[2, 7]
-    right[4:6] = frac[6:8]
-    right[6:8] = guess[6:8]
-    left[0:2] = vel[0, 0:2]
-    left[2] = vel[1, 0]
-    left[3] = vel[2, 0]
-    left[4:6] = frac[0:2]
-    left[6:8] = guess[0:2]
+    emit_faces(flags, vel, frac, guess, paired, other, packed)
+
+
+def emit_faces(flags, vel, frac, guess, paired, other, packed):
+    even = flags[2] == 1
+    for out, upper in ((paired, even), (other, jnp.logical_not(even))):
+        two = jnp.where(upper, NX - 2, 0)
+        one = jnp.where(upper, NX - 1, 0)
+        for k in range(2):
+            out[k] = vel[0, two + k]
+            out[4 + k] = frac[two + k]
+            out[6 + k] = guess[two + k]
+        out[2] = vel[1, one]
+        out[3] = vel[2, one]
 
     def field(k, x):
         return vel[k, x] if k < 3 else (frac[x] if k == 3 else guess[x])
@@ -148,9 +150,9 @@
 
 
 def predict_body(
-    flags, vel, frac, guess, low, high, sides, sides_low, sides_high, profile, moments,
+    flags, vel, frac, guess, paired, other, sides, profile, moments,
     mid, frac_new, source, pack,
-    U, V, W, F, G, FM, FP, Z, end_mid, sem,
+    U, V, W, F, G, FM, FP, Z, Z_ends, end_mid, sem,
 ):
     own = pl.ds(TOP, NY)
     copies = []
@@ -164,12 +166,18 @@
         fetch(vel.at[k], buf.at[pl.ds(2, NX), own])
     fetch(frac, F.at[pl.ds(2, NX), own])
     fetch(guess, G.at[pl.ds(2, NX), own])
-    for msg, far, near in ((low, 0, 1), (high, 10, 10)):
+    even = flags[2] == 1
+    for msg, upper in ((paired, even), (other, jnp.logical_not(even))):
+        far = jnp.where(upper, 10, 0)
+        near = jnp.where(upper, 10, 1)
         fetch(msg.at[pl.ds(0, 2)], U.at[pl.ds(far, 2), own])
         fetch(msg.at[2], V.at[near, own])
         fetch(msg.at[3], W.at[near, own])
         fetch(msg.at[pl.ds(4, 2)], F.at[pl.ds(far, 2), own])
         fetch(msg.at[pl.ds(6, 2)], G.at[pl.ds(far, 2), own])
+        fetch(msg.at[8], Z_ends.at[jnp.where(upper, 1, 0)])
+    for copy in copies:
+        copy.wait()
 
     first = flags[0] == 1
     last = flags[1] == 1
@@ -178,16 +186,13 @@
     slot = place % 12
     group = place // 12
     merged = sides[...]
-    below = pltpu.roll(sides_low[...], 112, 1)
-    above = pltpu.roll(sides_high[...], 16, 1)
+    below = pltpu.roll(Z_ends[0], 112, 1)
+    above = pltpu.roll(Z_ends[1], 16, 1)
     below_wall = jnp.where(group == 0, profile[0], jnp.where(group == 3, profile[1], 0.0))
     above_wall = jnp.where(slot == 10, pltpu.roll(merged, 2, 1), pltpu.roll(merged, 4, 1))
     below = jnp.where(first, below_wall, below)
     above = jnp.where(last, above_wall, above)
     Z[...] = jnp.where(slot < 2, below, jnp.where(slot >= 10, above, merged))
-
-    for copy in copies:
-        copy.wait()
 
     @pl.when(first)
     def _():
@@ -306,7 +311,7 @@
         frac_new[x, rows] = f
         return carry
 
-    lax.fori_loop(0, 16 * NX, block, 0)
+    lax.fori_loop(0, 16 * NX, block, 0, unroll=4)
 
     def end_block(i, carry):
         side = i // 16
@@ -315,7 +320,7 @@
         end_mid[side, pl.ds(y, 8)] = u
         return carry
 
-    lax.fori_loop(0, 32, end_block, 0)
+    lax.fori_loop(0, 32, end_block, 0, unroll=4)
 
     lane = lanes(NY)
     row = lax.broadcasted_iota(jnp.int32, (NY, 128), 0)
@@ -337,19 +342,32 @@
         pack[...] += pltpu.roll(part, 16 * x, 1) if x else part
 
 
-def combine_body(a, b, c, d, table, out):
+def combine_body(a, b, c, d, table, _, message, out, sem):
     total = 0.0
     for k, ref in enumerate((a, b, c, d)):
         total = total + jnp.dot(ref[...], table[k], precision=HIGHEST, preferred_element_type=F32)
     out[...] = total
+    copy = pltpu.make_async_copy(out, message.at[NX], sem)
+    copy.start()
+    copy.wait()
+
+
+def merge_body(before, after, _, __, right, left, out, sem):
+    lane = lanes(NY)
+    out[...] = jnp.where(lane % 2 == 1, before[...], pltpu.roll(after[...], 126, 1))
+    copies = [pltpu.make_async_copy(out, m.at[NX], sem.at[k]) for k, m in enumerate((right, left))]
+    for copy in copies:
+        copy.start()
+    for copy in copies:
+        copy.wait()
 
 
 def solve_body(more, *refs):
-    (flags, mid, frac, now, source, low, high, far, far_low, far_high, table) = refs[:11]
-    vel, pressure = refs[11:13]
-    U, Q, lhs = refs[-3:]
+    (flags, mid, frac, now, source, paired, other, far, table) = refs[:9]
+    vel, pressure = refs[9:11]
+    U, E, lhs = refs[-3:]
     if more:
-        right, left, packed, guess = refs[13:17]
+        faces_paired, faces_other, packed, guess = refs[11:15]
     first = flags[0] == 1
     last = flags[1] == 1
     halo = POWERS
@@ -373,17 +391,17 @@
         lhs[:, 128:256] = tail
         lhs[:, 256:384] = head
         lhs[:, 384:512] = side.astype(BF16)
-        left_side = lhs[...]
-        for kind, out in enumerate((U, Q)):
-            base = kind * POWERS * 128
-            result = jnp.dot(
-                left_side,
-                table[:, base + start * 128 : base + POWERS * 128],
-                preferred_element_type=F32,
-            )
-            for m in range(start, POWERS):
-                out[m, plane, pl.ds(TOP, NY)] = result[:, (m - start) * 128 : (m - start + 1) * 128]
-                ghosts(out, m, plane)
+        result = jnp.dot(lhs[...], table[:, start * 128 :], preferred_element_type=F32)
+        for m in range(start, POWERS):
+            U[m, plane, pl.ds(TOP, NY)] = result[:, (m - start) * 128 : (m - start + 1) * 128]
+            ghosts(U, m, plane)
+        ends = result[:, (POWERS - start) * 128 :]
+        group, offset = plane // 8, 16 * (plane % 8)
+        E[group] += pltpu.roll(ends, offset, 1)
+
+    def inside(plane):
+        kept = ((plane >= halo) | jnp.logical_not(first)) & ((plane < halo + NX) | jnp.logical_not(last))
+        return jnp.where(kept, 1.0, 0.0).astype(F32)
 
     def ghosts(out, m, plane):
         out[m, plane, pl.ds(TOP - 1, 1)] = out[m, plane, pl.ds(TOP, 1)]
@@ -394,38 +412,64 @@
         terms(x + halo, source[x], moments, 0)
         return carry
 
+    E[...] = jnp.zeros((3, NY, 128), F32)
     lax.fori_loop(0, NX, own_plane, 0)
+    even = flags[2] == 1
     for k in range(1, halo + 1):
-        x = NX - k
-        moments = pltpu.roll(far_low[...], (128 - 16 * x) % 128, 1)
-        terms(halo - k, low[x], moments, k - 1)
-        x = k - 1
-        moments = pltpu.roll(far_high[...], (128 - 16 * x) % 128, 1)
-        terms(halo + NX - 1 + k, high[x], moments, k - 1)
+        for message, upper in ((paired, even), (other, jnp.logical_not(even))):
+            x = jnp.where(upper, k - 1, NX - k)
+            moments = pltpu.roll(message[NX], (128 - 16 * x) % 128, 1)
+            terms(jnp.where(upper, halo + NX - 1 + k, halo - k), message[x], moments, k - 1)
 
     for m in range(POWERS - 2, -1, -1):
-        for out, extra in ((U, 1), (Q, 0)):
-            reach = m + extra
-
-            def sweep(plane, carry, out=out, m=m):
-                inside = ((plane >= halo) | jnp.logical_not(first)) & (
-                    (plane < halo + NX) | jnp.logical_not(last)
+        reach = m + 1
+
+        def sweep(plane, carry, m=m):
+            keep = inside(plane)
+            for y in range(0, NY, 32):
+                here = pl.ds(TOP + y, 32)
+                beside = (U[m + 1, plane - 1, here] + U[m + 1, plane + 1, here]) + (
+                    U[m + 1, plane, pl.ds(TOP + y - 1, 32)]
+                    + U[m + 1, plane, pl.ds(TOP + y + 1, 32)]
                 )
-                keep = jnp.where(inside, 1.0, 0.0).astype(F32)
-                for y in range(0, NY, 32):
-                    here = pl.ds(TOP + y, 32)
-                    beside = (out[m + 1, plane - 1, here] + out[m + 1, plane + 1, here]) + (
-                        out[m + 1, plane, pl.ds(TOP + y - 1, 32)]
-                        + out[m + 1, plane, pl.ds(TOP + y + 1, 32)]
-                    )
-                    out[m, plane, here] += keep * beside
-                ghosts(out, m, plane)
-                return carry
-
-            lax.fori_loop(halo - reach, halo + NX + reach, sweep, 0)
+                U[m, plane, here] += keep * beside
+            ghosts(U, m, plane)
+            return carry
+
+        lax.fori_loop(halo - reach, halo + NX + reach, sweep, 0)
+
+    lane = lanes(NY)
+    row = lax.broadcasted_iota(jnp.int32, (NY, 128), 0)
+    used = lane % 16 < 14
+    keeps = []
+    for g in range(3):
+        plane = 8 * g + lane // 16
+        keeps.append(jnp.where(used, inside(plane), 0.0))
+    start = [E[g] for g in range(3)]
+    ends = start
+    for m in range(POWERS - 1):
+        before = [pltpu.roll(e, 14, 1) for e in ends]
+        after = [pltpu.roll(e, 110, 1) for e in ends]
+        same = [pltpu.roll(e, 126, 1) for e in ends]
+        updated = []
+        for g in range(3):
+            behind = jnp.where(lane < 16, before[g - 1], before[g]) if g else before[0]
+            ahead = jnp.where(lane >= 112, after[g + 1], after[g]) if g < 2 else after[2]
+            up = jnp.where(row == NY - 1, same[g], pltpu.roll(same[g], NY - 1, 0))
+            down = jnp.where(row == 0, same[g], pltpu.roll(same[g], 1, 0))
+            updated.append(start[g] + keeps[g] * ((behind + ahead) + (up + down)))
+        ends = updated
+    for g in range(3):
+        E[g] = ends[g]
 
     def correct(x, carry):
         plane = x + halo
+        lane = lanes(NY)
+        turned = pltpu.roll(E[plane // 8], (128 - 16 * (plane % 8) - 1) % 128, 1)
+        centre = U[0, plane, pl.ds(TOP, NY)]
+        ahead = jnp.where(lane == NZ - 1, turned, pltpu.roll(centre, NZ - 1, 1))
+        behind = jnp.where(lane == 0, turned, pltpu.roll(centre, 1, 1))
+        vel[2, x] = mid[2, x] + 0.1 * (ahead - behind)
         for y in range(0, NY, 32):
             here = pl.ds(TOP + y, 32)
             rows = pl.ds(y, 32)
@@ -435,14 +479,13 @@
             vel[1, x, rows] = mid[1, x, rows] + 0.1 * (
                 U[0, plane, pl.ds(TOP + y + 1, 32)] - U[0, plane, pl.ds(TOP + y - 1, 32)]
             )
-            vel[2, x, rows] = mid[2, x, rows] + 0.2 * Q[0, plane, here]
             if more:
                 guess[x, rows] = 2.0 * p - now[x, rows]
         return carry
 
     lax.fori_loop(0, NX, correct, 0)
     if more:
-        emit_faces(vel, frac, guess, right, left, packed)
+        emit_faces(flags, vel, frac, guess, faces_paired, faces_other, packed)
 
 
 def shape(*dims):
@@ -452,79 +495,95 @@
 IN_VMEM = pl.BlockSpec(memory_space=pltpu.VMEM)
 IN_SMEM = pl.BlockSpec(memory_space=pltpu.SMEM)
 ANYWHERE = pl.BlockSpec(memory_space=pl.ANY)
-PARAMS = pltpu.CompilerParams(vmem_limit_bytes=VMEM_LIMIT)
 BLOCK = (NX, NY, NZ)
-
-
-def pack_call(velocity, fraction, now, old):
+MESSAGE = (NX + 1, NY, NZ)
+
+
+def pack_call(flags, velocity, fraction, now, old):
     return pl.pallas_call(
         pack_body,
-        out_shape=(shape(*BLOCK), shape(*BLOCK), shape(NY, 128), shape(*BLOCK)),
-        in_specs=[IN_VMEM] * 4,
+        out_shape=(shape(*MESSAGE), shape(*MESSAGE), shape(NY, 128), shape(*BLOCK)),
+        in_specs=[IN_SMEM] + [IN_VMEM] * 4,
         out_specs=(IN_VMEM,) * 4,
-        compiler_params=PARAMS,
+        compiler_params=pltpu.CompilerParams(vmem_limit_bytes=10 * MIB),
         name="pack",
-    )(velocity, fraction, now, old)
-
-
-def predict_call(flags, velocity, fraction, guess, low, high, sides, sides_low, sides_high, profile, moments):
+    )(flags, velocity, fraction, now, old)
+
+
+def predict_call(flags, velocity, fraction, guess, paired, other, sides, profile, moments):
     padded = pltpu.VMEM((12, ROWS, NZ), F32)
     return pl.pallas_call(
         predict_body,
-        out_shape=(shape(3, *BLOCK), shape(*BLOCK), shape(*BLOCK), shape(NY, 128)),
-        in_specs=[IN_SMEM] + [ANYWHERE] * 5 + [IN_VMEM] * 5,
+        out_shape=(shape(3, *BLOCK), shape(*BLOCK), shape(*MESSAGE), shape(NY, 128)),
+        in_specs=[IN_SMEM] + [ANYWHERE] * 5 + [IN_VMEM] * 3,
         out_specs=(IN_VMEM,) * 4,
         scratch_shapes=[padded] * 7
         + [
             pltpu.VMEM((NY, 128), F32),
+            pltpu.VMEM((2, NY, 128), F32),
             pltpu.VMEM((2, NY, NZ), F32),
-            pltpu.SemaphoreType.DMA((15,)),
+            pltpu.SemaphoreType.DMA((17,)),
         ],
-        compiler_params=PARAMS,
+        compiler_params=pltpu.CompilerParams(vmem_limit_bytes=18 * MIB),
         name="predict",
-    )(flags, velocity, fraction, guess, low, high, sides, sides_low, sides_high, profile, moments)
-
-
-def combine_call(packs, table):
+    )(flags, velocity, fraction, guess, paired, other, sides, profile, moments)
+
+
+def combine_call(packs, table, message):
     return pl.pallas_call(
         combine_body,
-        out_shape=shape(NY, 128),
-        in_specs=[IN_VMEM] * 5,
-        out_specs=IN_VMEM,
-        compiler_params=PARAMS,
+        out_shape=(shape(*MESSAGE), shape(NY, 128)),
+        in_specs=[IN_VMEM] * 5 + [ANYWHERE],
+        out_specs=(ANYWHERE, IN_VMEM),
+        scratch_shapes=[pltpu.SemaphoreType.DMA],
+        input_output_aliases={5: 0},
+        compiler_params=pltpu.CompilerParams(vmem_limit_bytes=4 * MIB),
         name="combine",
-    )(*packs, table)
-
-
-def solve_call(more, flags, mid, frac, now, source, low, high, far, far_low, far_high, table):
+    )(*packs, table, message)
+
+
+def merge_call(before, after, right, left):
+    return pl.pallas_call(
+        merge_body,
+        out_shape=(shape(*MESSAGE), shape(*MESSAGE), shape(NY, 128)),
+        in_specs=[IN_VMEM] * 2 + [ANYWHERE] * 2,
+        out_specs=(ANYWHERE, ANYWHERE, IN_VMEM),
+        scratch_shapes=[pltpu.SemaphoreType.DMA((2,))],
+        input_output_aliases={2: 0, 3: 1},
+        compiler_params=pltpu.CompilerParams(vmem_limit_bytes=4 * MIB),
+        name="merge",
+    )(before, after, right, left)
+
+
+def solve_call(more, flags, mid, frac, now, source, paired, other, far, table):
     outs = [shape(3, *BLOCK), shape(*BLOCK)]
     if more:
-        outs += [shape(*BLOCK), shape(*BLOCK), shape(NY, 128), shape(*BLOCK)]
+        outs += [shape(*MESSAGE), shape(*MESSAGE), shape(NY, 128), shape(*BLOCK)]
     planes = NX + 2 * POWERS
     return pl.pallas_call(
         functools.partial(solve_body, more),
         out_shape=tuple(outs),
-        in_specs=[IN_SMEM] + [IN_VMEM] * 10,
+        in_specs=[IN_SMEM] + [IN_VMEM] * 8,
         out_specs=(IN_VMEM,) * len(outs),
         scratch_shapes=[
             pltpu.VMEM((POWERS, planes, ROWS, NZ), F32),
-            pltpu.VMEM((POWERS, planes, ROWS, NZ), F32),
+            pltpu.VMEM((3, NY, 128), F32),
             pltpu.VMEM((NY, 512), BF16),
         ],
-        compiler_params=PARAMS,
+        compiler_params=pltpu.CompilerParams(vmem_limit_bytes=24 * MIB),
         name="solve",
-    )(flags, mid, frac, now, source, low, high, far, far_low, far_high, table)
+    )(flags, mid, frac, now, source, paired, other, far, table)
 
 
 def per_device(velocity, fraction, pressure_now, pressure_old, inflow):
     stream = lax.axis_index("stream")
     count = lax.axis_size("stream")
-    flags = jnp.stack([stream == 0, stream == count - 1]).astype(jnp.int32)
-    forward = [(i, i + 1) for i in range(count - 1)]
-    backward = [(i + 1, i) for i in range(count - 1)]
-
-    def along(block, step):
-        return lax.ppermute(block, "stream", forward if step > 0 else backward)
+    flags = jnp.stack([stream == 0, stream == count - 1, stream % 2 == 0]).astype(jnp.int32)
+    pairs = [(i, i ^ 1) for i in range(count)]
+    others = [(i, ((i + 1) ^ 1) - 1) for i in range(1, count - 1)]
+
+    def exchange(block, with_pair):
+        return lax.ppermute(block, "stream", pairs if with_pair else others)
 
     def around(block, offset):
         return lax.ppermute(
@@ -532,35 +591,28 @@
         )
 
     profile = jnp.broadcast_to(inflow[:, :, None], (2, NY, NZ))
-    odd = lanes(NY) % 2 == 1
     moments = jnp.asarray(moment_table())
     combine = jnp.asarray(combine_table())
     table = jnp.asarray(solve_table())
 
-    right, left, packed, guess = pack_call(velocity, fraction, pressure_now, pressure_old)
+    paired, other, packed, guess = pack_call(flags, velocity, fraction, pressure_now, pressure_old)
     now = pressure_now
     for step in range(STEPS):
         more = step < STEPS - 1
-        low = along(right, 1)
-        high = along(left, -1)
-        sides = jnp.where(odd, around(packed, -1), jnp.roll(around(packed, 1), -2, axis=1))
-        sides_low = along(sides, 1)
-        sides_high = along(sides, -1)
+        paired, other, sides = merge_call(around(packed, -1), around(packed, 1), paired, other)
+        other = exchange(other, False)
+        paired = exchange(paired, True)
         mid, fraction, source, pack = predict_call(
-            flags, velocity, fraction, guess, low, high, sides, sides_low, sides_high, profile, moments
+            flags, velocity, fraction, guess, paired, other, sides, profile, moments
         )
-        source_low = along(source, 1)
-        source_high = along(source, -1)
-        far = combine_call([pack] + [around(pack, o) for o in (1, 2, 3)], combine)
-        far_low = along(far, 1)
-        far_high = along(far, -1)
+        source, far = combine_call([pack] + [around(pack, o) for o in (1, 2, 3)], combine, source)
         results = solve_call(
-            more, flags, mid, fraction, now, source, source_low, source_high, far, far_low, far_high, table
+            more, flags, mid, fraction, now, source, exchange(source, True), exchange(source, False), far, table
         )
         velocity, pressure = results[:2]
         old, now = now, pressure
         if more:
-            right, left, packed, guess = results[2:]
+            paired, other, packed, guess = results[2:]
     return (velocity, fraction, now, old)
 
 

time: 246 us -> 171 us (0.70)
  starting transfers between devices: 85.1 us -> 42.2 us
  Pallas kernels: 85.5 us -> 50.4 us
  waiting for transfers between devices: 67.3 us -> 71.2 us
    ppermute x16 -> x8, starting transfers between devices: 75.2 us -> 32.4 us  [exchange(): return lax.ppermute(block, 'stream', pairs if with_pair else others)]
    ppermute x16 -> x8, waiting for transfers between devices: 34.7 us -> 58.1 us  [exchange(): return lax.ppermute(block, 'stream', pairs if with_pair else others)]
    pallas_call x2, Pallas kernels: 42.3 us -> 20.7 us  [predict_call(): pl.pallas_call(predict_body, out_shape=(shape(3, *BLOCK), shape(*BLOCK),...]
    ppermute x10, waiting for transfers between devices: 32.6 us -> 13.1 us  [around(): lax.ppermute(block, 'span', [((i + offset) % BLOCKS, i) for i in range(BL...]
    pallas_call x2, Pallas kernels: 35.4 us -> 26.8 us  [solve_call(): pl.pallas_call(functools.partial(solve_body, more), out_shape=tuple(outs)...]
    pallas_call x3 -> x5, Pallas kernels: 7.77 us -> 2.88 us  [the longest x1 1.41 us: pack_call(): pl.pallas_call(pack_body, out_shape=(shape(*MESSAGE), shape(*MESSAGE), sh...]
    unnamed x50 -> x26, local copies, waits for them, and re-layouts: 4.83 us -> 5.61 us
  transfers between devices with their start and end apart: 26 -> 18, of which waited for: 13 -> 13; matrix products, arithmetic and copies ran while one was open for 0% -> 0% of each run, Pallas kernels for 2% -> 0%
where the time goes in v2:
time: 171 us; the launch traced here: 170 us
  waiting for transfers between devices  71.2 us (42%)
  Pallas kernels  50.4 us (29%)
  starting transfers between devices  42.2 us (25%)
  local copies, waits for them, and re-layouts  5.7 us (3%)
    ppermute x8, waiting for transfers between devices, exchange(): return lax.ppermute(block, 'stream', pairs if with_pair else others)  58.1 us
    ppermute x8, starting transfers between devices, exchange(): return lax.ppermute(block, 'stream', pairs if with_pair else others)  32.4 us
    pallas_call x2, Pallas kernels, solve_call(): pl.pallas_call(functools.partial(solve_body, more), out_shape=tuple(outs)...  26.8 us
    pallas_call x2, Pallas kernels, predict_call(): pl.pallas_call(predict_body, out_shape=(shape(3, *BLOCK), shape(*BLOCK),...  20.7 us
    ppermute x10, waiting for transfers between devices, around(): lax.ppermute(block, 'span', [((i + offset) % BLOCKS, i) for i in range(BL...  13.1 us
    ppermute x10, starting transfers between devices, around(): lax.ppermute(block, 'span', [((i + offset) % BLOCKS, i) for i in range(BL...  9.79 us
    unnamed x26, local copies, waits for them, and re-layouts  5.61 us
  transfers between devices with their start and end apart: 18, of which 13 were waited for; matrix products, arithmetic and copies ran while one was open for 0% of the time, Pallas kernels for 0%

profile of v2, /device:TPU:7, one launch (start us, length us, event | category | flops | bytes accessed | tf_op | source)
XLA Modules:
  0.0 170.4 jit_solution(10005658804207349162)
XLA Ops:
  0.7 1.4 copy-done
  5.3 1.4 pack.1
  8.5 2.7 %collective-permute-done.1.after = f32[128,128]{1,0:T(8,128)S(1)} collective-permute-done((f32[128,128]{1,0:T(8,128)S(1)}, f32[128,128]{1,0:T(8,128)S(1)}, u32[]{:S(2)}, u32[]{:S(2)}) %collective-permute-start.1) | collective-permute-done | bytes 65568 | tf_op jit(solution)/shard_map/ppermute | solution.py:589
  11.5 1.7 %collective-permute-start.2 = (f32[9,128,128]{2,1,0:T(8,128)S(1)}, f32[9,128,128]{2,1,0:T(8,128)S(1)}, u32[]{:S(2)}, u32[]{:S(2)}) collective-permute-start(f32[9,128,128]{2,1,0:T(8,128)S(1)} %get-tuple-element.38), channel_id=1, source_target_pairs={{0,4},{4,0},{8,12},{12,8},{16,20},{20,16},{24,28},{28,24},{32,36},... | collective-permute-start | bytes 1769480 | tf_op jit(solution)/shard_map/ppermute | solution.py:586
  13.2 7.6 %collective-permute-start.3 = (f32[9,128,128]{2,1,0:T(8,128)S(1)}, f32[9,128,128]{2,1,0:T(8,128)S(1)}, u32[]{:S(2)}, u32[]{:S(2)}) collective-permute-start(f32[9,128,128]{2,1,0:T(8,128)S(1)} %get-tuple-element.39), channel_id=1, source_target_pairs={{4,8},{8,4},{12,16},{16,12},{20,24},{24,20},{28,32},{32,28},{36,40... | collective-permute-start | bytes 1769480 | tf_op jit(solution)/shard_map/ppermute | solution.py:586
  20.8 5.3 %collective-permute-done.2.paired = f32[9,128,128]{2,1,0:T(8,128)S(1)} collective-permute-done((f32[9,128,128]{2,1,0:T(8,128)S(1)}, f32[9,128,128]{2,1,0:T(8,128)S(1)}, u32[]{:S(2)}, u32[]{:S(2)}) %collective-permute-start.2) | collective-permute-done | bytes 589856 | tf_op jit(solution)/shard_map/ppermute | solution.py:586
  26.1 8.5 %collective-permute-done.3.other = f32[9,128,128]{2,1,0:T(8,128)S(1)} collective-permute-done((f32[9,128,128]{2,1,0:T(8,128)S(1)}, f32[9,128,128]{2,1,0:T(8,128)S(1)}, u32[]{:S(2)}, u32[]{:S(2)}) %collective-permute-start.3) | collective-permute-done | bytes 589856 | tf_op jit(solution)/shard_map/ppermute | solution.py:586
  34.8 10.2 %predict.2 = (f32[3,8,128,128]{3,2,1,0:T(8,128)S(1)}, f32[8,128,128]{2,1,0:T(8,128)S(1)}, f32[9,128,128]{2,1,0:T(8,128)S(1)}, f32[128,128]{1,0:T(8,128)S(1)}) custom-call(s32[3]{0:T(128)S(1)} %add_convert_fusion.flags.refs_0_, f32[3,8,128,128]{3,2,1,0:T(8,128)S(1)} %copy-done.1, f32[8,128,128]{2,1,0:T(8,128)S(1)} %copy-done.4, ...), custom_call_target="tpu_custom_call" | custom-call | tf_op jit(solution)/shard_map/predict/pallas_call | solution.py:515
  45.1 2.0 %collective-permute-start.6 = (f32[128,128]{1,0:T(8,128)S(1)}, f32[128,128]{1,0:T(8,128)S(1)}, u32[]{:S(2)}, u32[]{:S(2)}) collective-permute-start(f32[128,128]{1,0:T(8,128)S(1)} %get-tuple-element.43.a), channel_id=1, source_target_pairs={{3,0},{0,1},{1,2},{2,3},{7,4},{4,5},{5,6},{6,7},{11,8},{8,9},{9,10... | collective-permute-start | bytes 196616 | tf_op jit(solution)/shard_map/ppermute | solution.py:589
  47.1 1.2 collective-permute-start.5
  48.5 3.2 %collective-permute-done.5.c = f32[128,128]{1,0:T(8,128)S(1)} collective-permute-done((f32[128,128]{1,0:T(8,128)S(1)}, f32[128,128]{1,0:T(8,128)S(1)}, u32[]{:S(2)}, u32[]{:S(2)}) %collective-permute-start.5) | collective-permute-done | bytes 65568 | tf_op jit(solution)/shard_map/ppermute | solution.py:589
  52.6 7.6 %collective-permute-start.8 = (f32[9,128,128]{2,1,0:T(8,128)S(1)}, f32[9,128,128]{2,1,0:T(8,128)S(1)}, u32[]{:S(2)}, u32[]{:S(2)}) collective-permute-start(f32[9,128,128]{2,1,0:T(8,128)S(1)} %get-tuple-element.45.refs_4_), channel_id=1, source_target_pairs={{4,8},{8,4},{12,16},{16,12},{20,24},{24,20},{28,32},{32,28},{36,40... | collective-permute-start | bytes 1769480 | tf_op jit(solution)/shard_map/ppermute | solution.py:586
  60.3 15.0 %collective-permute-done.8.refs_6_ = f32[9,128,128]{2,1,0:T(8,128)S(1)} collective-permute-done((f32[9,128,128]{2,1,0:T(8,128)S(1)}, f32[9,128,128]{2,1,0:T(8,128)S(1)}, u32[]{:S(2)}, u32[]{:S(2)}) %collective-permute-start.8) | collective-permute-done | bytes 589856 | tf_op jit(solution)/shard_map/ppermute | solution.py:586
  75.3 13.6 %solve.2 = (f32[3,8,128,128]{3,2,1,0:T(8,128)S(1)}, f32[8,128,128]{2,1,0:T(8,128)}, f32[9,128,128]{2,1,0:T(8,128)S(1)}, f32[9,128,128]{2,1,0:T(8,128)S(1)}, f32[...) custom-call(s32[3]{0:T(128)S(1)} %add_convert_fusion.flags.refs_0_, f32[3,8,128,128]{3,2,1,0:T(8,128)S(1)} %get-tuple-element.41.refs_1_, ...), custom_call_target="tpu_custom_call" | custom-call | tf_op jit(solution)/shard_map/solve/pallas_call | solution.py:563
  90.7 2.9 %collective-permute-done.10.after = f32[128,128]{1,0:T(8,128)S(1)} collective-permute-done((f32[128,128]{1,0:T(8,128)S(1)}, f32[128,128]{1,0:T(8,128)S(1)}, u32[]{:S(2)}, u32[]{:S(2)}) %collective-permute-start.10) | collective-permute-done | bytes 65568 | tf_op jit(solution)/shard_map/ppermute | solution.py:589
  94.0 7.5 %collective-permute-start.12 = (f32[9,128,128]{2,1,0:T(8,128)S(1)}, f32[9,128,128]{2,1,0:T(8,128)S(1)}, u32[]{:S(2)}, u32[]{:S(2)}) collective-permute-start(f32[9,128,128]{2,1,0:T(8,128)S(1)} %get-tuple-element.53), channel_id=1, source_target_pairs={{4,8},{8,4},{12,16},{16,12},{20,24},{24,20},{28,32},{32,28},{36,40... | collective-permute-start | bytes 1769480 | tf_op jit(solution)/shard_map/ppermute | solution.py:586
  101.6 6.8 %collective-permute-done.11.paired = f32[9,128,128]{2,1,0:T(8,128)S(1)} collective-permute-done((f32[9,128,128]{2,1,0:T(8,128)S(1)}, f32[9,128,128]{2,1,0:T(8,128)S(1)}, u32[]{:S(2)}, u32[]{:S(2)}) %collective-permute-start.11) | collective-permute-done | bytes 589856 | tf_op jit(solution)/shard_map/ppermute | solution.py:586
  108.4 7.5 %collective-permute-done.12.other = f32[9,128,128]{2,1,0:T(8,128)S(1)} collective-permute-done((f32[9,128,128]{2,1,0:T(8,128)S(1)}, f32[9,128,128]{2,1,0:T(8,128)S(1)}, u32[]{:S(2)}, u32[]{:S(2)}) %collective-permute-start.12) | collective-permute-done | bytes 589856 | tf_op jit(solution)/shard_map/ppermute | solution.py:586
  115.8 10.4 %predict.3 = (f32[3,8,128,128]{3,2,1,0:T(8,128)S(1)}, f32[8,128,128]{2,1,0:T(8,128)}, f32[9,128,128]{2,1,0:T(8,128)S(1)}, f32[128,128]{1,0:T(8,128)S(1)}) custom-call(s32[3]{0:T(128)S(1)} %add_convert_fusion.flags.refs_0_, f32[3,8,128,128]{3,2,1,0:T(8,128)S(1)} %get-tuple-element.47.vel, f32[8,128,128]{2,1,0:T(8,128)S(1)} %get-tuple-element.42.refs_2_.frac, ...), custom_call_target="tpu_custom_call" | custom-call | tf_op jit(solution)/shard_map/predict/pallas_call | solution.py:515
  127.1 2.1 %collective-permute-start.14 = (f32[128,128]{1,0:T(8,128)S(1)}, f32[128,128]{1,0:T(8,128)S(1)}, u32[]{:S(2)}, u32[]{:S(2)}) collective-permute-start(f32[128,128]{1,0:T(8,128)S(1)} %get-tuple-element.58.a), channel_id=1, source_target_pairs={{2,0},{3,1},{0,2},{1,3},{6,4},{7,5},{4,6},{5,7},{10,8},{11,9},{8,1... | collective-permute-start | bytes 196616 | tf_op jit(solution)/shard_map/ppermute | solution.py:589
  129.2 3.3 %collective-permute-done.14.c = f32[128,128]{1,0:T(8,128)S(1)} collective-permute-done((f32[128,128]{1,0:T(8,128)S(1)}, f32[128,128]{1,0:T(8,128)S(1)}, u32[]{:S(2)}, u32[]{:S(2)}) %collective-permute-start.14) | collective-permute-done | bytes 65568 | tf_op jit(solution)/shard_map/ppermute | solution.py:589
  133.5 7.6 %collective-permute-start.17 = (f32[9,128,128]{2,1,0:T(8,128)S(1)}, f32[9,128,128]{2,1,0:T(8,128)S(1)}, u32[]{:S(2)}, u32[]{:S(2)}) collective-permute-start(f32[9,128,128]{2,1,0:T(8,128)S(1)} %get-tuple-element.60.refs_4_), channel_id=1, source_target_pairs={{4,8},{8,4},{12,16},{16,12},{20,24},{24,20},{28,32},{32,28},{36,40... | collective-permute-start | bytes 1769480 | tf_op jit(solution)/shard_map/ppermute | solution.py:586
  141.1 15.0 %collective-permute-done.17.refs_6_ = f32[9,128,128]{2,1,0:T(8,128)S(1)} collective-permute-done((f32[9,128,128]{2,1,0:T(8,128)S(1)}, f32[9,128,128]{2,1,0:T(8,128)S(1)}, u32[]{:S(2)}, u32[]{:S(2)}) %collective-permute-start.17) | collective-permute-done | bytes 589856 | tf_op jit(solution)/shard_map/ppermute | solution.py:586
  157.2 13.2 %solve.3 = (f32[3,8,128,128]{3,2,1,0:T(8,128)}, f32[8,128,128]{2,1,0:T(8,128)}) custom-call(s32[3]{0:T(128)S(1)} %add_convert_fusion.flags.refs_0_, f32[3,8,128,128]{3,2,1,0:T(8,128)S(1)} %get-tuple-element.55.refs_1_, f32[8,128,128]{2,1,0:T(8,128)S(1)} %copy-done.11, f32[8,128,128]{2,1,0:T(8,128)S(1)} %copy-done.10, ...), custom_call_target="tpu_custom_call" | custom-call | tf_op jit(solution)/shard_map/solve/pallas_call | solution.py:563
  (49 shorter events, 11.7 us)
Async XLA Ops:
  5.3 29.5 %copy-start.1 = (f32[3,8,128,128]{3,2,1,0:T(8,128)S(1)}, f32[3,8,128,128]{3,2,1,0:T(8,128)}, u32[]{:S(2)}) copy-start(f32[3,8,128,128]{3,2,1,0:T(8,128)} %vel.3) | copy-start | bytes 4718596
  5.3 29.5 %copy-start.4 = (f32[8,128,128]{2,1,0:T(8,128)S(1)}, f32[8,128,128]{2,1,0:T(8,128)}, u32[]{:S(2)}) copy-start(f32[8,128,128]{2,1,0:T(8,128)} %frac.3) | copy-start | bytes 1572868
  5.3 29.5 %copy-start.8 = (f32[2,128,128]{2,1,0:T(8,128)S(1)}, f32[2,128,128]{2,1,0:T(8,128)}, u32[]{:S(2)}) copy-start(f32[2,128,128]{2,1,0:T(8,128)} %constant.28.clone.moments) | copy-start | bytes 393220
  6.7 4.5 %collective-permute-start.1 = (f32[128,128]{1,0:T(8,128)S(1)}, f32[128,128]{1,0:T(8,128)S(1)}, u32[]{:S(2)}, u32[]{:S(2)}) collective-permute-start(f32[128,128]{1,0:T(8,128)S(1)} %get-tuple-element.35), channel_id=1, source_target_pairs={{1,0},{2,1},{3,2},{0,3},{5,4},{6,5},{7,6},{4,7},{9,8},{10,9},{11,1... | collective-permute-start | bytes 196616 | tf_op jit(solution)/shard_map/ppermute | solution.py:589
  7.4 3.8 %collective-permute-start = (f32[128,128]{1,0:T(8,128)S(1)}, f32[128,128]{1,0:T(8,128)S(1)}, u32[]{:S(2)}, u32[]{:S(2)}) collective-permute-start(f32[128,128]{1,0:T(8,128)S(1)} %get-tuple-element.35), channel_id=1, source_target_pairs={{3,0},{0,1},{1,2},{2,3},{7,4},{4,5},{5,6},{6,7},{11,8},{8,9},{9,10... | collective-permute-start | bytes 196616 | tf_op jit(solution)/shard_map/ppermute | solution.py:589
  11.5 14.7 %collective-permute-start.2 = (f32[9,128,128]{2,1,0:T(8,128)S(1)}, f32[9,128,128]{2,1,0:T(8,128)S(1)}, u32[]{:S(2)}, u32[]{:S(2)}) collective-permute-start(f32[9,128,128]{2,1,0:T(8,128)S(1)} %get-tuple-element.38), channel_id=1, source_target_pairs={{0,4},{4,0},{8,12},{12,8},{16,20},{20,16},{24,28},{28,24},{32,36},... | collective-permute-start | bytes 1769480 | tf_op jit(solution)/shard_map/ppermute | solution.py:586
  13.2 21.5 %collective-permute-start.3 = (f32[9,128,128]{2,1,0:T(8,128)S(1)}, f32[9,128,128]{2,1,0:T(8,128)S(1)}, u32[]{:S(2)}, u32[]{:S(2)}) collective-permute-start(f32[9,128,128]{2,1,0:T(8,128)S(1)} %get-tuple-element.39), channel_id=1, source_target_pairs={{4,8},{8,4},{12,16},{16,12},{20,24},{24,20},{28,32},{32,28},{36,40... | collective-permute-start | bytes 1769480 | tf_op jit(solution)/shard_map/ppermute | solution.py:586
  34.8 40.5 %copy-start.6 = (f32[8,128,128]{2,1,0:T(8,128)S(1)}, f32[8,128,128]{2,1,0:T(8,128)}, u32[]{:S(2)}) copy-start(f32[8,128,128]{2,1,0:T(8,128)} %refs_3_.1) | copy-start | bytes 1572868
  45.1 30.2 %copy-start.2 = (bf16[512,1024]{1,0:T(8,128)(2,1)S(1)}, bf16[512,1024]{1,0:T(8,128)(2,1)}, u32[]{:S(2)}) copy-start(bf16[512,1024]{1,0:T(8,128)(2,1)} %constant.30.clone.refs_8_) | copy-start | bytes 3145732
  45.1 3.4 %collective-permute-start.6 = (f32[128,128]{1,0:T(8,128)S(1)}, f32[128,128]{1,0:T(8,128)S(1)}, u32[]{:S(2)}, u32[]{:S(2)}) collective-permute-start(f32[128,128]{1,0:T(8,128)S(1)} %get-tuple-element.43.a), channel_id=1, source_target_pairs={{3,0},{0,1},{1,2},{2,3},{7,4},{4,5},{5,6},{6,7},{11,8},{8,9},{9,10... | collective-permute-start | bytes 196616 | tf_op jit(solution)/shard_map/ppermute | solution.py:589
  47.1 4.5 %collective-permute-start.5 = (f32[128,128]{1,0:T(8,128)S(1)}, f32[128,128]{1,0:T(8,128)S(1)}, u32[]{:S(2)}, u32[]{:S(2)}) collective-permute-start(f32[128,128]{1,0:T(8,128)S(1)} %get-tuple-element.43.a), channel_id=1, source_target_pairs={{2,0},{3,1},{0,2},{1,3},{6,4},{7,5},{4,6},{5,7},{10,8},{11,9},{8,1... | collective-permute-start | bytes 196616 | tf_op jit(solution)/shard_map/ppermute | solution.py:589
  48.4 3.8 %collective-permute-start.4 = (f32[128,128]{1,0:T(8,128)S(1)}, f32[128,128]{1,0:T(8,128)S(1)}, u32[]{:S(2)}, u32[]{:S(2)}) collective-permute-start(f32[128,128]{1,0:T(8,128)S(1)} %get-tuple-element.43.a), channel_id=1, source_target_pairs={{1,0},{2,1},{3,2},{0,3},{5,4},{6,5},{7,6},{4,7},{9,8},{10,9},{11,1... | collective-permute-start | bytes 196616 | tf_op jit(solution)/shard_map/ppermute | solution.py:589
  52.6 22.7 %collective-permute-start.8 = (f32[9,128,128]{2,1,0:T(8,128)S(1)}, f32[9,128,128]{2,1,0:T(8,128)S(1)}, u32[]{:S(2)}, u32[]{:S(2)}) collective-permute-start(f32[9,128,128]{2,1,0:T(8,128)S(1)} %get-tuple-element.45.refs_4_), channel_id=1, source_target_pairs={{4,8},{8,4},{12,16},{16,12},{20,24},{24,20},{28,32},{32,28},{36,40... | collective-permute-start | bytes 1769480 | tf_op jit(solution)/shard_map/ppermute | solution.py:586
  60.2 15.1 %collective-permute-start.7 = (f32[9,128,128]{2,1,0:T(8,128)S(1)}, f32[9,128,128]{2,1,0:T(8,128)S(1)}, u32[]{:S(2)}, u32[]{:S(2)}) collective-permute-start(f32[9,128,128]{2,1,0:T(8,128)S(1)} %get-tuple-element.45.refs_4_), channel_id=1, source_target_pairs={{0,4},{4,0},{8,12},{12,8},{16,20},{20,16},{24,28},{28,24},{32,36},... | collective-permute-start | bytes 1769480 | tf_op jit(solution)/shard_map/ppermute | solution.py:586
  88.9 4.6 %collective-permute-start.10 = (f32[128,128]{1,0:T(8,128)S(1)}, f32[128,128]{1,0:T(8,128)S(1)}, u32[]{:S(2)}, u32[]{:S(2)}) collective-permute-start(f32[128,128]{1,0:T(8,128)S(1)} %get-tuple-element.49), channel_id=1, source_target_pairs={{1,0},{2,1},{3,2},{0,3},{5,4},{6,5},{7,6},{4,7},{9,8},{10,9},{11,1... | collective-permute-start | bytes 196616 | tf_op jit(solution)/shard_map/ppermute | solution.py:589
  89.7 3.9 %collective-permute-start.9 = (f32[128,128]{1,0:T(8,128)S(1)}, f32[128,128]{1,0:T(8,128)S(1)}, u32[]{:S(2)}, u32[]{:S(2)}) collective-permute-start(f32[128,128]{1,0:T(8,128)S(1)} %get-tuple-element.49), channel_id=1, source_target_pairs={{3,0},{0,1},{1,2},{2,3},{7,4},{4,5},{5,6},{6,7},{11,8},{8,9},{9,10... | collective-permute-start | bytes 196616 | tf_op jit(solution)/shard_map/ppermute | solution.py:589
  93.8 14.5 %collective-permute-start.11 = (f32[9,128,128]{2,1,0:T(8,128)S(1)}, f32[9,128,128]{2,1,0:T(8,128)S(1)}, u32[]{:S(2)}, u32[]{:S(2)}) collective-permute-start(f32[9,128,128]{2,1,0:T(8,128)S(1)} %get-tuple-element.52), channel_id=1, source_target_pairs={{0,4},{4,0},{8,12},{12,8},{16,20},{20,16},{24,28},{28,24},{32,36},... | collective-permute-start | bytes 1769480 | tf_op jit(solution)/shard_map/ppermute | solution.py:586
  94.0 21.8 %collective-permute-start.12 = (f32[9,128,128]{2,1,0:T(8,128)S(1)}, f32[9,128,128]{2,1,0:T(8,128)S(1)}, u32[]{:S(2)}, u32[]{:S(2)}) collective-permute-start(f32[9,128,128]{2,1,0:T(8,128)S(1)} %get-tuple-element.53), channel_id=1, source_target_pairs={{4,8},{8,4},{12,16},{16,12},{20,24},{24,20},{28,32},{32,28},{36,40... | collective-permute-start | bytes 1769480 | tf_op jit(solution)/shard_map/ppermute | solution.py:586
  115.8 40.3 %copy-start.10 = (f32[8,128,128]{2,1,0:T(8,128)S(1)}, f32[8,128,128]{2,1,0:T(8,128)}, u32[]{:S(2)}) copy-start(f32[8,128,128]{2,1,0:T(8,128)} %get-tuple-element.33.refs_3_) | copy-start | bytes 1572868
  126.3 3.0 %collective-permute-start.15 = (f32[128,128]{1,0:T(8,128)S(1)}, f32[128,128]{1,0:T(8,128)S(1)}, u32[]{:S(2)}, u32[]{:S(2)}) collective-permute-start(f32[128,128]{1,0:T(8,128)S(1)} %get-tuple-element.58.a), channel_id=1, source_target_pairs={{3,0},{0,1},{1,2},{2,3},{7,4},{4,5},{5,6},{6,7},{11,8},{8,9},{9,10... | collective-permute-start | bytes 196616 | tf_op jit(solution)/shard_map/ppermute | solution.py:589
  127.1 5.4 %collective-permute-start.14 = (f32[128,128]{1,0:T(8,128)S(1)}, f32[128,128]{1,0:T(8,128)S(1)}, u32[]{:S(2)}, u32[]{:S(2)}) collective-permute-start(f32[128,128]{1,0:T(8,128)S(1)} %get-tuple-element.58.a), channel_id=1, source_target_pairs={{2,0},{3,1},{0,2},{1,3},{6,4},{7,5},{4,6},{5,7},{10,8},{11,9},{8,1... | collective-permute-start | bytes 196616 | tf_op jit(solution)/shard_map/ppermute | solution.py:589
  129.2 3.8 %collective-permute-start.13 = (f32[128,128]{1,0:T(8,128)S(1)}, f32[128,128]{1,0:T(8,128)S(1)}, u32[]{:S(2)}, u32[]{:S(2)}) collective-permute-start(f32[128,128]{1,0:T(8,128)S(1)} %get-tuple-element.58.a), channel_id=1, source_target_pairs={{1,0},{2,1},{3,2},{0,3},{5,4},{6,5},{7,6},{4,7},{9,8},{10,9},{11,1... | collective-permute-start | bytes 196616 | tf_op jit(solution)/shard_map/ppermute | solution.py:589
  133.5 22.7 %collective-permute-start.17 = (f32[9,128,128]{2,1,0:T(8,128)S(1)}, f32[9,128,128]{2,1,0:T(8,128)S(1)}, u32[]{:S(2)}, u32[]{:S(2)}) collective-permute-start(f32[9,128,128]{2,1,0:T(8,128)S(1)} %get-tuple-element.60.refs_4_), channel_id=1, source_target_pairs={{4,8},{8,4},{12,16},{16,12},{20,24},{24,20},{28,32},{32,28},{36,40... | collective-permute-start | bytes 1769480 | tf_op jit(solution)/shard_map/ppermute | solution.py:586
  141.0 15.1 %collective-permute-start.16 = (f32[9,128,128]{2,1,0:T(8,128)S(1)}, f32[9,128,128]{2,1,0:T(8,128)S(1)}, u32[]{:S(2)}, u32[]{:S(2)}) collective-permute-start(f32[9,128,128]{2,1,0:T(8,128)S(1)} %get-tuple-element.60.refs_4_), channel_id=1, source_target_pairs={{0,4},{4,0},{8,12},{12,8},{16,20},{20,16},{24,28},{28,24},{32,36},... | collective-permute-start | bytes 1769480 | tf_op jit(solution)/shard_map/ppermute | solution.py:586
  (7 other events, 52.3 us)

commit v3 on v2

--- a/solution.py
+++ b/solution.py
@@ -149,34 +149,181 @@
     packed[...] = pack_columns(field)
 
 
-def predict_body(
-    flags, vel, frac, guess, paired, other, sides, profile, moments,
-    mid, frac_new, source, pack,
-    U, V, W, F, G, FM, FP, Z, Z_ends, end_mid, sem,
-):
+def fill_shifts(buffers, ends, planes, slots):
+    U, V, W, F, G, FM, FP = buffers
     own = pl.ds(TOP, NY)
-    copies = []
-
-    def fetch(src, dst):
-        copy = pltpu.make_async_copy(src, dst, sem.at[len(copies)])
+    below, above = pl.ds(TOP - 1, 1), pl.ds(TOP + NY, 1)
+    bottom, top = pl.ds(TOP, 1), pl.ds(TOP + NY - 1, 1)
+    lane = lanes(NY)
+    for e, slot in zip(planes, slots):
+        centre = F[e, own]
+        turned = pltpu.roll(ends, 128 - 2 * (36 + slot) - 1, 1)
+        FM[e, own] = jnp.where(lane == 0, turned, pltpu.roll(centre, 1, 1))
+        FP[e, own] = jnp.where(lane == 127, turned, pltpu.roll(centre, 127, 1))
+        for buf in (F, FM, FP, G):
+            buf[e, below] = buf[e, bottom]
+            buf[e, above] = buf[e, top]
+        for buf, wall in ((U, 2.0), (V, 0.0), (W, 0.0)):
+            buf[e, below] = wall - buf[e, bottom]
+            buf[e, above] = -buf[e, top]
+
+
+def cells(low, at, high, Z, e, y, components):
+    U, V, W, F, G, FM, FP = range(7)
+
+    def get(plane, k, rows):
+        return plane[0][k][plane[1], rows]
+
+    lane = lanes(8)
+    at_low = lane == 0
+    at_high = lane == 127
+    here, up, down = pl.ds(y + TOP, 8), pl.ds(y + TOP + 1, 8), pl.ds(y + TOP - 1, 8)
+    ends_all = Z[pl.ds(y, 8), :]
+
+    def star(k, group):
+        centre = get(at, k, here)
+        ends = pltpu.roll(ends_all, 128 - 2 * (12 * group + e) - 1, 1)
+        behind = jnp.where(at_low, ends, pltpu.roll(centre, 1, 1))
+        ahead = jnp.where(at_high, ends, pltpu.roll(centre, 127, 1))
+        return centre, (
+            (get(high, k, here), get(low, k, here)),
+            (get(at, k, up), get(at, k, down)),
+            (ahead, behind),
+        )
+
+    c = get(at, F, here)
+    around = ((get(high, F, here), get(low, F, here)), (get(at, F, up), get(at, F, down)), (get(at, FP, here), get(at, FM, here)))
+    d = [p - m for p, m in around]
+    second = [p + m - 2.0 * c for p, m in around]
+    mxy = (get(high, F, up) - get(high, F, down)) - (get(low, F, up) - get(low, F, down))
+    mxz = (get(high, FP, here) - get(high, FM, here)) - (get(low, FP, here) - get(low, FM, here))
+    myz = (get(at, FP, up) - get(at, FM, up)) - (get(at, FP, down) - get(at, FM, down))
+    dd = [v * v for v in d]
+    inverse = lax.rsqrt(jnp.maximum(dd[0] + dd[1] + dd[2], 1.0))
+    bend = (dd[0] * second[0] + dd[1] * second[1] + dd[2] * second[2]) + 0.5 * (
+        d[0] * (d[1] * mxy + d[2] * mxz) + d[1] * d[2] * myz
+    )
+    laplace = second[0] + second[1] + second[2]
+    volume = 1.0 / (0.5 + 0.5 * c)
+    pull = (bend * (inverse * inverse) - laplace) * (0.5 * inverse) * volume
+    nu = (0.02 + 0.03 * c) * volume
+    if len(components) == 3:
+        stars = [star(k, k) for k in (U, V, W)]
+        centres = [s[0] for s in stars]
+    else:
+        stars = [star(U, 0)]
+        centres = [stars[0][0], get(at, V, here), get(at, W, here)]
+    speeds = [jnp.abs(v) for v in centres]
+    if len(components) == 3:
+        guesses = star(G, 4)[1]
+    else:
+        guesses = ((get(high, G, here), get(low, G, here)),)
+    lift = 2.0 - volume
+    out = []
+    for k in components:
+        centre, sides_ = stars[k]
+        twice = 2.0 * centre
+        transport = 0.0
+        diffusion = 0.0
+        for a in range(3):
+            p, m = sides_[a]
+            curve = p + m - twice
+            transport = transport + (centres[a] * (p - m) - speeds[a] * curve)
+            diffusion = diffusion + curve
+        change = nu * diffusion + pull * d[k] - 0.5 * transport
+        p, m = guesses[k]
+        out.append(centre + 0.1 * (change + 0.5 * (lift * (p - m))))
+    if len(components) == 1:
+        return out
+    net = 0.0
+    for a in range(3):
+        p, m = stars[a][1][a]
+        fp, fm = around[a]
+        ahead = centres[a] + p
+        behind = centres[a] + m
+        net = net + (
+            (jnp.maximum(ahead, 0.0) - jnp.minimum(behind, 0.0)) * c
+            + (jnp.minimum(ahead, 0.0) * fp - jnp.maximum(behind, 0.0) * fm)
+        )
+    return out + [c - 0.05 * net]
+
+
+def source_plane(x, before, after, mid, mx, moments, source, pack):
+    lane = lanes(NY)
+    row = lax.broadcasted_iota(jnp.int32, (NY, 128), 0)
+    v = mid[1, mx]
+    w = mid[2, mx]
+    v_up = jnp.where(row == NY - 1, 0.0, pltpu.roll(v, NY - 1, 0))
+    v_down = jnp.where(row == 0, 0.0, pltpu.roll(v, 1, 0))
+    w_up = jnp.where(lane == NZ - 1, 0.0, pltpu.roll(w, NZ - 1, 1))
+    w_down = jnp.where(lane == 0, 0.0, pltpu.roll(w, 1, 1))
+    s = 2.5 * ((after - before) + (v_up - v_down) + (w_up - w_down))
+    source[x] = s
+    part = jnp.dot(s, moments[0], precision=HIGHEST, preferred_element_type=F32) + jnp.dot(
+        w, moments[1], precision=HIGHEST, preferred_element_type=F32
+    )
+    pack[...] += pltpu.roll(part, 16 * x, 1) if x else part
+
+
+def start_copies(pairs, sem):
+    copies = [pltpu.make_async_copy(src, dst, sem.at[k]) for k, (src, dst) in enumerate(pairs)]
+    for copy in copies:
         copy.start()
-        copies.append(copy)
-
-    for k, buf in enumerate((U, V, W)):
-        fetch(vel.at[k], buf.at[pl.ds(2, NX), own])
-    fetch(frac, F.at[pl.ds(2, NX), own])
-    fetch(guess, G.at[pl.ds(2, NX), own])
+    return copies
+
+
+def inner_body(vel, frac, guess, sides, moments, *refs):
+    buffers = refs[:7]
+    mid, frac_new, source, pack, sem = refs[7:]
+    U, V, W, F, G = buffers[:5]
+    own = pl.ds(TOP, NY)
+    sources = [vel.at[0], vel.at[1], vel.at[2], frac, guess]
+    copies = start_copies([(src, buf.at[pl.ds(0, NX), own]) for src, buf in zip(sources, (U, V, W, F, G))], sem)
+    pack[...] = jnp.zeros((NY, 128), F32)
+    for copy in copies:
+        copy.wait()
+    fill_shifts(buffers, sides[...], range(NX), range(2, 2 + NX))
+
+    def block(i, carry):
+        x = 1 + i // 16
+        y = pl.multiple_of((i % 16) * 8, 8)
+        rows = pl.ds(y, 8)
+        mid[0, x, rows], mid[1, x, rows], mid[2, x, rows], frac_new[x, rows] = cells(
+            (buffers, x - 1), (buffers, x), (buffers, x + 1), sides, x + 2, y, (0, 1, 2)
+        )
+        return carry
+
+    lax.fori_loop(0, 16 * (NX - 2), block, 0, unroll=4)
+    for x in range(2, NX - 2):
+        source_plane(x, mid[0, x - 1], mid[0, x + 1], mid, x, moments, source, pack)
+
+
+def outer_body(flags, paired, other, sides, profile, moments, *refs):
+    given, (given_mid, given_frac, given_source, given_pack) = refs[:7], refs[7:11]
+    mid, frac_new, source, pack = refs[11:15]
+    buffers = refs[15:22]
+    Z, Z_ends, end_mid, sem, keep_sem = refs[22:]
+    U, V, W, F, G = buffers[:5]
+    own = pl.ds(TOP, NY)
+    middle = pl.ds(1, NX - 2)
+    kept = [(given_mid.at[k, middle], mid.at[k, middle]) for k in range(3)]
+    kept += [(given_frac.at[middle], frac_new.at[middle])]
+    kept += [(given_source.at[pl.ds(2, NX - 4)], source.at[pl.ds(2, NX - 4)])]
+    kept = start_copies(kept, keep_sem)
     even = flags[2] == 1
+    pairs = []
     for msg, upper in ((paired, even), (other, jnp.logical_not(even))):
-        far = jnp.where(upper, 10, 0)
-        near = jnp.where(upper, 10, 1)
-        fetch(msg.at[pl.ds(0, 2)], U.at[pl.ds(far, 2), own])
-        fetch(msg.at[2], V.at[near, own])
-        fetch(msg.at[3], W.at[near, own])
-        fetch(msg.at[pl.ds(4, 2)], F.at[pl.ds(far, 2), own])
-        fetch(msg.at[pl.ds(6, 2)], G.at[pl.ds(far, 2), own])
-        fetch(msg.at[8], Z_ends.at[jnp.where(upper, 1, 0)])
-    for copy in copies:
+        far = jnp.where(upper, 2, 0)
+        near = jnp.where(upper, 2, 1)
+        pairs += [
+            (msg.at[pl.ds(0, 2)], U.at[pl.ds(far, 2), own]),
+            (msg.at[2], V.at[near, own]),
+            (msg.at[3], W.at[near, own]),
+            (msg.at[pl.ds(4, 2)], F.at[pl.ds(far, 2), own]),
+            (msg.at[pl.ds(6, 2)], G.at[pl.ds(far, 2), own]),
+            (msg.at[8], Z_ends.at[jnp.where(upper, 1, 0)]),
+        ]
+    for copy in start_copies(pairs, sem):
         copy.wait()
 
     first = flags[0] == 1
@@ -202,144 +349,35 @@
 
     @pl.when(last)
     def _():
-        for e in (10, 11):
-            U[e, own] = U[9, own]
-            F[e, own] = F[9, own]
-        V[10, own] = V[9, own]
-        W[10, own] = W[9, own]
-
-    def shift_fraction(e, carry):
-        lane = lanes(NY)
-        centre = F[e, own]
-        ends = pltpu.roll(Z[...], 128 - 2 * (36 + e) - 1, 1)
-        FM[e, own] = jnp.where(lane == 0, ends, pltpu.roll(centre, 1, 1))
-        FP[e, own] = jnp.where(lane == 127, ends, pltpu.roll(centre, 127, 1))
-        for buf in (F, FM, FP):
-            buf[e, pl.ds(TOP - 1, 1)] = buf[e, pl.ds(TOP, 1)]
-            buf[e, pl.ds(TOP + NY, 1)] = buf[e, pl.ds(TOP + NY - 1, 1)]
-        G[e, pl.ds(TOP - 1, 1)] = G[e, pl.ds(TOP, 1)]
-        G[e, pl.ds(TOP + NY, 1)] = G[e, pl.ds(TOP + NY - 1, 1)]
-        for buf, wall in ((U, 2.0), (V, 0.0), (W, 0.0)):
-            buf[e, pl.ds(TOP - 1, 1)] = wall - buf[e, pl.ds(TOP, 1)]
-            buf[e, pl.ds(TOP + NY, 1)] = -buf[e, pl.ds(TOP + NY - 1, 1)]
+        for e in (2, 3):
+            U[e, own] = given[0][NX - 1, own]
+            F[e, own] = given[3][NX - 1, own]
+        V[2, own] = given[1][NX - 1, own]
+        W[2, own] = given[2][NX - 1, own]
+
+    fill_shifts(buffers, Z[...], range(4), (0, 1, 10, 11))
+    line = [(buffers, 0), (buffers, 1), (given, 0), (given, 1)]
+    line_high = [(given, NX - 2), (given, NX - 1), (buffers, 2), (buffers, 3)]
+
+    def block(i, carry):
+        y = pl.multiple_of(i * 8, 8)
+        rows = pl.ds(y, 8)
+        for x, end, planes in ((0, 0, line), (NX - 1, 1, line_high)):
+            inner, outer = (planes[1:], planes[:3]) if x == 0 else (planes[:3], planes[1:])
+            mid[0, x, rows], mid[1, x, rows], mid[2, x, rows], frac_new[x, rows] = cells(
+                *inner, Z, x + 2, y, (0, 1, 2)
+            )
+            (end_mid[end, rows],) = cells(*outer, Z, 1 + 9 * end, y, (0,))
         return carry
 
-    lax.fori_loop(0, 12, shift_fraction, 0)
-
-    def cells(e, y, components):
-        lane = lanes(8)
-        at_low = lane == 0
-        at_high = lane == 127
-        here, up, down = pl.ds(y + TOP, 8), pl.ds(y + TOP + 1, 8), pl.ds(y + TOP - 1, 8)
-        ends_all = Z[pl.ds(y, 8), :]
-
-        def star(buf, k):
-            centre = buf[e, here]
-            ends = pltpu.roll(ends_all, 128 - 2 * (12 * k + e) - 1, 1)
-            behind = jnp.where(at_low, ends, pltpu.roll(centre, 1, 1))
-            ahead = jnp.where(at_high, ends, pltpu.roll(centre, 127, 1))
-            return centre, (
-                (buf[e + 1, here], buf[e - 1, here]),
-                (buf[e, up], buf[e, down]),
-                (ahead, behind),
-            )
-
-        c = F[e, here]
-        around = ((F[e + 1, here], F[e - 1, here]), (F[e, up], F[e, down]), (FP[e, here], FM[e, here]))
-        d = [p - m for p, m in around]
-        second = [p + m - 2.0 * c for p, m in around]
-        mxy = (F[e + 1, up] - F[e + 1, down]) - (F[e - 1, up] - F[e - 1, down])
-        mxz = (FP[e + 1, here] - FM[e + 1, here]) - (FP[e - 1, here] - FM[e - 1, here])
-        myz = (FP[e, up] - FM[e, up]) - (FP[e, down] - FM[e, down])
-        dd = [v * v for v in d]
-        inverse = lax.rsqrt(jnp.maximum(dd[0] + dd[1] + dd[2], 1.0))
-        bend = (dd[0] * second[0] + dd[1] * second[1] + dd[2] * second[2]) + 0.5 * (
-            d[0] * (d[1] * mxy + d[2] * mxz) + d[1] * d[2] * myz
-        )
-        laplace = second[0] + second[1] + second[2]
-        volume = 1.0 / (0.5 + 0.5 * c)
-        pull = (bend * (inverse * inverse) - laplace) * (0.5 * inverse) * volume
-        nu = (0.02 + 0.03 * c) * volume
-        if len(components) == 3:
-            stars = [star(buf, k) for k, buf in enumerate((U, V, W))]
-            centres = [s[0] for s in stars]
-        else:
-            stars = [star(U, 0)]
-            centres = [stars[0][0], V[e, here], W[e, here]]
-        speeds = [jnp.abs(v) for v in centres]
-        if len(components) == 3:
-            guesses = star(G, 4)[1]
-        else:
-            guesses = ((G[e + 1, here], G[e - 1, here]),)
-        lift = 2.0 - volume
-        out = []
-        for k in components:
-            centre, sides_ = stars[k]
-            twice = 2.0 * centre
-            transport = 0.0
-            diffusion = 0.0
-            for a in range(3):
-                p, m = sides_[a]
-                curve = p + m - twice
-                transport = transport + (centres[a] * (p - m) - speeds[a] * curve)
-                diffusion = diffusion + curve
-            change = nu * diffusion + pull * d[k] - 0.5 * transport
-            p, m = guesses[k]
-            out.append(centre + 0.1 * (change + 0.5 * (lift * (p - m))))
-        if len(components) == 1:
-            return out
-        net = 0.0
-        for a in range(3):
-            p, m = stars[a][1][a]
-            fp, fm = around[a]
-            ahead = centres[a] + p
-            behind = centres[a] + m
-            net = net + (
-                (jnp.maximum(ahead, 0.0) - jnp.minimum(behind, 0.0)) * c
-                + (jnp.minimum(ahead, 0.0) * fp - jnp.maximum(behind, 0.0) * fm)
-            )
-        return out + [c - 0.05 * net]
-
-    def block(i, carry):
-        x = i // 16
-        y = pl.multiple_of((i % 16) * 8, 8)
-        u, v, w, f = cells(x + 2, y, (0, 1, 2))
-        rows = pl.ds(y, 8)
-        mid[0, x, rows] = u
-        mid[1, x, rows] = v
-        mid[2, x, rows] = w
-        frac_new[x, rows] = f
-        return carry
-
-    lax.fori_loop(0, 16 * NX, block, 0, unroll=4)
-
-    def end_block(i, carry):
-        side = i // 16
-        y = pl.multiple_of((i % 16) * 8, 8)
-        (u,) = cells(1 + 9 * side, y, (0,))
-        end_mid[side, pl.ds(y, 8)] = u
-        return carry
-
-    lax.fori_loop(0, 32, end_block, 0, unroll=4)
-
-    lane = lanes(NY)
-    row = lax.broadcasted_iota(jnp.int32, (NY, 128), 0)
-    pack[...] = jnp.zeros((NY, 128), F32)
-    for x in range(NX):
-        before = mid[0, x - 1] if x > 0 else end_mid[0]
-        after = mid[0, x + 1] if x < NX - 1 else end_mid[1]
-        v = mid[1, x]
-        w = mid[2, x]
-        v_up = jnp.where(row == NY - 1, 0.0, pltpu.roll(v, NY - 1, 0))
-        v_down = jnp.where(row == 0, 0.0, pltpu.roll(v, 1, 0))
-        w_up = jnp.where(lane == NZ - 1, 0.0, pltpu.roll(w, NZ - 1, 1))
-        w_down = jnp.where(lane == 0, 0.0, pltpu.roll(w, 1, 1))
-        s = 2.5 * ((after - before) + (v_up - v_down) + (w_up - w_down))
-        source[x] = s
-        part = jnp.dot(s, moments[0], precision=HIGHEST, preferred_element_type=F32) + jnp.dot(
-            w, moments[1], precision=HIGHEST, preferred_element_type=F32
-        )
-        pack[...] += pltpu.roll(part, 16 * x, 1) if x else part
+    lax.fori_loop(0, 16, block, 0)
+    pack[...] = given_pack[...]
+    source_plane(0, end_mid[0], given_mid[0, 1], mid, 0, moments, source, pack)
+    source_plane(1, mid[0, 0], given_mid[0, 2], given_mid, 1, moments, source, pack)
+    source_plane(6, given_mid[0, 5], mid[0, 7], given_mid, 6, moments, source, pack)
+    source_plane(7, given_mid[0, 6], end_mid[1], mid, 7, moments, source, pack)
+    for copy in kept:
+        copy.wait()
 
 
 def combine_body(a, b, c, d, table, _, message, out, sem):
@@ -362,65 +400,84 @@
         copy.wait()
 
 
+HALO = POWERS
+
+
+def ghosts(out, m, plane):
+    out[m, plane, pl.ds(TOP - 1, 1)] = out[m, plane, pl.ds(TOP, 1)]
+    out[m, plane, pl.ds(TOP + NY, 1)] = out[m, plane, pl.ds(TOP + NY - 1, 1)]
+
+def own_plane(x, carry):
+    moments = pltpu.roll(far[...], (128 - 16 * x) % 128, 1)
+    terms(x + halo, source[x], moments, 0)
+    return carry
+
+
+def terms(table, U, E, lhs, row, plane, values, moments, start):
+    lane = lanes(NY)
+    head = values.astype(BF16)
+    tail = (values - head.astype(F32)).astype(BF16)
+    m_head = moments.astype(BF16).astype(F32)
+    m_tail = moments - m_head
+    side = jnp.where(
+        lane < 16,
+        m_head,
+        jnp.where(
+            lane < 32,
+            pltpu.roll(m_tail, 16, 1),
+            jnp.where(lane < 48, pltpu.roll(m_head, 32, 1), 0.0),
+        ),
+    )
+    lhs[:, 0:128] = head
+    lhs[:, 128:256] = tail
+    lhs[:, 256:384] = head
+    lhs[:, 384:512] = side.astype(BF16)
+    result = jnp.dot(lhs[...], table[:, start * 128 :], preferred_element_type=F32)
+    for m in range(start, POWERS):
+        U[m, row, pl.ds(TOP, NY)] = result[:, (m - start) * 128 : (m - start + 1) * 128]
+        ghosts(U, m, row)
+    ends = result[:, (POWERS - start) * 128 :]
+    group, offset = plane // 8, 16 * (plane % 8)
+    E[group] += pltpu.roll(ends, offset, 1)
+
+
+def own_terms_body(source, far, table, U, E, lhs):
+    E[...] = jnp.zeros((3, NY, 128), F32)
+
+    def own_plane(x, carry):
+        moments = pltpu.roll(far[...], (128 - 16 * x) % 128, 1)
+        terms(table, U, E, lhs, x, x + HALO, source[x], moments, 0)
+        return carry
+
+    lax.fori_loop(0, NX, own_plane, 0)
+
+
 def solve_body(more, *refs):
-    (flags, mid, frac, now, source, paired, other, far, table) = refs[:9]
+    (flags, mid, frac, now, paired, other, table, given_U, given_E) = refs[:9]
     vel, pressure = refs[9:11]
-    U, E, lhs = refs[-3:]
+    U, E, lhs, sem = refs[-4:]
     if more:
         faces_paired, faces_other, packed, guess = refs[11:15]
     first = flags[0] == 1
     last = flags[1] == 1
-    halo = POWERS
-
-    def terms(plane, values, moments, start):
-        lane = lanes(NY)
-        head = values.astype(BF16)
-        tail = (values - head.astype(F32)).astype(BF16)
-        m_head = moments.astype(BF16).astype(F32)
-        m_tail = moments - m_head
-        side = jnp.where(
-            lane < 16,
-            m_head,
-            jnp.where(
-                lane < 32,
-                pltpu.roll(m_tail, 16, 1),
-                jnp.where(lane < 48, pltpu.roll(m_head, 32, 1), 0.0),
-            ),
-        )
-        lhs[:, 0:128] = head
-        lhs[:, 128:256] = tail
-        lhs[:, 256:384] = head
-        lhs[:, 384:512] = side.astype(BF16)
-        result = jnp.dot(lhs[...], table[:, start * 128 :], preferred_element_type=F32)
-        for m in range(start, POWERS):
-            U[m, plane, pl.ds(TOP, NY)] = result[:, (m - start) * 128 : (m - start + 1) * 128]
-            ghosts(U, m, plane)
-        ends = result[:, (POWERS - start) * 128 :]
-        group, offset = plane // 8, 16 * (plane % 8)
-        E[group] += pltpu.roll(ends, offset, 1)
+    halo = HALO
+    fetch = pltpu.make_async_copy(given_U, U.at[:, pl.ds(halo, NX)], sem)
+    fetch.start()
+    E[...] = given_E[...]
 
     def inside(plane):
         kept = ((plane >= halo) | jnp.logical_not(first)) & ((plane < halo + NX) | jnp.logical_not(last))
         return jnp.where(kept, 1.0, 0.0).astype(F32)
 
-    def ghosts(out, m, plane):
-        out[m, plane, pl.ds(TOP - 1, 1)] = out[m, plane, pl.ds(TOP, 1)]
-        out[m, plane, pl.ds(TOP + NY, 1)] = out[m, plane, pl.ds(TOP + NY - 1, 1)]
-
-    def own_plane(x, carry):
-        moments = pltpu.roll(far[...], (128 - 16 * x) % 128, 1)
-        terms(x + halo, source[x], moments, 0)
-        return carry
-
-    E[...] = jnp.zeros((3, NY, 128), F32)
-    lax.fori_loop(0, NX, own_plane, 0)
     even = flags[2] == 1
     for k in range(1, halo + 1):
         for message, upper in ((paired, even), (other, jnp.logical_not(even))):
             x = jnp.where(upper, k - 1, NX - k)
             moments = pltpu.roll(message[NX], (128 - 16 * x) % 128, 1)
-            terms(jnp.where(upper, halo + NX - 1 + k, halo - k), message[x], moments, k - 1)
-
+            plane = jnp.where(upper, halo + NX - 1 + k, halo - k)
+            terms(table, U, E, lhs, plane, plane, message[x], moments, k - 1)
+
+    fetch.wait()
     for m in range(POWERS - 2, -1, -1):
         reach = m + 1
 
@@ -510,23 +567,45 @@
     )(flags, velocity, fraction, now, old)
 
 
-def predict_call(flags, velocity, fraction, guess, paired, other, sides, profile, moments):
-    padded = pltpu.VMEM((12, ROWS, NZ), F32)
+PADDED = (NX, ROWS, NZ)
+PREDICTED = tuple(shape(*PADDED) for _ in range(7)) + (
+    shape(3, *BLOCK),
+    shape(*BLOCK),
+    shape(*MESSAGE),
+    shape(NY, 128),
+)
+
+
+def inner_call(velocity, fraction, guess, sides, moments):
     return pl.pallas_call(
-        predict_body,
-        out_shape=(shape(3, *BLOCK), shape(*BLOCK), shape(*MESSAGE), shape(NY, 128)),
-        in_specs=[IN_SMEM] + [ANYWHERE] * 5 + [IN_VMEM] * 3,
+        inner_body,
+        out_shape=PREDICTED,
+        in_specs=[ANYWHERE] * 3 + [IN_VMEM] * 2,
+        out_specs=(IN_VMEM,) * 11,
+        scratch_shapes=[pltpu.SemaphoreType.DMA((5,))],
+        compiler_params=pltpu.CompilerParams(vmem_limit_bytes=16 * MIB),
+        cost_estimate=pl.CostEstimate(flops=20_000_000, bytes_accessed=16_000_000, transcendentals=100_000),
+        name="inner",
+    )(velocity, fraction, guess, sides, moments)
+
+
+def outer_call(flags, paired, other, sides, profile, moments, inner):
+    return pl.pallas_call(
+        outer_body,
+        out_shape=PREDICTED[7:],
+        in_specs=[IN_SMEM] + [ANYWHERE] * 2 + [IN_VMEM] * 3 + [IN_VMEM] * 8 + [ANYWHERE] * 2 + [IN_VMEM],
         out_specs=(IN_VMEM,) * 4,
-        scratch_shapes=[padded] * 7
+        scratch_shapes=[pltpu.VMEM((4, ROWS, NZ), F32)] * 7
         + [
             pltpu.VMEM((NY, 128), F32),
             pltpu.VMEM((2, NY, 128), F32),
             pltpu.VMEM((2, NY, NZ), F32),
-            pltpu.SemaphoreType.DMA((17,)),
+            pltpu.SemaphoreType.DMA((12,)),
+            pltpu.SemaphoreType.DMA((5,)),
         ],
-        compiler_params=pltpu.CompilerParams(vmem_limit_bytes=18 * MIB),
-        name="predict",
-    )(flags, velocity, fraction, guess, paired, other, sides, profile, moments)
+        compiler_params=pltpu.CompilerParams(vmem_limit_bytes=16 * MIB),
+        name="outer",
+    )(flags, paired, other, sides, profile, moments, *inner)
 
 
 def combine_call(packs, table, message):
@@ -555,24 +634,40 @@
     )(before, after, right, left)
 
 
-def solve_call(more, flags, mid, frac, now, source, paired, other, far, table):
+OWN_TERMS = (POWERS, NX, ROWS, NZ)
+
+
+def own_terms_call(source, far, table):
+    return pl.pallas_call(
+        own_terms_body,
+        out_shape=(shape(*OWN_TERMS), shape(3, NY, 128)),
+        in_specs=[IN_VMEM] * 3,
+        out_specs=(IN_VMEM,) * 2,
+        scratch_shapes=[pltpu.VMEM((NY, 512), BF16)],
+        compiler_params=pltpu.CompilerParams(vmem_limit_bytes=20 * MIB),
+        cost_estimate=pl.CostEstimate(flops=1_000_000_000, bytes_accessed=12_000_000, transcendentals=0),
+        name="own_terms",
+    )(source, far, table)
+
+
+def solve_call(more, flags, mid, frac, now, paired, other, table, own):
     outs = [shape(3, *BLOCK), shape(*BLOCK)]
     if more:
         outs += [shape(*MESSAGE), shape(*MESSAGE), shape(NY, 128), shape(*BLOCK)]
-    planes = NX + 2 * POWERS
     return pl.pallas_call(
         functools.partial(solve_body, more),
         out_shape=tuple(outs),
-        in_specs=[IN_SMEM] + [IN_VMEM] * 8,
+        in_specs=[IN_SMEM] + [IN_VMEM] * 6 + [ANYWHERE, IN_VMEM],
         out_specs=(IN_VMEM,) * len(outs),
         scratch_shapes=[
-            pltpu.VMEM((POWERS, planes, ROWS, NZ), F32),
+            pltpu.VMEM((POWERS, NX + 2 * HALO, ROWS, NZ), F32),
             pltpu.VMEM((3, NY, 128), F32),
             pltpu.VMEM((NY, 512), BF16),
+            pltpu.SemaphoreType.DMA,
         ],
-        compiler_params=pltpu.CompilerParams(vmem_limit_bytes=24 * MIB),
+        compiler_params=pltpu.CompilerParams(vmem_limit_bytes=20 * MIB),
         name="solve",
-    )(flags, mid, frac, now, source, paired, other, far, table)
+    )(flags, mid, frac, now, paired, other, table, *own)
 
 
 def per_device(velocity, fraction, pressure_now, pressure_old, inflow):
@@ -602,13 +697,13 @@
         paired, other, sides = merge_call(around(packed, -1), around(packed, 1), paired, other)
         other = exchange(other, False)
         paired = exchange(paired, True)
-        mid, fraction, source, pack = predict_call(
-            flags, velocity, fraction, guess, paired, other, sides, profile, moments
-        )
+        inner = inner_call(velocity, fraction, guess, sides, moments)
+        mid, fraction, source, pack = outer_call(flags, paired, other, sides, profile, moments, inner)
         source, far = combine_call([pack] + [around(pack, o) for o in (1, 2, 3)], combine, source)
-        results = solve_call(
-            more, flags, mid, fraction, now, source, exchange(source, True), exchange(source, False), far, table
-        )
+        other = exchange(source, False)
+        paired = exchange(source, True)
+        own = own_terms_call(source, far, table)
+        results = solve_call(more, flags, mid, fraction, now, paired, other, table, own)
         velocity, pressure = results[:2]
         old, now = now, pressure
         if more:

time: 171 us -> 154 us (0.901)
  waiting for transfers between devices: 71.2 us -> 53.1 us
  Pallas kernels: 50.4 us -> 52.3 us
    ppermute x8, waiting for transfers between devices: 58.1 us -> 40.1 us  [exchange(): return lax.ppermute(block, 'stream', pairs if with_pair else others)]
    pallas_call x2 -> x6, Pallas kernels: 20.7 us -> 29.8 us  [the longest x2 12.1 us: outer_call(): pl.pallas_call(outer_body, out_shape=PREDICTED[7:], in_specs=[IN_SMEM] +...]
    pallas_call x2, Pallas kernels: 26.8 us -> 19.7 us  [solve_call(): pl.pallas_call(functools.partial(solve_body, more), out_shape=tuple(outs)...]
  transfers between devices with their start and end apart: 18 -> 18, of which waited for: 13 -> 13; matrix products, arithmetic and copies ran while one was open for 0% -> 0% of each run, Pallas kernels for 0% -> 11%
where the time goes in v3:
time: 154 us
  waiting for transfers between devices  53.1 us (34%)
  Pallas kernels  52.3 us (34%)
  starting transfers between devices  42.6 us (28%)
  local copies, waits for them, and re-layouts  4.67 us (3%)
    ppermute x8, waiting for transfers between devices, exchange(): return lax.ppermute(block, 'stream', pairs if with_pair else others)  40.1 us
    ppermute x8, starting transfers between devices, exchange(): return lax.ppermute(block, 'stream', pairs if with_pair else others)  32.7 us
    pallas_call x2, Pallas kernels, solve_call(): pl.pallas_call(functools.partial(solve_body, more), out_shape=tuple(outs)...  19.7 us
    ppermute x10, waiting for transfers between devices, around(): lax.ppermute(block, 'span', [((i + offset) % BLOCKS, i) for i in range(BL...  13 us
    pallas_call x2, Pallas kernels, outer_call(): pl.pallas_call(outer_body, out_shape=PREDICTED[7:], in_specs=[IN_SMEM] +...  12.1 us
    pallas_call x2, Pallas kernels, inner_call(): pl.pallas_call(inner_body, out_shape=PREDICTED, in_specs=[ANYWHERE] * 3 +...  9.94 us
    ppermute x10, starting transfers between devices, around(): lax.ppermute(block, 'span', [((i + offset) % BLOCKS, i) for i in range(BL...  9.94 us
    pallas_call x2, Pallas kernels, own_terms_call(): pl.pallas_call(own_terms_body, out_shape=(shape(*OWN_TERMS), shape(3, NY,...  7.73 us
  transfers between devices with their start and end apart: 18, of which 13 were waited for; matrix products, arithmetic and copies ran while one was open for 0% of the time, Pallas kernels for 11%

profile of v3, /device:TPU:7, one launch (start us, length us, event | category | flops | bytes accessed | tf_op | source)
XLA Modules:
  0.0 153.8 jit_solution(9619513631172851934)
XLA Ops:
  8.5 2.7 %collective-permute-done.1.after = f32[128,128]{1,0:T(8,128)S(1)} collective-permute-done((f32[128,128]{1,0:T(8,128)S(1)}, f32[128,128]{1,0:T(8,128)S(1)}, u32[]{:S(2)}, u32[]{:S(2)}) %collective-permute-start.1) | collective-permute-done | bytes 65568 | tf_op jit(solution)/shard_map/ppermute | solution.py:684
  11.4 1.7 %collective-permute-start.2 = (f32[9,128,128]{2,1,0:T(8,128)S(1)}, f32[9,128,128]{2,1,0:T(8,128)S(1)}, u32[]{:S(2)}, u32[]{:S(2)}) collective-permute-start(f32[9,128,128]{2,1,0:T(8,128)S(1)} %get-tuple-element.63), channel_id=1, source_target_pairs={{0,4},{4,0},{8,12},{12,8},{16,20},{20,16},{24,28},{28,24},{32,36},... | collective-permute-start | bytes 1769480 | tf_op jit(solution)/shard_map/ppermute | solution.py:681
  13.2 7.6 %collective-permute-start.3 = (f32[9,128,128]{2,1,0:T(8,128)S(1)}, f32[9,128,128]{2,1,0:T(8,128)S(1)}, u32[]{:S(2)}, u32[]{:S(2)}) collective-permute-start(f32[9,128,128]{2,1,0:T(8,128)S(1)} %get-tuple-element.64), channel_id=1, source_target_pairs={{4,8},{8,4},{12,16},{16,12},{20,24},{24,20},{28,32},{32,28},{36,40... | collective-permute-start | bytes 1769480 | tf_op jit(solution)/shard_map/ppermute | solution.py:681
  20.8 5.0 %inner.2 = (f32[8,144,128]{2,1,0:T(8,128)S(1)}, f32[8,144,128]{2,1,0:T(8,128)S(1)}, f32[8,144,128]{2,1,0:T(8,128)S(1)}, f32[8,144,128]{2,1,0:T(8,128)S(1)}, f32[...) custom-call(f32[3,8,128,128]{3,2,1,0:T(8,128)S(1)} %copy-done.1, ...), custom_call_target="tpu_custom_call" | custom-call | flops 20000000 | bytes 16000000 | tf_op jit(solution)/shard_map/inner/pallas_call | solution.py:580
  26.1 8.5 %collective-permute-done.3.other = f32[9,128,128]{2,1,0:T(8,128)S(1)} collective-permute-done((f32[9,128,128]{2,1,0:T(8,128)S(1)}, f32[9,128,128]{2,1,0:T(8,128)S(1)}, u32[]{:S(2)}, u32[]{:S(2)}) %collective-permute-start.3) | collective-permute-done | bytes 589856 | tf_op jit(solution)/shard_map/ppermute | solution.py:681
  34.8 5.7 %outer.2 = (f32[3,8,128,128]{3,2,1,0:T(8,128)S(1)}, f32[8,128,128]{2,1,0:T(8,128)S(1)}, f32[9,128,128]{2,1,0:T(8,128)S(1)}, f32[128,128]{1,0:T(8,128)S(1)}) custom-call(s32[3]{0:T(128)S(1)} %add_convert_fusion.flags.refs_0_, f32[9,128,128]{2,1,0:T(8,128)S(1)} %collective-permute-done.2.paired, f32[9,128,128]{2,1,0:T(8,128)S(1)} %collective-permute-done.3.other, ...), custom_call_target="tpu_custom_call" | custom-call | tf_op jit(solution)/shard_map/outer/pallas_call | solution.py:593
  40.5 2.0 %collective-permute-start.6 = (f32[128,128]{1,0:T(8,128)S(1)}, f32[128,128]{1,0:T(8,128)S(1)}, u32[]{:S(2)}, u32[]{:S(2)}) collective-permute-start(f32[128,128]{1,0:T(8,128)S(1)} %get-tuple-element.80.a), channel_id=1, source_target_pairs={{3,0},{0,1},{1,2},{2,3},{7,4},{4,5},{5,6},{6,7},{11,8},{8,9},{9,10... | collective-permute-start | bytes 196616 | tf_op jit(solution)/shard_map/ppermute | solution.py:684
  43.8 3.2 %collective-permute-done.5.c = f32[128,128]{1,0:T(8,128)S(1)} collective-permute-done((f32[128,128]{1,0:T(8,128)S(1)}, f32[128,128]{1,0:T(8,128)S(1)}, u32[]{:S(2)}, u32[]{:S(2)}) %collective-permute-start.5) | collective-permute-done | bytes 65568 | tf_op jit(solution)/shard_map/ppermute | solution.py:684
  48.0 7.6 %collective-permute-start.8 = (f32[9,128,128]{2,1,0:T(8,128)S(1)}, f32[9,128,128]{2,1,0:T(8,128)S(1)}, u32[]{:S(2)}, u32[]{:S(2)}) collective-permute-start(f32[9,128,128]{2,1,0:T(8,128)S(1)} %get-tuple-element.82.source), channel_id=1, source_target_pairs={{4,8},{8,4},{12,16},{16,12},{20,24},{24,20},{28,32},{32,28},{36,40... | collective-permute-start | bytes 1769480 | tf_op jit(solution)/shard_map/ppermute | solution.py:681
  55.7 3.9 %own_terms.2 = (f32[7,8,144,128]{3,2,1,0:T(8,128)S(1)}, f32[3,128,128]{2,1,0:T(8,128)S(1)}) custom-call(f32[9,128,128]{2,1,0:T(8,128)S(1)} %get-tuple-element.82.source, f32[128,128]{1,0:T(8,128)S(1)} %get-tuple-element.83.far, bf16[512,1024]{1,0:T(8,128)(2,1)S(1)} %copy-done.2), custom_call_target="tpu_custom_call" | custom-call | flops 1000000000 | bytes 12000000 | tf_op jit(solution)/shard_map/own_terms/pallas_call | solution.py:641
  59.6 11.1 %collective-permute-done.8.refs_5_ = f32[9,128,128]{2,1,0:T(8,128)S(1)} collective-permute-done((f32[9,128,128]{2,1,0:T(8,128)S(1)}, f32[9,128,128]{2,1,0:T(8,128)S(1)}, u32[]{:S(2)}, u32[]{:S(2)}) %collective-permute-start.8) | collective-permute-done | bytes 589856 | tf_op jit(solution)/shard_map/ppermute | solution.py:681
  70.7 10.0 %solve.2 = (f32[3,8,128,128]{3,2,1,0:T(8,128)S(1)}, f32[8,128,128]{2,1,0:T(8,128)}, f32[9,128,128]{2,1,0:T(8,128)S(1)}, f32[9,128,128]{2,1,0:T(8,128)S(1)}, f32[...) custom-call(s32[3]{0:T(128)S(1)} %add_convert_fusion.flags.refs_0_, f32[3,8,128,128]{3,2,1,0:T(8,128)S(1)} %get-tuple-element.78.refs_1_, ...), custom_call_target="tpu_custom_call" | custom-call | tf_op jit(solution)/shard_map/solve/pallas_call | solution.py:657
  82.5 2.8 %collective-permute-done.10.after = f32[128,128]{1,0:T(8,128)S(1)} collective-permute-done((f32[128,128]{1,0:T(8,128)S(1)}, f32[128,128]{1,0:T(8,128)S(1)}, u32[]{:S(2)}, u32[]{:S(2)}) %collective-permute-start.10) | collective-permute-done | bytes 65568 | tf_op jit(solution)/shard_map/ppermute | solution.py:684
  85.9 7.7 %collective-permute-start.12 = (f32[9,128,128]{2,1,0:T(8,128)S(1)}, f32[9,128,128]{2,1,0:T(8,128)S(1)}, u32[]{:S(2)}, u32[]{:S(2)}) collective-permute-start(f32[9,128,128]{2,1,0:T(8,128)S(1)} %get-tuple-element.90), channel_id=1, source_target_pairs={{4,8},{8,4},{12,16},{16,12},{20,24},{24,20},{28,32},{32,28},{36,40... | collective-permute-start | bytes 1769480 | tf_op jit(solution)/shard_map/ppermute | solution.py:681
  93.6 5.0 %inner.3 = (f32[8,144,128]{2,1,0:T(8,128)S(1)}, f32[8,144,128]{2,1,0:T(8,128)S(1)}, f32[8,144,128]{2,1,0:T(8,128)S(1)}, f32[8,144,128]{2,1,0:T(8,128)S(1)}, f32[...) custom-call(f32[3,8,128,128]{3,2,1,0:T(8,128)S(1)} %get-tuple-elemen, ...), custom_call_target="tpu_custom_call" | custom-call | flops 20000000 | bytes 16000000 | tf_op jit(solution)/shard_map/inner/pallas_call | solution.py:580
  98.5 1.4 collective-permute-done.11.paired
  100.0 7.6 %collective-permute-done.12.other = f32[9,128,128]{2,1,0:T(8,128)S(1)} collective-permute-done((f32[9,128,128]{2,1,0:T(8,128)S(1)}, f32[9,128,128]{2,1,0:T(8,128)S(1)}, u32[]{:S(2)}, u32[]{:S(2)}) %collective-permute-start.12) | collective-permute-done | bytes 589856 | tf_op jit(solution)/shard_map/ppermute | solution.py:681
  107.6 6.5 %outer.3 = (f32[3,8,128,128]{3,2,1,0:T(8,128)S(1)}, f32[8,128,128]{2,1,0:T(8,128)}, f32[9,128,128]{2,1,0:T(8,128)S(1)}, f32[128,128]{1,0:T(8,128)S(1)}) custom-call(s32[3]{0:T(128)S(1)} %add_convert_fusion.flags.refs_0_, f32[9,128,128]{2,1,0:T(8,128)S(1)} %collective-permute-done.11.paired, f32[9,128,128]{2,1,0:T(8,128)S(1)} %collective-permute-done.12.other, ...), custom_call_target="tpu_custom_call" | custom-call | tf_op jit(solution)/shard_map/outer/pallas_call | solution.py:593
  115.0 2.1 %collective-permute-start.14 = (f32[128,128]{1,0:T(8,128)S(1)}, f32[128,128]{1,0:T(8,128)S(1)}, u32[]{:S(2)}, u32[]{:S(2)}) collective-permute-start(f32[128,128]{1,0:T(8,128)S(1)} %get-tuple-element.108.a), channel_id=1, source_target_pairs={{2,0},{3,1},{0,2},{1,3},{6,4},{7,5},{4,6},{5,7},{10,8},{11,9},{8,1... | collective-permute-start | bytes 196616 | tf_op jit(solution)/shard_map/ppermute | solution.py:684
  117.1 3.3 %collective-permute-done.14.c = f32[128,128]{1,0:T(8,128)S(1)} collective-permute-done((f32[128,128]{1,0:T(8,128)S(1)}, f32[128,128]{1,0:T(8,128)S(1)}, u32[]{:S(2)}, u32[]{:S(2)}) %collective-permute-start.14) | collective-permute-done | bytes 65568 | tf_op jit(solution)/shard_map/ppermute | solution.py:684
  121.3 7.6 %collective-permute-start.17 = (f32[9,128,128]{2,1,0:T(8,128)S(1)}, f32[9,128,128]{2,1,0:T(8,128)S(1)}, u32[]{:S(2)}, u32[]{:S(2)}) collective-permute-start(f32[9,128,128]{2,1,0:T(8,128)S(1)} %get-tuple-element.110.source), channel_id=1, source_target_pairs={{4,8},{8,4},{12,16},{16,12},{20,24},{24,20},{28,32},{32,28},{36,40... | collective-permute-start | bytes 1769480 | tf_op jit(solution)/shard_map/ppermute | solution.py:681
  129.0 3.9 %own_terms.3 = (f32[7,8,144,128]{3,2,1,0:T(8,128)S(1)}, f32[3,128,128]{2,1,0:T(8,128)S(1)}) custom-call(f32[9,128,128]{2,1,0:T(8,128)S(1)} %get-tuple-element.110.source, f32[128,128]{1,0:T(8,128)S(1)} %get-tuple-element.111.far, bf16[512,1024]{1,0:T(8,128)(2,1)S(1)} %copy-done.2), custom_call_target="tpu_custom_call" | custom-call | flops 1000000000 | bytes 12000000 | tf_op jit(solution)/shard_map/own_terms/pallas_call | solution.py:641
  132.9 11.1 %collective-permute-done.17.refs_5_ = f32[9,128,128]{2,1,0:T(8,128)S(1)} collective-permute-done((f32[9,128,128]{2,1,0:T(8,128)S(1)}, f32[9,128,128]{2,1,0:T(8,128)S(1)}, u32[]{:S(2)}, u32[]{:S(2)}) %collective-permute-start.17) | collective-permute-done | bytes 589856 | tf_op jit(solution)/shard_map/ppermute | solution.py:681
  144.0 9.6 %solve.3 = (f32[3,8,128,128]{3,2,1,0:T(8,128)}, f32[8,128,128]{2,1,0:T(8,128)}) custom-call(s32[3]{0:T(128)S(1)} %add_convert_fusion.flags.refs_0_, f32[3,8,128,128]{3,2,1,0:T(8,128)S(1)} %get-tuple-element.105.refs_1_, f32[8,128,128]{2,1,0:T(8,128)S(1)} %copy-done.10, f32[8,128,128]{2,1,0:T(8,128)S(1)} %copy-done.9, ...), custom_call_target="tpu_custom_call" | custom-call | tf_op jit(solution)/shard_map/solve/pallas_call | solution.py:657
  (53 shorter events, 15.3 us)
Async XLA Ops:
  5.3 15.5 %copy-start.1 = (f32[3,8,128,128]{3,2,1,0:T(8,128)S(1)}, f32[3,8,128,128]{3,2,1,0:T(8,128)}, u32[]{:S(2)}) copy-start(f32[3,8,128,128]{3,2,1,0:T(8,128)} %vel.3) | copy-start | bytes 4718596
  5.3 15.5 %copy-start.3 = (f32[2,128,128]{2,1,0:T(8,128)S(1)}, f32[2,128,128]{2,1,0:T(8,128)}, u32[]{:S(2)}) copy-start(f32[2,128,128]{2,1,0:T(8,128)} %constant.28.clone.moments) | copy-start | bytes 393220
  5.3 15.5 %copy-start.7 = (f32[8,128,128]{2,1,0:T(8,128)S(1)}, f32[8,128,128]{2,1,0:T(8,128)}, u32[]{:S(2)}) copy-start(f32[8,128,128]{2,1,0:T(8,128)} %frac.3) | copy-start | bytes 1572868
  6.7 4.5 %collective-permute-start.1 = (f32[128,128]{1,0:T(8,128)S(1)}, f32[128,128]{1,0:T(8,128)S(1)}, u32[]{:S(2)}, u32[]{:S(2)}) collective-permute-start(f32[128,128]{1,0:T(8,128)S(1)} %get-tuple-element.60), channel_id=1, source_target_pairs={{1,0},{2,1},{3,2},{0,3},{5,4},{6,5},{7,6},{4,7},{9,8},{10,9},{11,1... | collective-permute-start | bytes 196616 | tf_op jit(solution)/shard_map/ppermute | solution.py:684
  7.4 3.8 %collective-permute-start = (f32[128,128]{1,0:T(8,128)S(1)}, f32[128,128]{1,0:T(8,128)S(1)}, u32[]{:S(2)}, u32[]{:S(2)}) collective-permute-start(f32[128,128]{1,0:T(8,128)S(1)} %get-tuple-element.60), channel_id=1, source_target_pairs={{3,0},{0,1},{1,2},{2,3},{7,4},{4,5},{5,6},{6,7},{11,8},{8,9},{9,10... | collective-permute-start | bytes 196616 | tf_op jit(solution)/shard_map/ppermute | solution.py:684
  11.4 23.2 %copy-start.12 = (f32[2,128]{1,0:T(2,128)S(1)}, f32[2,128]{1,0:T(2,128)}, u32[]{:S(2)}) copy-start(f32[2,128]{1,0:T(2,128)} %param.12) | copy-start | bytes 3076
  11.4 14.7 %collective-permute-start.2 = (f32[9,128,128]{2,1,0:T(8,128)S(1)}, f32[9,128,128]{2,1,0:T(8,128)S(1)}, u32[]{:S(2)}, u32[]{:S(2)}) collective-permute-start(f32[9,128,128]{2,1,0:T(8,128)S(1)} %get-tuple-element.63), channel_id=1, source_target_pairs={{0,4},{4,0},{8,12},{12,8},{16,20},{20,16},{24,28},{28,24},{32,36},... | collective-permute-start | bytes 1769480 | tf_op jit(solution)/shard_map/ppermute | solution.py:681
  13.2 21.5 %collective-permute-start.3 = (f32[9,128,128]{2,1,0:T(8,128)S(1)}, f32[9,128,128]{2,1,0:T(8,128)S(1)}, u32[]{:S(2)}, u32[]{:S(2)}) collective-permute-start(f32[9,128,128]{2,1,0:T(8,128)S(1)} %get-tuple-element.64), channel_id=1, source_target_pairs={{4,8},{8,4},{12,16},{16,12},{20,24},{24,20},{28,32},{32,28},{36,40... | collective-permute-start | bytes 1769480 | tf_op jit(solution)/shard_map/ppermute | solution.py:681
  34.8 20.9 %copy-start.2 = (bf16[512,1024]{1,0:T(8,128)(2,1)S(1)}, bf16[512,1024]{1,0:T(8,128)(2,1)}, u32[]{:S(2)}) copy-start(bf16[512,1024]{1,0:T(8,128)(2,1)} %constant.30.clone.table.refs_6_) | copy-start | bytes 3145732
  40.5 3.4 %collective-permute-start.6 = (f32[128,128]{1,0:T(8,128)S(1)}, f32[128,128]{1,0:T(8,128)S(1)}, u32[]{:S(2)}, u32[]{:S(2)}) collective-permute-start(f32[128,128]{1,0:T(8,128)S(1)} %get-tuple-element.80.a), channel_id=1, source_target_pairs={{3,0},{0,1},{1,2},{2,3},{7,4},{4,5},{5,6},{6,7},{11,8},{8,9},{9,10... | collective-permute-start | bytes 196616 | tf_op jit(solution)/shard_map/ppermute | solution.py:684
  42.5 4.5 %collective-permute-start.5 = (f32[128,128]{1,0:T(8,128)S(1)}, f32[128,128]{1,0:T(8,128)S(1)}, u32[]{:S(2)}, u32[]{:S(2)}) collective-permute-start(f32[128,128]{1,0:T(8,128)S(1)} %get-tuple-element.80.a), channel_id=1, source_target_pairs={{2,0},{3,1},{0,2},{1,3},{6,4},{7,5},{4,6},{5,7},{10,8},{11,9},{8,1... | collective-permute-start | bytes 196616 | tf_op jit(solution)/shard_map/ppermute | solution.py:684
  43.7 3.8 %collective-permute-start.4 = (f32[128,128]{1,0:T(8,128)S(1)}, f32[128,128]{1,0:T(8,128)S(1)}, u32[]{:S(2)}, u32[]{:S(2)}) collective-permute-start(f32[128,128]{1,0:T(8,128)S(1)} %get-tuple-element.80.a), channel_id=1, source_target_pairs={{1,0},{2,1},{3,2},{0,3},{5,4},{6,5},{7,6},{4,7},{9,8},{10,9},{11,1... | collective-permute-start | bytes 196616 | tf_op jit(solution)/shard_map/ppermute | solution.py:684
  48.0 22.7 %collective-permute-start.8 = (f32[9,128,128]{2,1,0:T(8,128)S(1)}, f32[9,128,128]{2,1,0:T(8,128)S(1)}, u32[]{:S(2)}, u32[]{:S(2)}) collective-permute-start(f32[9,128,128]{2,1,0:T(8,128)S(1)} %get-tuple-element.82.source), channel_id=1, source_target_pairs={{4,8},{8,4},{12,16},{16,12},{20,24},{24,20},{28,32},{32,28},{36,40... | collective-permute-start | bytes 1769480 | tf_op jit(solution)/shard_map/ppermute | solution.py:681
  55.6 15.1 %collective-permute-start.7 = (f32[9,128,128]{2,1,0:T(8,128)S(1)}, f32[9,128,128]{2,1,0:T(8,128)S(1)}, u32[]{:S(2)}, u32[]{:S(2)}) collective-permute-start(f32[9,128,128]{2,1,0:T(8,128)S(1)} %get-tuple-element.82.source), channel_id=1, source_target_pairs={{0,4},{4,0},{8,12},{12,8},{16,20},{20,16},{24,28},{28,24},{32,36},... | collective-permute-start | bytes 1769480 | tf_op jit(solution)/shard_map/ppermute | solution.py:681
  80.7 4.6 %collective-permute-start.10 = (f32[128,128]{1,0:T(8,128)S(1)}, f32[128,128]{1,0:T(8,128)S(1)}, u32[]{:S(2)}, u32[]{:S(2)}) collective-permute-start(f32[128,128]{1,0:T(8,128)S(1)} %get-tuple-element.86), channel_id=1, source_target_pairs={{1,0},{2,1},{3,2},{0,3},{5,4},{6,5},{7,6},{4,7},{9,8},{10,9},{11,1... | collective-permute-start | bytes 196616 | tf_op jit(solution)/shard_map/ppermute | solution.py:684
  81.5 3.8 %collective-permute-start.9 = (f32[128,128]{1,0:T(8,128)S(1)}, f32[128,128]{1,0:T(8,128)S(1)}, u32[]{:S(2)}, u32[]{:S(2)}) collective-permute-start(f32[128,128]{1,0:T(8,128)S(1)} %get-tuple-element.86), channel_id=1, source_target_pairs={{3,0},{0,1},{1,2},{2,3},{7,4},{4,5},{5,6},{6,7},{11,8},{8,9},{9,10... | collective-permute-start | bytes 196616 | tf_op jit(solution)/shard_map/ppermute | solution.py:684
  85.6 14.4 %collective-permute-start.11 = (f32[9,128,128]{2,1,0:T(8,128)S(1)}, f32[9,128,128]{2,1,0:T(8,128)S(1)}, u32[]{:S(2)}, u32[]{:S(2)}) collective-permute-start(f32[9,128,128]{2,1,0:T(8,128)S(1)} %get-tuple-element.89), channel_id=1, source_target_pairs={{0,4},{4,0},{8,12},{12,8},{16,20},{20,16},{24,28},{28,24},{32,36},... | collective-permute-start | bytes 1769480 | tf_op jit(solution)/shard_map/ppermute | solution.py:681
  85.9 21.7 %collective-permute-start.12 = (f32[9,128,128]{2,1,0:T(8,128)S(1)}, f32[9,128,128]{2,1,0:T(8,128)S(1)}, u32[]{:S(2)}, u32[]{:S(2)}) collective-permute-start(f32[9,128,128]{2,1,0:T(8,128)S(1)} %get-tuple-element.90), channel_id=1, source_target_pairs={{4,8},{8,4},{12,16},{16,12},{20,24},{24,20},{28,32},{32,28},{36,40... | collective-permute-start | bytes 1769480 | tf_op jit(solution)/shard_map/ppermute | solution.py:681
  114.0 3.0 %collective-permute-start.15 = (f32[128,128]{1,0:T(8,128)S(1)}, f32[128,128]{1,0:T(8,128)S(1)}, u32[]{:S(2)}, u32[]{:S(2)}) collective-permute-start(f32[128,128]{1,0:T(8,128)S(1)} %get-tuple-element.108.a), channel_id=1, source_target_pairs={{3,0},{0,1},{1,2},{2,3},{7,4},{4,5},{5,6},{6,7},{11,8},{8,9},{9,10... | collective-permute-start | bytes 196616 | tf_op jit(solution)/shard_map/ppermute | solution.py:684
  115.0 5.3 %collective-permute-start.14 = (f32[128,128]{1,0:T(8,128)S(1)}, f32[128,128]{1,0:T(8,128)S(1)}, u32[]{:S(2)}, u32[]{:S(2)}) collective-permute-start(f32[128,128]{1,0:T(8,128)S(1)} %get-tuple-element.108.a), channel_id=1, source_target_pairs={{2,0},{3,1},{0,2},{1,3},{6,4},{7,5},{4,6},{5,7},{10,8},{11,9},{8,1... | collective-permute-start | bytes 196616 | tf_op jit(solution)/shard_map/ppermute | solution.py:684
  117.1 3.8 %collective-permute-start.13 = (f32[128,128]{1,0:T(8,128)S(1)}, f32[128,128]{1,0:T(8,128)S(1)}, u32[]{:S(2)}, u32[]{:S(2)}) collective-permute-start(f32[128,128]{1,0:T(8,128)S(1)} %get-tuple-element.108.a), channel_id=1, source_target_pairs={{1,0},{2,1},{3,2},{0,3},{5,4},{6,5},{7,6},{4,7},{9,8},{10,9},{11,1... | collective-permute-start | bytes 196616 | tf_op jit(solution)/shard_map/ppermute | solution.py:684
  121.3 22.7 %collective-permute-start.17 = (f32[9,128,128]{2,1,0:T(8,128)S(1)}, f32[9,128,128]{2,1,0:T(8,128)S(1)}, u32[]{:S(2)}, u32[]{:S(2)}) collective-permute-start(f32[9,128,128]{2,1,0:T(8,128)S(1)} %get-tuple-element.110.source), channel_id=1, source_target_pairs={{4,8},{8,4},{12,16},{16,12},{20,24},{24,20},{28,32},{32,28},{36,40... | collective-permute-start | bytes 1769480 | tf_op jit(solution)/shard_map/ppermute | solution.py:681
  128.9 15.1 %collective-permute-start.16 = (f32[9,128,128]{2,1,0:T(8,128)S(1)}, f32[9,128,128]{2,1,0:T(8,128)S(1)}, u32[]{:S(2)}, u32[]{:S(2)}) collective-permute-start(f32[9,128,128]{2,1,0:T(8,128)S(1)} %get-tuple-element.110.source), channel_id=1, source_target_pairs={{0,4},{4,0},{8,12},{12,8},{16,20},{20,16},{24,28},{28,24},{32,36},... | collective-permute-start | bytes 1769480 | tf_op jit(solution)/shard_map/ppermute | solution.py:681
  129.0 15.0 %copy-start.9 = (f32[8,128,128]{2,1,0:T(8,128)S(1)}, f32[8,128,128]{2,1,0:T(8,128)}, u32[]{:S(2)}) copy-start(f32[8,128,128]{2,1,0:T(8,128)} %get-tuple-element.59.refs_3_) | copy-start | bytes 1572868
  (7 other events, 47.3 us)

commit v4 on v3

--- a/solution.py
+++ b/solution.py
@@ -125,7 +125,10 @@
     return packed
 
 
-def pack_body(flags, vel, frac, now, old, paired, other, packed, guess):
+def pack_body(flags, vel_far, frac_far, now_far, old_far, paired, other, packed, guess, vel, frac, now, old, sem):
+    pairs = [(now_far, now), (old_far, old), (frac_far, frac)] + [(vel_far.at[k], vel.at[k]) for k in range(3)]
+    for copy in start_copies(pairs, sem):
+        copy.wait()
     for x in range(NX):
         guess[x] = 2.0 * now[x] - old[x]
     emit_faces(flags, vel, frac, guess, paired, other, packed)
@@ -248,21 +251,19 @@
     return out + [c - 0.05 * net]
 
 
-def source_plane(x, before, after, mid, mx, moments, source, pack):
+def source_plane(x, before, after, v, w, moments, pack):
     lane = lanes(NY)
     row = lax.broadcasted_iota(jnp.int32, (NY, 128), 0)
-    v = mid[1, mx]
-    w = mid[2, mx]
     v_up = jnp.where(row == NY - 1, 0.0, pltpu.roll(v, NY - 1, 0))
     v_down = jnp.where(row == 0, 0.0, pltpu.roll(v, 1, 0))
     w_up = jnp.where(lane == NZ - 1, 0.0, pltpu.roll(w, NZ - 1, 1))
     w_down = jnp.where(lane == 0, 0.0, pltpu.roll(w, 1, 1))
     s = 2.5 * ((after - before) + (v_up - v_down) + (w_up - w_down))
-    source[x] = s
     part = jnp.dot(s, moments[0], precision=HIGHEST, preferred_element_type=F32) + jnp.dot(
         w, moments[1], precision=HIGHEST, preferred_element_type=F32
     )
     pack[...] += pltpu.roll(part, 16 * x, 1) if x else part
+    return s
 
 
 def start_copies(pairs, sem):
@@ -295,87 +296,115 @@
 
     lax.fori_loop(0, 16 * (NX - 2), block, 0, unroll=4)
     for x in range(2, NX - 2):
-        source_plane(x, mid[0, x - 1], mid[0, x + 1], mid, x, moments, source, pack)
-
-
-def outer_body(flags, paired, other, sides, profile, moments, *refs):
-    given, (given_mid, given_frac, given_source, given_pack) = refs[:7], refs[7:11]
-    mid, frac_new, source, pack = refs[11:15]
-    buffers = refs[15:22]
-    Z, Z_ends, end_mid, sem, keep_sem = refs[22:]
+        source[x] = source_plane(x, mid[0, x - 1], mid[0, x + 1], mid[1, x], mid[2, x], moments, pack)
+
+
+def side_part(up, at_end, message, sides, profile, moments, given, given_mid, mid, frac, source, pack, scratch):
+    buffers, (Z, end_mid, sem) = scratch[:7], scratch[7:]
     U, V, W, F, G = buffers[:5]
     own = pl.ds(TOP, NY)
-    middle = pl.ds(1, NX - 2)
-    kept = [(given_mid.at[k, middle], mid.at[k, middle]) for k in range(3)]
-    kept += [(given_frac.at[middle], frac_new.at[middle])]
-    kept += [(given_source.at[pl.ds(2, NX - 4)], source.at[pl.ds(2, NX - 4)])]
-    kept = start_copies(kept, keep_sem)
-    even = flags[2] == 1
-    pairs = []
-    for msg, upper in ((paired, even), (other, jnp.logical_not(even))):
-        far = jnp.where(upper, 2, 0)
-        near = jnp.where(upper, 2, 1)
-        pairs += [
-            (msg.at[pl.ds(0, 2)], U.at[pl.ds(far, 2), own]),
-            (msg.at[2], V.at[near, own]),
-            (msg.at[3], W.at[near, own]),
-            (msg.at[pl.ds(4, 2)], F.at[pl.ds(far, 2), own]),
-            (msg.at[pl.ds(6, 2)], G.at[pl.ds(far, 2), own]),
-            (msg.at[8], Z_ends.at[jnp.where(upper, 1, 0)]),
-        ]
+    near = 0 if up else 1
+    pairs = [
+        (message.at[pl.ds(0, 2)], U.at[:, own]),
+        (message.at[2], V.at[near, own]),
+        (message.at[3], W.at[near, own]),
+        (message.at[pl.ds(4, 2)], F.at[:, own]),
+        (message.at[pl.ds(6, 2)], G.at[:, own]),
+        (message.at[8], Z),
+    ]
     for copy in start_copies(pairs, sem):
         copy.wait()
-
-    first = flags[0] == 1
-    last = flags[1] == 1
     lane = lanes(NY)
-    place = lane // 2
-    slot = place % 12
-    group = place // 12
+    slot = lane // 2 % 12
+    group = lane // 2 // 12
     merged = sides[...]
-    below = pltpu.roll(Z_ends[0], 112, 1)
-    above = pltpu.roll(Z_ends[1], 16, 1)
-    below_wall = jnp.where(group == 0, profile[0], jnp.where(group == 3, profile[1], 0.0))
-    above_wall = jnp.where(slot == 10, pltpu.roll(merged, 2, 1), pltpu.roll(merged, 4, 1))
-    below = jnp.where(first, below_wall, below)
-    above = jnp.where(last, above_wall, above)
-    Z[...] = jnp.where(slot < 2, below, jnp.where(slot >= 10, above, merged))
-
-    @pl.when(first)
-    def _():
-        for e in range(2):
-            U[e, own] = profile[0]
-            F[e, own] = profile[1]
-
-    @pl.when(last)
-    def _():
-        for e in (2, 3):
-            U[e, own] = given[0][NX - 1, own]
-            F[e, own] = given[3][NX - 1, own]
-        V[2, own] = given[1][NX - 1, own]
-        W[2, own] = given[2][NX - 1, own]
-
-    fill_shifts(buffers, Z[...], range(4), (0, 1, 10, 11))
-    line = [(buffers, 0), (buffers, 1), (given, 0), (given, 1)]
-    line_high = [(given, NX - 2), (given, NX - 1), (buffers, 2), (buffers, 3)]
+    if up:
+        beyond = pltpu.roll(Z[...], 16, 1)
+        if at_end is not None:
+            wall = jnp.where(slot == 10, pltpu.roll(merged, 2, 1), pltpu.roll(merged, 4, 1))
+            beyond = jnp.where(at_end, wall, beyond)
+        Z[...] = jnp.where(slot >= 10, beyond, merged)
+    else:
+        beyond = pltpu.roll(Z[...], 112, 1)
+        if at_end is not None:
+            wall = jnp.where(group == 0, profile[0], jnp.where(group == 3, profile[1], 0.0))
+            beyond = jnp.where(at_end, wall, beyond)
+        Z[...] = jnp.where(slot < 2, beyond, merged)
+    if at_end is not None:
+
+        @pl.when(at_end)
+        def _():
+            for e in range(2):
+                U[e, own] = given[0][NX - 1, own] if up else profile[0]
+                F[e, own] = given[3][NX - 1, own] if up else profile[1]
+            if up:
+                V[near, own] = given[1][NX - 1, own]
+                W[near, own] = given[2][NX - 1, own]
+
+    fill_shifts(buffers, Z[...], range(2), (10, 11) if up else (0, 1))
+    halo = [(buffers, 0), (buffers, 1)]
+    line = [(given, NX - 2), (given, NX - 1)] + halo if up else halo + [(given, 0), (given, 1)]
+    inside, outside = (line[:3], line[1:]) if up else (line[1:], line[:3])
 
     def block(i, carry):
         y = pl.multiple_of(i * 8, 8)
         rows = pl.ds(y, 8)
-        for x, end, planes in ((0, 0, line), (NX - 1, 1, line_high)):
-            inner, outer = (planes[1:], planes[:3]) if x == 0 else (planes[:3], planes[1:])
-            mid[0, x, rows], mid[1, x, rows], mid[2, x, rows], frac_new[x, rows] = cells(
-                *inner, Z, x + 2, y, (0, 1, 2)
+        mid[0, rows], mid[1, rows], mid[2, rows], frac[rows] = cells(*inside, Z, 9 if up else 2, y, (0, 1, 2))
+        (end_mid[rows],) = cells(*outside, Z, 10 if up else 1, y, (0,))
+        return carry
+
+    lax.fori_loop(0, 16, block, 0, unroll=2)
+    if up:
+        source[0] = source_plane(6, given_mid[0, 5], mid[0], given_mid[1, 6], given_mid[2, 6], moments, pack)
+        source[1] = source_plane(7, given_mid[0, 6], end_mid[...], mid[1], mid[2], moments, pack)
+    else:
+        source[0] = source_plane(0, end_mid[...], given_mid[0, 1], mid[1], mid[2], moments, pack)
+        source[1] = source_plane(1, mid[0], given_mid[0, 2], given_mid[1, 1], given_mid[2, 1], moments, pack)
+
+
+def paired_body(flags, message, sides, profile, moments, *refs):
+    given, given_mid, given_pack = refs[:7], refs[7], refs[8]
+    mid, frac, source, pack = refs[9:13]
+    pack[...] = given_pack[...]
+    for up in (True, False):
+
+        @pl.when(flags[2] == int(up))
+        def _(up=up):
+            side_part(
+                up, None, message, sides, profile, moments, given, given_mid, mid.at[:, 0], frac, source, pack, refs[13:]
             )
-            (end_mid[end, rows],) = cells(*outer, Z, 1 + 9 * end, y, (0,))
-        return carry
-
-    lax.fori_loop(0, 16, block, 0)
+
+
+def other_body(flags, message, sides, profile, moments, *refs):
+    given, (given_mid, given_frac, given_source) = refs[:7], refs[7:10]
+    paired_frac, paired_source, given_pack = refs[10:13]
+    mid, frac_new, source, pack = refs[13:17]
+    scratch, keep_sem = refs[17:-1], refs[-1]
+    even = flags[2] == 1
+    middle = pl.ds(1, NX - 2)
+    kept = [
+        (given_frac.at[middle], frac_new.at[middle]),
+        (paired_frac, frac_new.at[jnp.where(even, NX - 1, 0)]),
+        (given_source.at[pl.ds(2, NX - 4)], source.at[pl.ds(2, NX - 4)]),
+        (paired_source, source.at[pl.ds(jnp.where(even, NX - 2, 0), 2)]),
+    ]
+    kept = start_copies(kept, keep_sem)
     pack[...] = given_pack[...]
-    source_plane(0, end_mid[0], given_mid[0, 1], mid, 0, moments, source, pack)
-    source_plane(1, mid[0, 0], given_mid[0, 2], given_mid, 1, moments, source, pack)
-    source_plane(6, given_mid[0, 5], mid[0, 7], given_mid, 6, moments, source, pack)
-    source_plane(7, given_mid[0, 6], end_mid[1], mid, 7, moments, source, pack)
+    for up in (True, False):
+
+        @pl.when(flags[2] == 1 - int(up))
+        def _(up=up):
+            side_part(
+                up,
+                flags[1 if up else 0] == 1,
+                message, sides, profile, moments, given, given_mid,
+                mid.at[:, 0],
+                frac_new.at[NX - 1 if up else 0],
+                source.at[pl.ds(NX - 2 if up else 0, 2)],
+                pack,
+                scratch,
+            )
+
     for copy in kept:
         copy.wait()
 
@@ -403,14 +432,13 @@
 HALO = POWERS
 
 
-def ghosts(out, m, plane):
-    out[m, plane, pl.ds(TOP - 1, 1)] = out[m, plane, pl.ds(TOP, 1)]
-    out[m, plane, pl.ds(TOP + NY, 1)] = out[m, plane, pl.ds(TOP + NY - 1, 1)]
-
-def own_plane(x, carry):
-    moments = pltpu.roll(far[...], (128 - 16 * x) % 128, 1)
-    terms(x + halo, source[x], moments, 0)
-    return carry
+def put(out, m, plane, y, value):
+    size = value.shape[0]
+    out[m, plane, pl.ds(TOP + y, size)] = value
+    if y == 0:
+        out[m, plane, pl.ds(TOP - 1, 1)] = value[:1]
+    if y + size == NY:
+        out[m, plane, pl.ds(TOP + NY, 1)] = value[size - 1 :]
 
 
 def terms(table, U, E, lhs, row, plane, values, moments, start):
@@ -434,8 +462,7 @@
     lhs[:, 384:512] = side.astype(BF16)
     result = jnp.dot(lhs[...], table[:, start * 128 :], preferred_element_type=F32)
     for m in range(start, POWERS):
-        U[m, row, pl.ds(TOP, NY)] = result[:, (m - start) * 128 : (m - start + 1) * 128]
-        ghosts(U, m, row)
+        put(U, m, row, 0, result[:, (m - start) * 128 : (m - start + 1) * 128])
     ends = result[:, (POWERS - start) * 128 :]
     group, offset = plane // 8, 16 * (plane % 8)
     E[group] += pltpu.roll(ends, offset, 1)
@@ -452,48 +479,76 @@
     lax.fori_loop(0, NX, own_plane, 0)
 
 
+def side_terms_body(flags, paired, given_E, table, U, E, lhs):
+    even = flags[2] == 1
+    E[...] = given_E[...]
+    for k in range(1, HALO + 1):
+        x = jnp.where(even, k - 1, NX - k)
+        moments = pltpu.roll(paired[NX], (128 - 16 * x) % 128, 1)
+        plane = jnp.where(even, HALO + NX - 1 + k, HALO - k)
+        place = jnp.where(even, k - 1, HALO - k)
+        terms(table, U, E, lhs, place, plane, paired[x], moments, k - 1)
+
+
 def solve_body(more, *refs):
-    (flags, mid, frac, now, paired, other, table, given_U, given_E) = refs[:9]
-    vel, pressure = refs[9:11]
-    U, E, lhs, sem = refs[-4:]
+    (flags, mid, mid_paired, mid_other, frac, now, other, table, given_U, given_side, given_E) = refs[:11]
+    vel, pressure = refs[11:13]
+    U, E, lhs, sem, side_sem = refs[-5:]
     if more:
-        faces_paired, faces_other, packed, guess = refs[11:15]
+        faces_paired, faces_other, packed, guess = refs[13:17]
     first = flags[0] == 1
     last = flags[1] == 1
     halo = HALO
-    fetch = pltpu.make_async_copy(given_U, U.at[:, pl.ds(halo, NX)], sem)
+    top = POWERS - 1
+    fetch = pltpu.make_async_copy(given_U.at[top], U.at[top, pl.ds(halo, NX)], sem)
     fetch.start()
+    even = flags[2] == 1
+    fetch_side = pltpu.make_async_copy(
+        given_side.at[top], U.at[top, pl.ds(jnp.where(even, halo + NX, 0), halo)], side_sem
+    )
+    fetch_side.start()
     E[...] = given_E[...]
 
     def inside(plane):
         kept = ((plane >= halo) | jnp.logical_not(first)) & ((plane < halo + NX) | jnp.logical_not(last))
         return jnp.where(kept, 1.0, 0.0).astype(F32)
 
-    even = flags[2] == 1
     for k in range(1, halo + 1):
-        for message, upper in ((paired, even), (other, jnp.logical_not(even))):
-            x = jnp.where(upper, k - 1, NX - k)
-            moments = pltpu.roll(message[NX], (128 - 16 * x) % 128, 1)
-            plane = jnp.where(upper, halo + NX - 1 + k, halo - k)
-            terms(table, U, E, lhs, plane, plane, message[x], moments, k - 1)
-
+        x = jnp.where(even, NX - k, k - 1)
+        moments = pltpu.roll(other[NX], (128 - 16 * x) % 128, 1)
+        plane = jnp.where(even, halo - k, halo + NX - 1 + k)
+        terms(table, U, E, lhs, plane, plane, other[x], moments, k - 1)
+
+    fetch_side.wait()
     fetch.wait()
     for m in range(POWERS - 2, -1, -1):
         reach = m + 1
 
-        def sweep(plane, carry, m=m):
-            keep = inside(plane)
+        def beside(plane, y, m=m):
+            here = pl.ds(TOP + y, 32)
+            return (U[m + 1, plane - 1, here] + U[m + 1, plane + 1, here]) + (
+                U[m + 1, plane, pl.ds(TOP + y - 1, 32)] + U[m + 1, plane, pl.ds(TOP + y + 1, 32)]
+            )
+
+        def sweep(i, carry, m=m):
+            low, high = halo - 1 - i, halo + NX + i
+            plane = jnp.where(even, high, low)
+            place = jnp.where(even, i, halo - 1 - i)
+            far_plane = jnp.where(even, low, high)
+            keep = inside(far_plane)
             for y in range(0, NY, 32):
                 here = pl.ds(TOP + y, 32)
-                beside = (U[m + 1, plane - 1, here] + U[m + 1, plane + 1, here]) + (
-                    U[m + 1, plane, pl.ds(TOP + y - 1, 32)]
-                    + U[m + 1, plane, pl.ds(TOP + y + 1, 32)]
-                )
-                U[m, plane, here] += keep * beside
-            ghosts(U, m, plane)
+                put(U, m, plane, y, given_side[m, place, here] + beside(plane, y))
+                put(U, m, far_plane, y, U[m, far_plane, here] + keep * beside(far_plane, y))
             return carry
 
-        lax.fori_loop(halo - reach, halo + NX + reach, sweep, 0)
+        def sweep_own(x, carry, m=m):
+            for y in range(0, NY, 32):
+                put(U, m, x + halo, y, given_U[m, x, pl.ds(TOP + y, 32)] + beside(x + halo, y))
+            return carry
+
+        lax.fori_loop(0, reach, sweep, 0)
+        lax.fori_loop(0, NX, sweep_own, 0, unroll=2)
 
     lane = lanes(NY)
     row = lax.broadcasted_iota(jnp.int32, (NY, 128), 0)
@@ -519,28 +574,33 @@
     for g in range(3):
         E[g] = ends[g]
 
-    def correct(x, carry):
+    def correct(x, mid, mx):
         plane = x + halo
         lane = lanes(NY)
         turned = pltpu.roll(E[plane // 8], (128 - 16 * (plane % 8) - 1) % 128, 1)
         centre = U[0, plane, pl.ds(TOP, NY)]
         ahead = jnp.where(lane == NZ - 1, turned, pltpu.roll(centre, NZ - 1, 1))
         behind = jnp.where(lane == 0, turned, pltpu.roll(centre, 1, 1))
-        vel[2, x] = mid[2, x] + 0.1 * (ahead - behind)
+        vel[2, x] = mid[2, mx] + 0.1 * (ahead - behind)
         for y in range(0, NY, 32):
             here = pl.ds(TOP + y, 32)
             rows = pl.ds(y, 32)
             p = -U[0, plane, here]
             pressure[x, rows] = p
-            vel[0, x, rows] = mid[0, x, rows] + 0.1 * (U[0, plane + 1, here] - U[0, plane - 1, here])
-            vel[1, x, rows] = mid[1, x, rows] + 0.1 * (
+            vel[0, x, rows] = mid[0, mx, rows] + 0.1 * (U[0, plane + 1, here] - U[0, plane - 1, here])
+            vel[1, x, rows] = mid[1, mx, rows] + 0.1 * (
                 U[0, plane, pl.ds(TOP + y + 1, 32)] - U[0, plane, pl.ds(TOP + y - 1, 32)]
             )
             if more:
                 guess[x, rows] = 2.0 * p - now[x, rows]
+
+    def correct_inner(x, carry):
+        correct(x, mid, x)
         return carry
 
-    lax.fori_loop(0, NX, correct, 0)
+    lax.fori_loop(1, NX - 1, correct_inner, 0, unroll=2)
+    correct(jnp.where(even, NX - 1, 0), mid_paired, 0)
+    correct(jnp.where(even, 0, NX - 1), mid_other, 0)
     if more:
         emit_faces(flags, vel, frac, guess, faces_paired, faces_other, packed)
 
@@ -551,6 +611,7 @@
 
 IN_VMEM = pl.BlockSpec(memory_space=pltpu.VMEM)
 IN_SMEM = pl.BlockSpec(memory_space=pltpu.SMEM)
+IN_HBM = pl.BlockSpec(memory_space=pltpu.HBM)
 ANYWHERE = pl.BlockSpec(memory_space=pl.ANY)
 BLOCK = (NX, NY, NZ)
 MESSAGE = (NX + 1, NY, NZ)
@@ -560,9 +621,12 @@
     return pl.pallas_call(
         pack_body,
         out_shape=(shape(*MESSAGE), shape(*MESSAGE), shape(NY, 128), shape(*BLOCK)),
-        in_specs=[IN_SMEM] + [IN_VMEM] * 4,
+        in_specs=[IN_SMEM] + [IN_HBM] * 4,
         out_specs=(IN_VMEM,) * 4,
-        compiler_params=pltpu.CompilerParams(vmem_limit_bytes=10 * MIB),
+        scratch_shapes=[pltpu.VMEM((3, *BLOCK), F32)]
+        + [pltpu.VMEM(BLOCK, F32)] * 3
+        + [pltpu.SemaphoreType.DMA((6,))],
+        compiler_params=pltpu.CompilerParams(vmem_limit_bytes=60 * MIB),
         name="pack",
     )(flags, velocity, fraction, now, old)
 
@@ -589,23 +653,38 @@
     )(velocity, fraction, guess, sides, moments)
 
 
-def outer_call(flags, paired, other, sides, profile, moments, inner):
+SIDE_SCRATCH = [pltpu.VMEM((2, ROWS, NZ), F32)] * 7 + [
+    pltpu.VMEM((NY, 128), F32),
+    pltpu.VMEM((NY, NZ), F32),
+    pltpu.SemaphoreType.DMA((6,)),
+]
+
+
+def paired_call(flags, message, sides, profile, moments, inner):
+    *buffers, mid, _, _, pack = inner
     return pl.pallas_call(
-        outer_body,
-        out_shape=PREDICTED[7:],
-        in_specs=[IN_SMEM] + [ANYWHERE] * 2 + [IN_VMEM] * 3 + [IN_VMEM] * 8 + [ANYWHERE] * 2 + [IN_VMEM],
+        paired_body,
+        out_shape=(shape(3, 1, NY, NZ), shape(NY, NZ), shape(2, NY, NZ), shape(NY, 128)),
+        in_specs=[IN_SMEM] + [ANYWHERE] + [IN_VMEM] * 12,
         out_specs=(IN_VMEM,) * 4,
-        scratch_shapes=[pltpu.VMEM((4, ROWS, NZ), F32)] * 7
-        + [
-            pltpu.VMEM((NY, 128), F32),
-            pltpu.VMEM((2, NY, 128), F32),
-            pltpu.VMEM((2, NY, NZ), F32),
-            pltpu.SemaphoreType.DMA((12,)),
-            pltpu.SemaphoreType.DMA((5,)),
-        ],
-        compiler_params=pltpu.CompilerParams(vmem_limit_bytes=16 * MIB),
-        name="outer",
-    )(flags, paired, other, sides, profile, moments, *inner)
+        scratch_shapes=SIDE_SCRATCH,
+        compiler_params=pltpu.CompilerParams(vmem_limit_bytes=12 * MIB),
+        cost_estimate=pl.CostEstimate(flops=6_000_000, bytes_accessed=6_000_000, transcendentals=30_000),
+        name="paired_side",
+    )(flags, message, sides, profile, moments, *buffers, mid, pack)
+
+
+def other_call(flags, message, sides, profile, moments, inner, frac, source, pack):
+    *buffers, mid, inner_frac, inner_source, _ = inner
+    return pl.pallas_call(
+        other_body,
+        out_shape=(shape(3, 1, NY, NZ), shape(*BLOCK), shape(*MESSAGE), shape(NY, 128)),
+        in_specs=[IN_SMEM] + [ANYWHERE] + [IN_VMEM] * 11 + [ANYWHERE] * 4 + [IN_VMEM],
+        out_specs=(IN_VMEM,) * 4,
+        scratch_shapes=SIDE_SCRATCH + [pltpu.SemaphoreType.DMA((4,))],
+        compiler_params=pltpu.CompilerParams(vmem_limit_bytes=12 * MIB),
+        name="other_side",
+    )(flags, message, sides, profile, moments, *buffers, mid, inner_frac, inner_source, frac, source, pack)
 
 
 def combine_call(packs, table, message):
@@ -650,24 +729,38 @@
     )(source, far, table)
 
 
-def solve_call(more, flags, mid, frac, now, paired, other, table, own):
+def side_terms_call(flags, paired, ends, table):
+    return pl.pallas_call(
+        side_terms_body,
+        out_shape=(shape(POWERS, HALO, ROWS, NZ), shape(3, NY, 128)),
+        in_specs=[IN_SMEM] + [IN_VMEM] * 3,
+        out_specs=(IN_VMEM,) * 2,
+        scratch_shapes=[pltpu.VMEM((NY, 512), BF16)],
+        compiler_params=pltpu.CompilerParams(vmem_limit_bytes=12 * MIB),
+        cost_estimate=pl.CostEstimate(flops=500_000_000, bytes_accessed=6_000_000, transcendentals=0),
+        name="side_terms",
+    )(flags, paired, ends, table)
+
+
+def solve_call(more, flags, mid, mid_paired, mid_other, frac, now, other, table, own, side, ends):
     outs = [shape(3, *BLOCK), shape(*BLOCK)]
     if more:
         outs += [shape(*MESSAGE), shape(*MESSAGE), shape(NY, 128), shape(*BLOCK)]
     return pl.pallas_call(
         functools.partial(solve_body, more),
         out_shape=tuple(outs),
-        in_specs=[IN_SMEM] + [IN_VMEM] * 6 + [ANYWHERE, IN_VMEM],
+        in_specs=[IN_SMEM] + [IN_VMEM] * 10,
         out_specs=(IN_VMEM,) * len(outs),
         scratch_shapes=[
             pltpu.VMEM((POWERS, NX + 2 * HALO, ROWS, NZ), F32),
             pltpu.VMEM((3, NY, 128), F32),
             pltpu.VMEM((NY, 512), BF16),
             pltpu.SemaphoreType.DMA,
+            pltpu.SemaphoreType.DMA,
         ],
         compiler_params=pltpu.CompilerParams(vmem_limit_bytes=20 * MIB),
         name="solve",
-    )(flags, mid, frac, now, paired, other, table, *own)
+    )(flags, mid, mid_paired, mid_other, frac, now, other, table, own, side, ends)
 
 
 def per_device(velocity, fraction, pressure_now, pressure_old, inflow):
@@ -698,12 +791,18 @@
         other = exchange(other, False)
         paired = exchange(paired, True)
         inner = inner_call(velocity, fraction, guess, sides, moments)
-        mid, fraction, source, pack = outer_call(flags, paired, other, sides, profile, moments, inner)
+        mid_paired, frac, source, pack = paired_call(flags, paired, sides, profile, moments, inner)
+        mid_other, fraction, source, pack = other_call(
+            flags, other, sides, profile, moments, inner, frac, source, pack
+        )
         source, far = combine_call([pack] + [around(pack, o) for o in (1, 2, 3)], combine, source)
         other = exchange(source, False)
         paired = exchange(source, True)
-        own = own_terms_call(source, far, table)
-        results = solve_call(more, flags, mid, fraction, now, paired, other, table, own)
+        own, ends = own_terms_call(source, far, table)
+        side, ends = side_terms_call(flags, paired, ends, table)
+        results = solve_call(
+            more, flags, inner[7], mid_paired, mid_other, fraction, now, other, table, own, side, ends
+        )
         velocity, pressure = results[:2]
         old, now = now, pressure
         if more:

time: 154 us -> 146 us (0.948)
  waiting for transfers between devices: 53.1 us -> 44.3 us
  local copies, waits for them, and re-layouts: 4.67 us -> 0.14 us
  Pallas kernels: 52.3 us -> 56.7 us
    ppermute x8, waiting for transfers between devices: 40.1 us -> 31 us  [exchange(): return lax.ppermute(block, 'stream', pairs if with_pair else others)]
    unnamed x26 -> x22, local copies, waits for them, and re-layouts: 4.58 us -> 0.05 us
    pallas_call x2 -> x6, Pallas kernels: 12.1 us -> 16.6 us  [the longest x2 7.53 us: other_call(): pl.pallas_call(other_body, out_shape=(shape(3, 1, NY, NZ), shape(*BLOCK),...]
    pallas_call x2, Pallas kernels: 19.7 us -> 15.9 us  [solve_call(): pl.pallas_call(functools.partial(solve_body, more), out_shape=tuple(outs)...]
    pallas_call x1, Pallas kernels: 1.38 us -> 4.51 us  [pack_call(): pl.pallas_call(pack_body, out_shape=(shape(*MESSAGE), shape(*MESSAGE), sh...]
  transfers between devices with their start and end apart: 18 -> 18, of which waited for: 13 -> 15; matrix products, arithmetic and copies ran while one was open for 0% -> 0% of each run, Pallas kernels for 11% -> 18%
where the time goes in v4:
time: 146 us
  Pallas kernels  56.7 us (39%)
  waiting for transfers between devices  44.3 us (30%)
  starting transfers between devices  42.7 us (29%)
    ppermute x8, starting transfers between devices, exchange(): return lax.ppermute(block, 'stream', pairs if with_pair else others)  33.1 us
    ppermute x8, waiting for transfers between devices, exchange(): return lax.ppermute(block, 'stream', pairs if with_pair else others)  31 us
    pallas_call x2, Pallas kernels, solve_call(): pl.pallas_call(functools.partial(solve_body, more), out_shape=tuple(outs)...  15.9 us
    ppermute x10, waiting for transfers between devices, around(): lax.ppermute(block, 'span', [((i + offset) % BLOCKS, i) for i in range(BL...  13.3 us
    pallas_call x2, Pallas kernels, inner_call(): pl.pallas_call(inner_body, out_shape=PREDICTED, in_specs=[ANYWHERE] * 3 +...  9.93 us
    ppermute x10, starting transfers between devices, around(): lax.ppermute(block, 'span', [((i + offset) % BLOCKS, i) for i in range(BL...  9.61 us
    pallas_call x2, Pallas kernels, own_terms_call(): pl.pallas_call(own_terms_body, out_shape=(shape(*OWN_TERMS), shape(3, NY,...  7.73 us
    pallas_call x2, Pallas kernels, other_call(): pl.pallas_call(other_body, out_shape=(shape(3, 1, NY, NZ), shape(*BLOCK),...  7.53 us
  transfers between devices with their start and end apart: 18, of which 15 were waited for; matrix products, arithmetic and copies ran while one was open for 0% of the time, Pallas kernels for 18%

profile of v4, /device:TPU:7, one launch (start us, length us, event | category | flops | bytes accessed | tf_op | source)
XLA Modules:
  0.0 145.6 jit_solution(16590795044016659393)
XLA Ops:
  1.3 4.5 %pack.1 = (f32[9,128,128]{2,1,0:T(8,128)}, f32[9,128,128]{2,1,0:T(8,128)}, f32[128,128]{1,0:T(8,128)}, f32[8,128,128]{2,1,0:T(8,128)}) custom-call(s32[3]{0:T(128)} %add_convert_fusion.flags.refs_0_, f32[3,8,128,128]{3,2,1,0:T(8,128)} %vel.1, f32[8,128,128]{2,1,0:T(8,128)} %frac.1, f32[8,128,128]{2,1,0:T(8,128)} %refs_5_.1, f32[8,128,128]{2,1,0:T(8,128)} %old_far.1), custom_call_target="tpu_custom_call" | custom-call | tf_op jit(solution)/shard_map/pack/pallas_call | solution.py:621
  7.7 2.9 %collective-permute-done.1.after = f32[128,128]{1,0:T(8,128)S(1)} collective-permute-done((f32[128,128]{1,0:T(8,128)}, f32[128,128]{1,0:T(8,128)S(1)}, u32[]{:S(2)}, u32[]{:S(2)}) %collective-permute-start.1) | collective-permute-done | bytes 65568 | tf_op jit(solution)/shard_map/ppermute | solution.py:777
  13.1 7.6 %collective-permute-start.3 = (f32[9,128,128]{2,1,0:T(8,128)}, f32[9,128,128]{2,1,0:T(8,128)S(1)}, u32[]{:S(2)}, u32[]{:S(2)}) collective-permute-start(f32[9,128,128]{2,1,0:T(8,128)} %get-tuple-element.88), channel_id=1, source_target_pairs={{4,8},{8,4},{12,16},{16,12},{20,24},{24,20},{28,32},{32,28},{36,40... | collective-permute-start | bytes 1769480 | tf_op jit(solution)/shard_map/ppermute | solution.py:774
  20.7 4.9 %inner.2 = (f32[8,144,128]{2,1,0:T(8,128)S(1)}, f32[8,144,128]{2,1,0:T(8,128)S(1)}, f32[8,144,128]{2,1,0:T(8,128)S(1)}, f32[8,144,128]{2,1,0:T(8,128)S(1)}, f32[...) custom-call(f32[3,8,128,128]{3,2,1,0:T(8,128)S(1)} %copy-done, ...), custom_call_target="tpu_custom_call" | custom-call | flops 20000000 | bytes 16000000 | tf_op jit(solution)/shard_map/inner/pallas_call | solution.py:644
  29.2 5.6 %collective-permute-done.3.message = f32[9,128,128]{2,1,0:T(8,128)S(1)} collective-permute-done((f32[9,128,128]{2,1,0:T(8,128)}, f32[9,128,128]{2,1,0:T(8,128)S(1)}, u32[]{:S(2)}, u32[]{:S(2)}) %collective-permute-start.3) | collective-permute-done | bytes 589856 | tf_op jit(solution)/shard_map/ppermute | solution.py:774
  34.8 3.4 %other_side.2 = (f32[3,1,128,128]{3,2,1,0:T(8,128)S(1)}, f32[8,128,128]{2,1,0:T(8,128)S(1)}, f32[9,128,128]{2,1,0:T(8,128)S(1)}, f32[128,128]{1,0:T(8,128)S(1)}) custom-call(s32[3]{0:T(128)S(1)} %copy-done.9, f32[9,128,128]{2,1,0:T(8,128)S(1)} %collective-permute-done.3.message, f32[128,128]{1,0:T(8,128)S(1)} %get-tuple-element.76.sides, ...), custom_call_target="tpu_custom_call" | custom-call | tf_op jit(solution)/shard_map/other_side/pallas_call | solution.py:679
  41.5 3.2 %collective-permute-done.5.c = f32[128,128]{1,0:T(8,128)S(1)} collective-permute-done((f32[128,128]{1,0:T(8,128)S(1)}, f32[128,128]{1,0:T(8,128)S(1)}, u32[]{:S(2)}, u32[]{:S(2)}) %collective-permute-start.5) | collective-permute-done | bytes 65568 | tf_op jit(solution)/shard_map/ppermute | solution.py:777
  45.7 7.9 %collective-permute-start.7 = (f32[9,128,128]{2,1,0:T(8,128)S(1)}, f32[9,128,128]{2,1,0:T(8,128)S(1)}, u32[]{:S(2)}, u32[]{:S(2)}) collective-permute-start(f32[9,128,128]{2,1,0:T(8,128)S(1)} %get-tuple-element.98.source), channel_id=1, source_target_pairs={{4,8},{8,4},{12,16},{16,12},{20,24},{24,20},{28,32},{32,28},{36,40... | collective-permute-start | bytes 1769480 | tf_op jit(solution)/shard_map/ppermute | solution.py:774
  53.6 3.9 %own_terms.2 = (f32[7,8,144,128]{3,2,1,0:T(8,128)S(1)}, f32[3,128,128]{2,1,0:T(8,128)S(1)}) custom-call(f32[9,128,128]{2,1,0:T(8,128)S(1)} %get-tuple-element.98.source, f32[128,128]{1,0:T(8,128)S(1)} %get-tuple-element.99.far, bf16[512,1024]{1,0:T(8,128)(2,1)S(1)} %copy-done.2), custom_call_target="tpu_custom_call" | custom-call | flops 1000000000 | bytes 12000000 | tf_op jit(solution)/shard_map/own_terms/pallas_call | solution.py:720
  57.5 3.3 %collective-permute-done.8.paired = f32[9,128,128]{2,1,0:T(8,128)S(1)} collective-permute-done((f32[9,128,128]{2,1,0:T(8,128)S(1)}, f32[9,128,128]{2,1,0:T(8,128)S(1)}, u32[]{:S(2)}, u32[]{:S(2)}) %collective-permute-start.8) | collective-permute-done | bytes 589856 | tf_op jit(solution)/shard_map/ppermute | solution.py:774
  62.5 5.9 %collective-permute-done.7.refs_6_ = f32[9,128,128]{2,1,0:T(8,128)S(1)} collective-permute-done((f32[9,128,128]{2,1,0:T(8,128)S(1)}, f32[9,128,128]{2,1,0:T(8,128)S(1)}, u32[]{:S(2)}, u32[]{:S(2)}) %collective-permute-start.7) | collective-permute-done | bytes 589856 | tf_op jit(solution)/shard_map/ppermute | solution.py:774
  68.4 8.1 %solve.2 = (f32[3,8,128,128]{3,2,1,0:T(8,128)S(1)}, f32[8,128,128]{2,1,0:T(8,128)}, f32[9,128,128]{2,1,0:T(8,128)S(1)}, f32[9,128,128]{2,1,0:T(8,128)S(1)}, f32[...) custom-call(s32[3]{0:T(128)S(1)} %copy-done.9, f32[3,8,128,128]{3,2,1,0:T(8,128)S(1)} %get-tuple-element.77.refs_7_.refs_1_, ...), custom_call_target="tpu_custom_call" | custom-call | tf_op jit(solution)/shard_map/solve/pallas_call | solution.py:749
  78.3 2.9 %collective-permute-done.10.after = f32[128,128]{1,0:T(8,128)S(1)} collective-permute-done((f32[128,128]{1,0:T(8,128)S(1)}, f32[128,128]{1,0:T(8,128)S(1)}, u32[]{:S(2)}, u32[]{:S(2)}) %collective-permute-start.10) | collective-permute-done | bytes 65568 | tf_op jit(solution)/shard_map/ppermute | solution.py:777
  81.6 7.7 %collective-permute-start.12 = (f32[9,128,128]{2,1,0:T(8,128)S(1)}, f32[9,128,128]{2,1,0:T(8,128)S(1)}, u32[]{:S(2)}, u32[]{:S(2)}) collective-permute-start(f32[9,128,128]{2,1,0:T(8,128)S(1)} %get-tuple-element.121), channel_id=1, source_target_pairs={{4,8},{8,4},{12,16},{16,12},{20,24},{24,20},{28,32},{32,28},{36,40... | collective-permute-start | bytes 1769480 | tf_op jit(solution)/shard_map/ppermute | solution.py:774
  89.3 5.0 %inner.3 = (f32[8,144,128]{2,1,0:T(8,128)S(1)}, f32[8,144,128]{2,1,0:T(8,128)S(1)}, f32[8,144,128]{2,1,0:T(8,128)S(1)}, f32[8,144,128]{2,1,0:T(8,128)S(1)}, f32[...) custom-call(f32[3,8,128,128]{3,2,1,0:T(8,128)S(1)} %get-tuple-elemen, ...), custom_call_target="tpu_custom_call" | custom-call | flops 20000000 | bytes 16000000 | tf_op jit(solution)/shard_map/inner/pallas_call | solution.py:644
  96.0 2.8 %paired_side.3 = (f32[3,1,128,128]{3,2,1,0:T(8,128)S(1)}, f32[128,128]{1,0:T(8,128)S(1)}, f32[2,128,128]{2,1,0:T(8,128)S(1)}, f32[128,128]{1,0:T(8,128)S(1)}) custom-call(s32[3]{0:T(128)S(1)} %copy-done.9, f32[9,128,128]{2,1,0:T(8,128)S(1)} %collective-permute-done.11.message, f32[128,128]{1,0:T(8,128)S(1)} %get-tuple-element.109.sides, ...), custom_call_target="tpu_custom_call" | custom-call | flops 6000000 | bytes 6000000 | tf_op jit(solution)/shard_map/paired_side/pallas_call | solution.py:665
  98.9 4.8 %collective-permute-done.12.message = f32[9,128,128]{2,1,0:T(8,128)S(1)} collective-permute-done((f32[9,128,128]{2,1,0:T(8,128)S(1)}, f32[9,128,128]{2,1,0:T(8,128)S(1)}, u32[]{:S(2)}, u32[]{:S(2)}) %collective-permute-start.12) | collective-permute-done | bytes 589856 | tf_op jit(solution)/shard_map/ppermute | solution.py:774
  103.7 4.2 %other_side.3 = (f32[3,1,128,128]{3,2,1,0:T(8,128)S(1)}, f32[8,128,128]{2,1,0:T(8,128)}, f32[9,128,128]{2,1,0:T(8,128)S(1)}, f32[128,128]{1,0:T(8,128)S(1)}) custom-call(s32[3]{0:T(128)S(1)} %copy-done.9, f32[9,128,128]{2,1,0:T(8,128)S(1)} %collective-permute-done.12.message, f32[128,128]{1,0:T(8,128)S(1)} %get-tuple-element.109.sides, ...), custom_call_target="tpu_custom_call" | custom-call | tf_op jit(solution)/shard_map/other_side/pallas_call | solution.py:679
  110.6 3.3 %collective-permute-done.14.c = f32[128,128]{1,0:T(8,128)S(1)} collective-permute-done((f32[128,128]{1,0:T(8,128)S(1)}, f32[128,128]{1,0:T(8,128)S(1)}, u32[]{:S(2)}, u32[]{:S(2)}) %collective-permute-start.14) | collective-permute-done | bytes 65568 | tf_op jit(solution)/shard_map/ppermute | solution.py:777
  114.9 8.0 %collective-permute-start.16 = (f32[9,128,128]{2,1,0:T(8,128)S(1)}, f32[9,128,128]{2,1,0:T(8,128)S(1)}, u32[]{:S(2)}, u32[]{:S(2)}) collective-permute-start(f32[9,128,128]{2,1,0:T(8,128)S(1)} %get-tuple-element.132.source), channel_id=1, source_target_pairs={{4,8},{8,4},{12,16},{16,12},{20,24},{24,20},{28,32},{32,28},{36,40... | collective-permute-start | bytes 1769480 | tf_op jit(solution)/shard_map/ppermute | solution.py:774
  122.8 3.9 %own_terms.3 = (f32[7,8,144,128]{3,2,1,0:T(8,128)S(1)}, f32[3,128,128]{2,1,0:T(8,128)S(1)}) custom-call(f32[9,128,128]{2,1,0:T(8,128)S(1)} %get-tuple-element.132.source, f32[128,128]{1,0:T(8,128)S(1)} %get-tuple-element.133.far, bf16[512,1024]{1,0:T(8,128)(2,1)S(1)} %copy-done.2), custom_call_target="tpu_custom_call" | custom-call | flops 1000000000 | bytes 12000000 | tf_op jit(solution)/shard_map/own_terms/pallas_call | solution.py:720
  126.7 3.2 %collective-permute-done.17.paired = f32[9,128,128]{2,1,0:T(8,128)S(1)} collective-permute-done((f32[9,128,128]{2,1,0:T(8,128)S(1)}, f32[9,128,128]{2,1,0:T(8,128)S(1)}, u32[]{:S(2)}, u32[]{:S(2)}) %collective-permute-start.17) | collective-permute-done | bytes 589856 | tf_op jit(solution)/shard_map/ppermute | solution.py:774
  131.7 5.9 %collective-permute-done.16.refs_6_ = f32[9,128,128]{2,1,0:T(8,128)S(1)} collective-permute-done((f32[9,128,128]{2,1,0:T(8,128)S(1)}, f32[9,128,128]{2,1,0:T(8,128)S(1)}, u32[]{:S(2)}, u32[]{:S(2)}) %collective-permute-start.16) | collective-permute-done | bytes 589856 | tf_op jit(solution)/shard_map/ppermute | solution.py:774
  137.6 7.9 %solve.3 = (f32[3,8,128,128]{3,2,1,0:T(8,128)}, f32[8,128,128]{2,1,0:T(8,128)}) custom-call(s32[3]{0:T(128)S(1)} %copy-done.9, f32[3,8,128,128]{3,2,1,0:T(8,128)S(1)} %get-tuple-element.110.refs_7_.refs_1_, f32[3,1,128,128]{3,2,1,0:T(8,128)S(1)} %get-tuple-element.120.refs_2_, f32[3,1,128,128]{3,2,1,0:T(8,128)S(1)} %get-tuple-element.127.refs_3_, ...), custom_call_target="tpu_custom_call" | custom-call | tf_op jit(solution)/shard_map/solve/pallas_call | solution.py:749
  (53 shorter events, 24.0 us)
Async XLA Ops:
  1.3 19.4 %copy-start = (f32[3,8,128,128]{3,2,1,0:T(8,128)S(1)}, f32[3,8,128,128]{3,2,1,0:T(8,128)}, u32[]{:S(2)}) copy-start(f32[3,8,128,128]{3,2,1,0:T(8,128)} %vel.1) | copy-start | bytes 4718596
  1.3 19.4 %copy-start.1 = (f32[2,128,128]{2,1,0:T(8,128)S(1)}, f32[2,128,128]{2,1,0:T(8,128)}, u32[]{:S(2)}) copy-start(f32[2,128,128]{2,1,0:T(8,128)} %constant.28.clone.moments) | copy-start | bytes 393220
  1.3 19.4 %copy-start.4 = (f32[8,128,128]{2,1,0:T(8,128)S(1)}, f32[8,128,128]{2,1,0:T(8,128)}, u32[]{:S(2)}) copy-start(f32[8,128,128]{2,1,0:T(8,128)} %frac.1) | copy-start | bytes 1572868
  5.8 4.7 %collective-permute-start.1 = (f32[128,128]{1,0:T(8,128)}, f32[128,128]{1,0:T(8,128)S(1)}, u32[]{:S(2)}, u32[]{:S(2)}) collective-permute-start(f32[128,128]{1,0:T(8,128)} %get-tuple-element.73), channel_id=1, source_target_pairs={{1,0},{2,1},{3,2},{0,3},{5,4},{6,5},{7,6},{4,7},{9,8},{10,9},{11,1... | collective-permute-start | bytes 196616 | tf_op jit(solution)/shard_map/ppermute | solution.py:777
  6.6 4.0 %collective-permute-start = (f32[128,128]{1,0:T(8,128)}, f32[128,128]{1,0:T(8,128)S(1)}, u32[]{:S(2)}, u32[]{:S(2)}) collective-permute-start(f32[128,128]{1,0:T(8,128)} %get-tuple-element.73), channel_id=1, source_target_pairs={{3,0},{0,1},{1,2},{2,3},{7,4},{4,5},{5,6},{6,7},{11,8},{8,9},{9,10... | collective-permute-start | bytes 196616 | tf_op jit(solution)/shard_map/ppermute | solution.py:777
  11.3 14.9 %copy-start.10 = (f32[2,128]{1,0:T(2,128)S(1)}, f32[2,128]{1,0:T(2,128)}, u32[]{:S(2)}) copy-start(f32[2,128]{1,0:T(2,128)} %param.12) | copy-start | bytes 3076
  11.3 15.0 %copy-start.9 = (s32[3]{0:T(128)S(1)}, s32[3]{0:T(128)}, u32[]{:S(2)}) copy-start(s32[3]{0:T(128)} %add_convert_fusion.flags.refs_0_) | copy-start | bytes 40
  11.3 14.9 %collective-permute-start.2 = (f32[9,128,128]{2,1,0:T(8,128)}, f32[9,128,128]{2,1,0:T(8,128)S(1)}, u32[]{:S(2)}, u32[]{:S(2)}) collective-permute-start(f32[9,128,128]{2,1,0:T(8,128)} %get-tuple-element.78), channel_id=1, source_target_pairs={{0,4},{4,0},{8,12},{12,8},{16,20},{20,16},{24,28},{28,24},{32,36},... | collective-permute-start | bytes 1769480 | tf_op jit(solution)/shard_map/ppermute | solution.py:774
  13.1 21.7 %collective-permute-start.3 = (f32[9,128,128]{2,1,0:T(8,128)}, f32[9,128,128]{2,1,0:T(8,128)S(1)}, u32[]{:S(2)}, u32[]{:S(2)}) collective-permute-start(f32[9,128,128]{2,1,0:T(8,128)} %get-tuple-element.88), channel_id=1, source_target_pairs={{4,8},{8,4},{12,16},{16,12},{20,24},{24,20},{28,32},{32,28},{36,40... | collective-permute-start | bytes 1769480 | tf_op jit(solution)/shard_map/ppermute | solution.py:774
  34.8 18.8 %copy-start.2 = (bf16[512,1024]{1,0:T(8,128)(2,1)S(1)}, bf16[512,1024]{1,0:T(8,128)(2,1)}, u32[]{:S(2)}) copy-start(bf16[512,1024]{1,0:T(8,128)(2,1)} %constant.30.clone.table.refs_7_) | copy-start | bytes 3145732
  38.1 3.4 %collective-permute-start.6 = (f32[128,128]{1,0:T(8,128)S(1)}, f32[128,128]{1,0:T(8,128)S(1)}, u32[]{:S(2)}, u32[]{:S(2)}) collective-permute-start(f32[128,128]{1,0:T(8,128)S(1)} %get-tuple-element.96.a), channel_id=1, source_target_pairs={{3,0},{0,1},{1,2},{2,3},{7,4},{4,5},{5,6},{6,7},{11,8},{8,9},{9,10... | collective-permute-start | bytes 196616 | tf_op jit(solution)/shard_map/ppermute | solution.py:777
  40.2 4.5 %collective-permute-start.5 = (f32[128,128]{1,0:T(8,128)S(1)}, f32[128,128]{1,0:T(8,128)S(1)}, u32[]{:S(2)}, u32[]{:S(2)}) collective-permute-start(f32[128,128]{1,0:T(8,128)S(1)} %get-tuple-element.96.a), channel_id=1, source_target_pairs={{2,0},{3,1},{0,2},{1,3},{6,4},{7,5},{4,6},{5,7},{10,8},{11,9},{8,1... | collective-permute-start | bytes 196616 | tf_op jit(solution)/shard_map/ppermute | solution.py:777
  41.4 3.8 %collective-permute-start.4 = (f32[128,128]{1,0:T(8,128)S(1)}, f32[128,128]{1,0:T(8,128)S(1)}, u32[]{:S(2)}, u32[]{:S(2)}) collective-permute-start(f32[128,128]{1,0:T(8,128)S(1)} %get-tuple-element.96.a), channel_id=1, source_target_pairs={{1,0},{2,1},{3,2},{0,3},{5,4},{6,5},{7,6},{4,7},{9,8},{10,9},{11,1... | collective-permute-start | bytes 196616 | tf_op jit(solution)/shard_map/ppermute | solution.py:777
  45.6 15.2 %collective-permute-start.8 = (f32[9,128,128]{2,1,0:T(8,128)S(1)}, f32[9,128,128]{2,1,0:T(8,128)S(1)}, u32[]{:S(2)}, u32[]{:S(2)}) collective-permute-start(f32[9,128,128]{2,1,0:T(8,128)S(1)} %get-tuple-element.98.source), channel_id=1, source_target_pairs={{0,4},{4,0},{8,12},{12,8},{16,20},{20,16},{24,28},{28,24},{32,36},... | collective-permute-start | bytes 1769480 | tf_op jit(solution)/shard_map/ppermute | solution.py:774
  45.7 22.7 %collective-permute-start.7 = (f32[9,128,128]{2,1,0:T(8,128)S(1)}, f32[9,128,128]{2,1,0:T(8,128)S(1)}, u32[]{:S(2)}, u32[]{:S(2)}) collective-permute-start(f32[9,128,128]{2,1,0:T(8,128)S(1)} %get-tuple-element.98.source), channel_id=1, source_target_pairs={{4,8},{8,4},{12,16},{16,12},{20,24},{24,20},{28,32},{32,28},{36,40... | collective-permute-start | bytes 1769480 | tf_op jit(solution)/shard_map/ppermute | solution.py:774
  76.5 4.7 %collective-permute-start.10 = (f32[128,128]{1,0:T(8,128)S(1)}, f32[128,128]{1,0:T(8,128)S(1)}, u32[]{:S(2)}, u32[]{:S(2)}) collective-permute-start(f32[128,128]{1,0:T(8,128)S(1)} %get-tuple-element.106), channel_id=1, source_target_pairs={{1,0},{2,1},{3,2},{0,3},{5,4},{6,5},{7,6},{4,7},{9,8},{10,9},{11,1... | collective-permute-start | bytes 196616 | tf_op jit(solution)/shard_map/ppermute | solution.py:777
  77.3 4.0 %collective-permute-start.9 = (f32[128,128]{1,0:T(8,128)S(1)}, f32[128,128]{1,0:T(8,128)S(1)}, u32[]{:S(2)}, u32[]{:S(2)}) collective-permute-start(f32[128,128]{1,0:T(8,128)S(1)} %get-tuple-element.106), channel_id=1, source_target_pairs={{3,0},{0,1},{1,2},{2,3},{7,4},{4,5},{5,6},{6,7},{11,8},{8,9},{9,10... | collective-permute-start | bytes 196616 | tf_op jit(solution)/shard_map/ppermute | solution.py:777
  81.5 14.5 %collective-permute-start.11 = (f32[9,128,128]{2,1,0:T(8,128)S(1)}, f32[9,128,128]{2,1,0:T(8,128)S(1)}, u32[]{:S(2)}, u32[]{:S(2)}) collective-permute-start(f32[9,128,128]{2,1,0:T(8,128)S(1)} %get-tuple-element.111), channel_id=1, source_target_pairs={{0,4},{4,0},{8,12},{12,8},{16,20},{20,16},{24,28},{28,24},{32,36},... | collective-permute-start | bytes 1769480 | tf_op jit(solution)/shard_map/ppermute | solution.py:774
  81.6 22.1 %collective-permute-start.12 = (f32[9,128,128]{2,1,0:T(8,128)S(1)}, f32[9,128,128]{2,1,0:T(8,128)S(1)}, u32[]{:S(2)}, u32[]{:S(2)}) collective-permute-start(f32[9,128,128]{2,1,0:T(8,128)S(1)} %get-tuple-element.121), channel_id=1, source_target_pairs={{4,8},{8,4},{12,16},{16,12},{20,24},{24,20},{28,32},{32,28},{36,40... | collective-permute-start | bytes 1769480 | tf_op jit(solution)/shard_map/ppermute | solution.py:774
  107.8 2.7 %collective-permute-start.15 = (f32[128,128]{1,0:T(8,128)S(1)}, f32[128,128]{1,0:T(8,128)S(1)}, u32[]{:S(2)}, u32[]{:S(2)}) collective-permute-start(f32[128,128]{1,0:T(8,128)S(1)} %get-tuple-element.130.a), channel_id=1, source_target_pairs={{3,0},{0,1},{1,2},{2,3},{7,4},{4,5},{5,6},{6,7},{11,8},{8,9},{9,10... | collective-permute-start | bytes 196616 | tf_op jit(solution)/shard_map/ppermute | solution.py:777
  108.5 5.4 %collective-permute-start.14 = (f32[128,128]{1,0:T(8,128)S(1)}, f32[128,128]{1,0:T(8,128)S(1)}, u32[]{:S(2)}, u32[]{:S(2)}) collective-permute-start(f32[128,128]{1,0:T(8,128)S(1)} %get-tuple-element.130.a), channel_id=1, source_target_pairs={{2,0},{3,1},{0,2},{1,3},{6,4},{7,5},{4,6},{5,7},{10,8},{11,9},{8,1... | collective-permute-start | bytes 196616 | tf_op jit(solution)/shard_map/ppermute | solution.py:777
  110.6 3.8 %collective-permute-start.13 = (f32[128,128]{1,0:T(8,128)S(1)}, f32[128,128]{1,0:T(8,128)S(1)}, u32[]{:S(2)}, u32[]{:S(2)}) collective-permute-start(f32[128,128]{1,0:T(8,128)S(1)} %get-tuple-element.130.a), channel_id=1, source_target_pairs={{1,0},{2,1},{3,2},{0,3},{5,4},{6,5},{7,6},{4,7},{9,8},{10,9},{11,1... | collective-permute-start | bytes 196616 | tf_op jit(solution)/shard_map/ppermute | solution.py:777
  114.8 15.2 %collective-permute-start.17 = (f32[9,128,128]{2,1,0:T(8,128)S(1)}, f32[9,128,128]{2,1,0:T(8,128)S(1)}, u32[]{:S(2)}, u32[]{:S(2)}) collective-permute-start(f32[9,128,128]{2,1,0:T(8,128)S(1)} %get-tuple-element.132.source), channel_id=1, source_target_pairs={{0,4},{4,0},{8,12},{12,8},{16,20},{20,16},{24,28},{28,24},{32,36},... | collective-permute-start | bytes 1769480 | tf_op jit(solution)/shard_map/ppermute | solution.py:774
  114.9 22.7 %collective-permute-start.16 = (f32[9,128,128]{2,1,0:T(8,128)S(1)}, f32[9,128,128]{2,1,0:T(8,128)S(1)}, u32[]{:S(2)}, u32[]{:S(2)}) collective-permute-start(f32[9,128,128]{2,1,0:T(8,128)S(1)} %get-tuple-element.132.source), channel_id=1, source_target_pairs={{4,8},{8,4},{12,16},{16,12},{20,24},{24,20},{28,32},{32,28},{36,40... | collective-permute-start | bytes 1769480 | tf_op jit(solution)/shard_map/ppermute | solution.py:774
  (5 other events, 57.9 us)

commit v5 on v4

--- a/solution.py
+++ b/solution.py
@@ -114,10 +114,12 @@
     return lax.broadcasted_iota(jnp.int32, (rows, 128), 1)
 
 
-def pack_columns(fields):
+def pack_columns(fields, ready=None):
     lane = lanes(NY)
     packed = jnp.zeros((NY, 128), F32)
-    for k in range(5):
+    for k in (4, 3, 0, 1, 2):
+        if ready is not None:
+            ready(k)
         for x in range(NX):
             pair = 12 * k + x + 2
             keep = (lane == 2 * pair + 1) | (lane == 2 * pair + 2)
@@ -127,14 +129,26 @@
 
 def pack_body(flags, vel_far, frac_far, now_far, old_far, paired, other, packed, guess, vel, frac, now, old, sem):
     pairs = [(now_far, now), (old_far, old), (frac_far, frac)] + [(vel_far.at[k], vel.at[k]) for k in range(3)]
-    for copy in start_copies(pairs, sem):
-        copy.wait()
-    for x in range(NX):
-        guess[x] = 2.0 * now[x] - old[x]
-    emit_faces(flags, vel, frac, guess, paired, other, packed)
-
-
-def emit_faces(flags, vel, frac, guess, paired, other, packed):
+    copies = start_copies(pairs, sem)
+
+    def ready(k):
+        if k == 4:
+            copies[0].wait()
+            copies[1].wait()
+            for x in range(NX):
+                guess[x] = 2.0 * now[x] - old[x]
+        else:
+            copies[2 if k == 3 else 3 + k].wait()
+
+    packed[...] = pack_columns(lambda k, x: fields_of(vel, frac, guess, k, x), ready)
+    emit_faces(flags, vel, frac, guess, paired, other)
+
+
+def fields_of(vel, frac, guess, k, x):
+    return vel[k, x] if k < 3 else (frac[x] if k == 3 else guess[x])
+
+
+def emit_faces(flags, vel, frac, guess, paired, other):
     even = flags[2] == 1
     for out, upper in ((paired, even), (other, jnp.logical_not(even))):
         two = jnp.where(upper, NX - 2, 0)
@@ -145,11 +159,6 @@
             out[6 + k] = guess[two + k]
         out[2] = vel[1, one]
         out[3] = vel[2, one]
-
-    def field(k, x):
-        return vel[k, x] if k < 3 else (frac[x] if k == 3 else guess[x])
-
-    packed[...] = pack_columns(field)
 
 
 def fill_shifts(buffers, ends, planes, slots):
@@ -441,7 +450,7 @@
         out[m, plane, pl.ds(TOP + NY, 1)] = value[size - 1 :]
 
 
-def terms(table, U, E, lhs, row, plane, values, moments, start):
+def terms(table, U, E, lhs, row, plane, values, moments, start, first_group=0):
     lane = lanes(NY)
     head = values.astype(BF16)
     tail = (values - head.astype(F32)).astype(BF16)
@@ -464,7 +473,7 @@
     for m in range(start, POWERS):
         put(U, m, row, 0, result[:, (m - start) * 128 : (m - start + 1) * 128])
     ends = result[:, (POWERS - start) * 128 :]
-    group, offset = plane // 8, 16 * (plane % 8)
+    group, offset = plane // 8 - first_group, 16 * (plane % 8)
     E[group] += pltpu.roll(ends, offset, 1)
 
 
@@ -490,106 +499,169 @@
         terms(table, U, E, lhs, place, plane, paired[x], moments, k - 1)
 
 
-def solve_body(more, *refs):
-    (flags, mid, mid_paired, mid_other, frac, now, other, table, given_U, given_side, given_E) = refs[:11]
-    vel, pressure = refs[11:13]
-    U, E, lhs, sem, side_sem = refs[-5:]
-    if more:
-        faces_paired, faces_other, packed, guess = refs[13:17]
+def domain(flags):
     first = flags[0] == 1
     last = flags[1] == 1
-    halo = HALO
-    top = POWERS - 1
-    fetch = pltpu.make_async_copy(given_U.at[top], U.at[top, pl.ds(halo, NX)], sem)
-    fetch.start()
-    even = flags[2] == 1
-    fetch_side = pltpu.make_async_copy(
-        given_side.at[top], U.at[top, pl.ds(jnp.where(even, halo + NX, 0), halo)], side_sem
+
+    def inside(plane):
+        kept = ((plane >= HALO) | jnp.logical_not(first)) & ((plane < HALO + NX) | jnp.logical_not(last))
+        return jnp.where(kept, 1.0, 0.0).astype(F32)
+
+    return inside
+
+
+def beside(U, m, plane, y):
+    here = pl.ds(TOP + y, 32)
+    return (U[m, plane - 1, here] + U[m, plane + 1, here]) + (
+        U[m, plane, pl.ds(TOP + y - 1, 32)] + U[m, plane, pl.ds(TOP + y + 1, 32)]
     )
-    fetch_side.start()
-    E[...] = given_E[...]
-
-    def inside(plane):
-        kept = ((plane >= halo) | jnp.logical_not(first)) & ((plane < halo + NX) | jnp.logical_not(last))
-        return jnp.where(kept, 1.0, 0.0).astype(F32)
-
-    for k in range(1, halo + 1):
-        x = jnp.where(even, NX - k, k - 1)
-        moments = pltpu.roll(other[NX], (128 - 16 * x) % 128, 1)
-        plane = jnp.where(even, halo - k, halo + NX - 1 + k)
-        terms(table, U, E, lhs, plane, plane, other[x], moments, k - 1)
-
-    fetch_side.wait()
-    fetch.wait()
-    for m in range(POWERS - 2, -1, -1):
-        reach = m + 1
-
-        def beside(plane, y, m=m):
-            here = pl.ds(TOP + y, 32)
-            return (U[m + 1, plane - 1, here] + U[m + 1, plane + 1, here]) + (
-                U[m + 1, plane, pl.ds(TOP + y - 1, 32)] + U[m + 1, plane, pl.ds(TOP + y + 1, 32)]
-            )
-
-        def sweep(i, carry, m=m):
-            low, high = halo - 1 - i, halo + NX + i
-            plane = jnp.where(even, high, low)
-            place = jnp.where(even, i, halo - 1 - i)
-            far_plane = jnp.where(even, low, high)
-            keep = inside(far_plane)
-            for y in range(0, NY, 32):
-                here = pl.ds(TOP + y, 32)
-                put(U, m, plane, y, given_side[m, place, here] + beside(plane, y))
-                put(U, m, far_plane, y, U[m, far_plane, here] + keep * beside(far_plane, y))
-            return carry
-
-        def sweep_own(x, carry, m=m):
-            for y in range(0, NY, 32):
-                put(U, m, x + halo, y, given_U[m, x, pl.ds(TOP + y, 32)] + beside(x + halo, y))
-            return carry
-
-        lax.fori_loop(0, reach, sweep, 0)
-        lax.fori_loop(0, NX, sweep_own, 0, unroll=2)
-
+
+
+def sweep_ends(start, first_plane, inside):
+    count = len(start)
     lane = lanes(NY)
     row = lax.broadcasted_iota(jnp.int32, (NY, 128), 0)
     used = lane % 16 < 14
-    keeps = []
-    for g in range(3):
-        plane = 8 * g + lane // 16
-        keeps.append(jnp.where(used, inside(plane), 0.0))
-    start = [E[g] for g in range(3)]
+    keeps = [jnp.where(used, inside(first_plane + 8 * g + lane // 16), 0.0) for g in range(count)]
     ends = start
     for m in range(POWERS - 1):
         before = [pltpu.roll(e, 14, 1) for e in ends]
         after = [pltpu.roll(e, 110, 1) for e in ends]
         same = [pltpu.roll(e, 126, 1) for e in ends]
         updated = []
-        for g in range(3):
-            behind = jnp.where(lane < 16, before[g - 1], before[g]) if g else before[0]
-            ahead = jnp.where(lane >= 112, after[g + 1], after[g]) if g < 2 else after[2]
+        for g in range(count):
+            behind = jnp.where(lane < 16, before[g - 1] if g else 0.0, before[g])
+            ahead = jnp.where(lane >= 112, after[g + 1] if g < count - 1 else 0.0, after[g])
             up = jnp.where(row == NY - 1, same[g], pltpu.roll(same[g], NY - 1, 0))
             down = jnp.where(row == 0, same[g], pltpu.roll(same[g], 1, 0))
             updated.append(start[g] + keeps[g] * ((behind + ahead) + (up + down)))
         ends = updated
-    for g in range(3):
-        E[g] = ends[g]
+    return ends
+
+
+def first_sweeps_body(flags, given_U, given_side, given_E, out, E, U, sem, side_sem):
+    inside = domain(flags)
+    even = flags[2] == 1
+    top = POWERS - 1
+    fetches = [
+        pltpu.make_async_copy(given_U.at[top], U.at[top, pl.ds(HALO, NX)], sem),
+        pltpu.make_async_copy(given_side.at[top], U.at[top, pl.ds(jnp.where(even, HALO + NX, 0), HALO)], side_sem),
+    ]
+    for fetch in fetches:
+        fetch.start()
+
+    def clear(i, carry):
+        U[top, jnp.where(even, i, HALO + NX + i)] = jnp.zeros((ROWS, NZ), F32)
+        return carry
+
+    lax.fori_loop(0, HALO, clear, 0)
+    for g, value in enumerate(sweep_ends([given_E[g] for g in range(3)], 0, inside)):
+        E[g] = value
+    for fetch in fetches:
+        fetch.wait()
+
+    for m in range(top - 1, -1, -1):
+
+        def sweep(i, carry, m=m):
+            low, high = HALO - 1 - i, HALO + NX + i
+            plane = jnp.where(even, high, low)
+            place = jnp.where(even, i, HALO - 1 - i)
+            far_plane = jnp.where(even, low, high)
+            keep = inside(far_plane)
+            for y in range(0, NY, 32):
+                here = pl.ds(TOP + y, 32)
+                put(U, m, plane, y, given_side[m, place, here] + beside(U, m + 1, plane, y))
+                put(U, m, far_plane, y, keep * beside(U, m + 1, far_plane, y))
+            return carry
+
+        def sweep_own(x, carry, m=m):
+            for y in range(0, NY, 32):
+                put(
+                    U, m, x + HALO, y,
+                    given_U[m, x, pl.ds(TOP + y, 32)] + beside(U, m + 1, x + HALO, y),
+                )
+            return carry
+
+        lax.fori_loop(0, m + 1, sweep, 0)
+        lax.fori_loop(0, NX, sweep_own, 0, unroll=2)
+
+    def emit(j, carry):
+        out[j] = U[0, HALO - 1 + j]
+        return carry
+
+    lax.fori_loop(0, NX + 2, emit, 0)
+
+
+def solve_body(more, *refs):
+    (flags, mid, mid_paired, mid_other, frac, now, other, table, given_sum, given_E) = refs[:10]
+    vel, pressure = refs[10:12]
+    if more:
+        faces_paired, faces_other, packed, guess = refs[12:16]
+    U, T, E, beyond, lhs = refs[-5:]
+    inside = domain(flags)
+    even = flags[2] == 1
+    top = POWERS - 1
+    first_group = jnp.where(even, 0, 1)
+
+    def halo_plane(k):
+        return jnp.where(even, HALO - k, HALO + NX - 1 + k)
+
+    def own_plane(depth):
+        return jnp.where(even, HALO + depth, HALO + NX - 1 - depth)
+
+    E[...] = jnp.zeros((2, NY, 128), F32)
+    for k in range(1, HALO + 1):
+        x = jnp.where(even, NX - k, k - 1)
+        moments = pltpu.roll(other[NX], (128 - 16 * x) % 128, 1)
+        plane = halo_plane(k)
+        terms(table, U, E, lhs, plane, plane, other[x], moments, k - 1, first_group)
+    for m in range(top, -1, -1):
+        for depth in (top - m, top + 1 - m):
+            U[m, own_plane(depth)] = jnp.zeros((ROWS, NZ), F32)
+    U[0, jnp.where(even, HALO + NX, HALO - 1)] = jnp.zeros((ROWS, NZ), F32)
+
+    for m in range(top - 1, -1, -1):
+
+        def sweep(i, carry, m=m):
+            plane = halo_plane(1 + i)
+            keep = inside(plane)
+            for y in range(0, NY, 32):
+                put(U, m, plane, y, U[m, plane, pl.ds(TOP + y, 32)] + keep * beside(U, m + 1, plane, y))
+            return carry
+
+        def sweep_own(depth, carry, m=m):
+            plane = own_plane(depth)
+            for y in range(0, NY, 32):
+                put(U, m, plane, y, beside(U, m + 1, plane, y))
+            return carry
+
+        lax.fori_loop(0, m + 1, sweep, 0)
+        lax.fori_loop(0, top - m, sweep_own, 0)
+
+    for j in range(NX + 2):
+        T[j] = given_sum[j] + U[0, HALO - 1 + j]
+    ends = sweep_ends([E[0], E[1]], 8 * first_group, inside)
+    beyond[...] = given_E[...]
+    beyond[first_group] += ends[0]
+    beyond[first_group + 1] += ends[1]
 
     def correct(x, mid, mx):
-        plane = x + halo
+        plane = x + 1
+        slot = x + HALO
         lane = lanes(NY)
-        turned = pltpu.roll(E[plane // 8], (128 - 16 * (plane % 8) - 1) % 128, 1)
-        centre = U[0, plane, pl.ds(TOP, NY)]
+        turned = pltpu.roll(beyond[slot // 8], (128 - 16 * (slot % 8) - 1) % 128, 1)
+        centre = T[plane, pl.ds(TOP, NY)]
         ahead = jnp.where(lane == NZ - 1, turned, pltpu.roll(centre, NZ - 1, 1))
         behind = jnp.where(lane == 0, turned, pltpu.roll(centre, 1, 1))
         vel[2, x] = mid[2, mx] + 0.1 * (ahead - behind)
         for y in range(0, NY, 32):
             here = pl.ds(TOP + y, 32)
             rows = pl.ds(y, 32)
-            p = -U[0, plane, here]
+            p = -T[plane, here]
             pressure[x, rows] = p
-            vel[0, x, rows] = mid[0, mx, rows] + 0.1 * (U[0, plane + 1, here] - U[0, plane - 1, here])
+            vel[0, x, rows] = mid[0, mx, rows] + 0.1 * (T[plane + 1, here] - T[plane - 1, here])
             vel[1, x, rows] = mid[1, mx, rows] + 0.1 * (
-                U[0, plane, pl.ds(TOP + y + 1, 32)] - U[0, plane, pl.ds(TOP + y - 1, 32)]
+                T[plane, pl.ds(TOP + y + 1, 32)] - T[plane, pl.ds(TOP + y - 1, 32)]
             )
             if more:
                 guess[x, rows] = 2.0 * p - now[x, rows]
@@ -602,7 +674,8 @@
     correct(jnp.where(even, NX - 1, 0), mid_paired, 0)
     correct(jnp.where(even, 0, NX - 1), mid_other, 0)
     if more:
-        emit_faces(flags, vel, frac, guess, faces_paired, faces_other, packed)
+        emit_faces(flags, vel, frac, guess, faces_paired, faces_other)
+        packed[...] = pack_columns(lambda k, x: fields_of(vel, frac, guess, k, x))
 
 
 def shape(*dims):
@@ -742,25 +815,42 @@
     )(flags, paired, ends, table)
 
 
-def solve_call(more, flags, mid, mid_paired, mid_other, frac, now, other, table, own, side, ends):
+SUM = (NX + 2, ROWS, NZ)
+TERMS_SCRATCH = pltpu.VMEM((POWERS, NX + 2 * HALO, ROWS, NZ), F32)
+
+
+def first_sweeps_call(flags, own, side, ends):
+    return pl.pallas_call(
+        first_sweeps_body,
+        out_shape=(shape(*SUM), shape(3, NY, 128)),
+        in_specs=[IN_SMEM] + [IN_VMEM] * 3,
+        out_specs=(IN_VMEM,) * 2,
+        scratch_shapes=[TERMS_SCRATCH, pltpu.SemaphoreType.DMA, pltpu.SemaphoreType.DMA],
+        compiler_params=pltpu.CompilerParams(vmem_limit_bytes=18 * MIB),
+        cost_estimate=pl.CostEstimate(flops=10_000_000, bytes_accessed=14_000_000, transcendentals=0),
+        name="first_sweeps",
+    )(flags, own, side, ends)
+
+
+def solve_call(more, flags, mid, mid_paired, mid_other, frac, now, other, table, part, ends):
     outs = [shape(3, *BLOCK), shape(*BLOCK)]
     if more:
         outs += [shape(*MESSAGE), shape(*MESSAGE), shape(NY, 128), shape(*BLOCK)]
     return pl.pallas_call(
         functools.partial(solve_body, more),
         out_shape=tuple(outs),
-        in_specs=[IN_SMEM] + [IN_VMEM] * 10,
+        in_specs=[IN_SMEM] + [IN_VMEM] * 9,
         out_specs=(IN_VMEM,) * len(outs),
         scratch_shapes=[
-            pltpu.VMEM((POWERS, NX + 2 * HALO, ROWS, NZ), F32),
+            TERMS_SCRATCH,
+            pltpu.VMEM(SUM, F32),
+            pltpu.VMEM((2, NY, 128), F32),
             pltpu.VMEM((3, NY, 128), F32),
             pltpu.VMEM((NY, 512), BF16),
-            pltpu.SemaphoreType.DMA,
-            pltpu.SemaphoreType.DMA,
         ],
         compiler_params=pltpu.CompilerParams(vmem_limit_bytes=20 * MIB),
         name="solve",
-    )(flags, mid, mid_paired, mid_other, frac, now, other, table, own, side, ends)
+    )(flags, mid, mid_paired, mid_other, frac, now, other, table, part, ends)
 
 
 def per_device(velocity, fraction, pressure_now, pressure_old, inflow):
@@ -800,8 +890,9 @@
         paired = exchange(source, True)
         own, ends = own_terms_call(source, far, table)
         side, ends = side_terms_call(flags, paired, ends, table)
+        part, ends = first_sweeps_call(flags, own, side, ends)
         results = solve_call(
-            more, flags, inner[7], mid_paired, mid_other, fraction, now, other, table, own, side, ends
+            more, flags, inner[7], mid_paired, mid_other, fraction, now, other, table, part, ends
         )
         velocity, pressure = results[:2]
         old, now = now, pressure

time: 146 us -> 142 us (0.973)
  waiting for transfers between devices: 44.3 us -> 35.2 us
  Pallas kernels: 56.7 us -> 62.2 us
    pallas_call x0 -> x2, Pallas kernels: none -> 9.41 us  [first_sweeps_call(): pl.pallas_call(first_sweeps_body, out_shape=(shape(*SUM), shape(3, NY, 12...]
    ppermute x8, waiting for transfers between devices: 31 us -> 21.9 us  [exchange(): return lax.ppermute(block, 'stream', pairs if with_pair else others)]
    pallas_call x2, Pallas kernels: 15.9 us -> 12.2 us  [solve_call(): pl.pallas_call(functools.partial(solve_body, more), out_shape=tuple(outs)...]
  transfers between devices with their start and end apart: 18 -> 18, of which waited for: 15 -> 15; matrix products, arithmetic and copies ran while one was open for 0% -> 0% of each run, Pallas kernels for 18% -> 26%
where the time goes in v5:
time: 142 us; the launch traced here: 141 us
  Pallas kernels  62.2 us (44%)
  starting transfers between devices  42.3 us (30%)
  waiting for transfers between devices  35.2 us (25%)
    ppermute x8, starting transfers between devices, exchange(): return lax.ppermute(block, 'stream', pairs if with_pair else others)  32.8 us
    ppermute x8, waiting for transfers between devices, exchange(): return lax.ppermute(block, 'stream', pairs if with_pair else others)  21.9 us
    ppermute x10, waiting for transfers between devices, around(): lax.ppermute(block, 'span', [((i + offset) % BLOCKS, i) for i in range(BL...  13.3 us
    pallas_call x2, Pallas kernels, solve_call(): pl.pallas_call(functools.partial(solve_body, more), out_shape=tuple(outs)...  12.2 us
    pallas_call x2, Pallas kernels, inner_call(): pl.pallas_call(inner_body, out_shape=PREDICTED, in_specs=[ANYWHERE] * 3 +...  9.92 us
    ppermute x10, starting transfers between devices, around(): lax.ppermute(block, 'span', [((i + offset) % BLOCKS, i) for i in range(BL...  9.48 us
    pallas_call x2, Pallas kernels, first_sweeps_call(): pl.pallas_call(first_sweeps_body, out_shape=(shape(*SUM), shape(3, NY, 12...  9.41 us
    pallas_call x2, Pallas kernels, own_terms_call(): pl.pallas_call(own_terms_body, out_shape=(shape(*OWN_TERMS), shape(3, NY,...  7.73 us
  transfers between devices with their start and end apart: 18, of which 15 were waited for; matrix products, arithmetic and copies ran while one was open for 0% of the time, Pallas kernels for 26%

profile of v5, /device:TPU:7, one launch (start us, length us, event | category | flops | bytes accessed | tf_op | source)
XLA Modules:
  0.0 141.4 jit_solution(10386131251908771671)
XLA Ops:
  1.3 4.3 %pack.1 = (f32[9,128,128]{2,1,0:T(8,128)}, f32[9,128,128]{2,1,0:T(8,128)}, f32[128,128]{1,0:T(8,128)}, f32[8,128,128]{2,1,0:T(8,128)}) custom-call(s32[3]{0:T(128)} %add_convert_fusion.flags.refs_0_, f32[3,8,128,128]{3,2,1,0:T(8,128)} %vel.1, f32[8,128,128]{2,1,0:T(8,128)} %frac.1, f32[8,128,128]{2,1,0:T(8,128)} %refs_5_.1, f32[8,128,128]{2,1,0:T(8,128)} %old_far.1), custom_call_target="tpu_custom_call" | custom-call | tf_op jit(solution)/shard_map/pack/pallas_call | solution.py:694
  7.4 2.9 %collective-permute-done.1.after = f32[128,128]{1,0:T(8,128)S(1)} collective-permute-done((f32[128,128]{1,0:T(8,128)}, f32[128,128]{1,0:T(8,128)S(1)}, u32[]{:S(2)}, u32[]{:S(2)}) %collective-permute-start.1) | collective-permute-done | bytes 65568 | tf_op jit(solution)/shard_map/ppermute | solution.py:867
  12.8 7.6 %collective-permute-start.3 = (f32[9,128,128]{2,1,0:T(8,128)}, f32[9,128,128]{2,1,0:T(8,128)S(1)}, u32[]{:S(2)}, u32[]{:S(2)}) collective-permute-start(f32[9,128,128]{2,1,0:T(8,128)} %get-tuple-element.92), channel_id=1, source_target_pairs={{4,8},{8,4},{12,16},{16,12},{20,24},{24,20},{28,32},{32,28},{36,40... | collective-permute-start | bytes 1769480 | tf_op jit(solution)/shard_map/ppermute | solution.py:864
  20.4 4.9 %inner.2 = (f32[8,144,128]{2,1,0:T(8,128)S(1)}, f32[8,144,128]{2,1,0:T(8,128)S(1)}, f32[8,144,128]{2,1,0:T(8,128)S(1)}, f32[8,144,128]{2,1,0:T(8,128)S(1)}, f32[...) custom-call(f32[3,8,128,128]{3,2,1,0:T(8,128)S(1)} %copy-done, ...), custom_call_target="tpu_custom_call" | custom-call | flops 20000000 | bytes 16000000 | tf_op jit(solution)/shard_map/inner/pallas_call | solution.py:717
  28.9 5.6 %collective-permute-done.3.message = f32[9,128,128]{2,1,0:T(8,128)S(1)} collective-permute-done((f32[9,128,128]{2,1,0:T(8,128)}, f32[9,128,128]{2,1,0:T(8,128)S(1)}, u32[]{:S(2)}, u32[]{:S(2)}) %collective-permute-start.3) | collective-permute-done | bytes 589856 | tf_op jit(solution)/shard_map/ppermute | solution.py:864
  34.5 3.4 %other_side.2 = (f32[3,1,128,128]{3,2,1,0:T(8,128)S(1)}, f32[8,128,128]{2,1,0:T(8,128)S(1)}, f32[9,128,128]{2,1,0:T(8,128)S(1)}, f32[128,128]{1,0:T(8,128)S(1)}) custom-call(s32[3]{0:T(128)S(1)} %copy-done.9, f32[9,128,128]{2,1,0:T(8,128)S(1)} %collective-permute-done.3.message, f32[128,128]{1,0:T(8,128)S(1)} %get-tuple-element.80.sides, ...), custom_call_target="tpu_custom_call" | custom-call | tf_op jit(solution)/shard_map/other_side/pallas_call | solution.py:752
  41.2 3.2 %collective-permute-done.5.c = f32[128,128]{1,0:T(8,128)S(1)} collective-permute-done((f32[128,128]{1,0:T(8,128)S(1)}, f32[128,128]{1,0:T(8,128)S(1)}, u32[]{:S(2)}, u32[]{:S(2)}) %collective-permute-start.5) | collective-permute-done | bytes 65568 | tf_op jit(solution)/shard_map/ppermute | solution.py:867
  45.5 7.8 %collective-permute-start.7 = (f32[9,128,128]{2,1,0:T(8,128)S(1)}, f32[9,128,128]{2,1,0:T(8,128)S(1)}, u32[]{:S(2)}, u32[]{:S(2)}) collective-permute-start(f32[9,128,128]{2,1,0:T(8,128)S(1)} %get-tuple-element.102.source), channel_id=1, source_target_pairs={{4,8},{8,4},{12,16},{16,12},{20,24},{24,20},{28,32},{32,28},{36,40... | collective-permute-start | bytes 1769480 | tf_op jit(solution)/shard_map/ppermute | solution.py:864
  53.3 3.9 %own_terms.2 = (f32[7,8,144,128]{3,2,1,0:T(8,128)S(1)}, f32[3,128,128]{2,1,0:T(8,128)S(1)}) custom-call(f32[9,128,128]{2,1,0:T(8,128)S(1)} %get-tuple-element.102.source, f32[128,128]{1,0:T(8,128)S(1)} %get-tuple-element.103.far, bf16[512,1024]{1,0:T(8,128)(2,1)S(1)} %copy-done.2), custom_call_target="tpu_custom_call" | custom-call | flops 1000000000 | bytes 12000000 | tf_op jit(solution)/shard_map/own_terms/pallas_call | solution.py:793
  57.2 3.3 %collective-permute-done.8.paired = f32[9,128,128]{2,1,0:T(8,128)S(1)} collective-permute-done((f32[9,128,128]{2,1,0:T(8,128)S(1)}, f32[9,128,128]{2,1,0:T(8,128)S(1)}, u32[]{:S(2)}, u32[]{:S(2)}) %collective-permute-start.8) | collective-permute-done | bytes 589856 | tf_op jit(solution)/shard_map/ppermute | solution.py:864
  62.3 4.7 %first_sweeps.2 = (f32[10,144,128]{2,1,0:T(8,128)S(1)}, f32[3,128,128]{2,1,0:T(8,128)S(1)}) custom-call(s32[3]{0:T(128)S(1)} %copy-done.9, f32[7,8,144,128]{3,2,1,0:T(8,128)S(1)} %get-tuple-element.104.given_U, f32[7,7,144,128]{3,2,1,0:T(8,128)S(1)} %get-tuple-element.106.given_side, f32[3,128,128]{2,1,0:T(8,128)S(1)} %get-tuple-element.107.given_E), custom_call_target="tpu_custom_call" | custom-call | flops 10000000 | bytes 14000000 | tf_op jit(solution)/shard_map/first_sweeps/pallas_call | solution.py:823
  68.2 6.2 %solve.2 = (f32[3,8,128,128]{3,2,1,0:T(8,128)S(1)}, f32[8,128,128]{2,1,0:T(8,128)}, f32[9,128,128]{2,1,0:T(8,128)S(1)}, f32[9,128,128]{2,1,0:T(8,128)S(1)}, f32[...) custom-call(s32[3]{0:T(128)S(1)} %copy-done.9, f32[3,8,128,128]{3,2,1,0:T(8,128)S(1)} %get-tuple-element.81.refs_7_.refs_1_, ...), custom_call_target="tpu_custom_call" | custom-call | tf_op jit(solution)/shard_map/solve/pallas_call | solution.py:839
  76.1 2.9 %collective-permute-done.10.after = f32[128,128]{1,0:T(8,128)S(1)} collective-permute-done((f32[128,128]{1,0:T(8,128)S(1)}, f32[128,128]{1,0:T(8,128)S(1)}, u32[]{:S(2)}, u32[]{:S(2)}) %collective-permute-start.10) | collective-permute-done | bytes 65568 | tf_op jit(solution)/shard_map/ppermute | solution.py:867
  79.4 7.7 %collective-permute-start.12 = (f32[9,128,128]{2,1,0:T(8,128)S(1)}, f32[9,128,128]{2,1,0:T(8,128)S(1)}, u32[]{:S(2)}, u32[]{:S(2)}) collective-permute-start(f32[9,128,128]{2,1,0:T(8,128)S(1)} %get-tuple-element.127), channel_id=1, source_target_pairs={{4,8},{8,4},{12,16},{16,12},{20,24},{24,20},{28,32},{32,28},{36,40... | collective-permute-start | bytes 1769480 | tf_op jit(solution)/shard_map/ppermute | solution.py:864
  87.1 5.0 %inner.3 = (f32[8,144,128]{2,1,0:T(8,128)S(1)}, f32[8,144,128]{2,1,0:T(8,128)S(1)}, f32[8,144,128]{2,1,0:T(8,128)S(1)}, f32[8,144,128]{2,1,0:T(8,128)S(1)}, f32[...) custom-call(f32[3,8,128,128]{3,2,1,0:T(8,128)S(1)} %get-tuple-elemen, ...), custom_call_target="tpu_custom_call" | custom-call | flops 20000000 | bytes 16000000 | tf_op jit(solution)/shard_map/inner/pallas_call | solution.py:717
  93.9 2.8 %paired_side.3 = (f32[3,1,128,128]{3,2,1,0:T(8,128)S(1)}, f32[128,128]{1,0:T(8,128)S(1)}, f32[2,128,128]{2,1,0:T(8,128)S(1)}, f32[128,128]{1,0:T(8,128)S(1)}) custom-call(s32[3]{0:T(128)S(1)} %copy-done.9, f32[9,128,128]{2,1,0:T(8,128)S(1)} %collective-permute-done.11.message, f32[128,128]{1,0:T(8,128)S(1)} %get-tuple-element.115.sides, ...), custom_call_target="tpu_custom_call" | custom-call | flops 6000000 | bytes 6000000 | tf_op jit(solution)/shard_map/paired_side/pallas_call | solution.py:738
  96.8 4.8 %collective-permute-done.12.message = f32[9,128,128]{2,1,0:T(8,128)S(1)} collective-permute-done((f32[9,128,128]{2,1,0:T(8,128)S(1)}, f32[9,128,128]{2,1,0:T(8,128)S(1)}, u32[]{:S(2)}, u32[]{:S(2)}) %collective-permute-start.12) | collective-permute-done | bytes 589856 | tf_op jit(solution)/shard_map/ppermute | solution.py:864
  101.5 4.2 %other_side.3 = (f32[3,1,128,128]{3,2,1,0:T(8,128)S(1)}, f32[8,128,128]{2,1,0:T(8,128)}, f32[9,128,128]{2,1,0:T(8,128)S(1)}, f32[128,128]{1,0:T(8,128)S(1)}) custom-call(s32[3]{0:T(128)S(1)} %copy-done.9, f32[9,128,128]{2,1,0:T(8,128)S(1)} %collective-permute-done.12.message, f32[128,128]{1,0:T(8,128)S(1)} %get-tuple-element.115.sides, ...), custom_call_target="tpu_custom_call" | custom-call | tf_op jit(solution)/shard_map/other_side/pallas_call | solution.py:752
  108.4 3.3 %collective-permute-done.14.c = f32[128,128]{1,0:T(8,128)S(1)} collective-permute-done((f32[128,128]{1,0:T(8,128)S(1)}, f32[128,128]{1,0:T(8,128)S(1)}, u32[]{:S(2)}, u32[]{:S(2)}) %collective-permute-start.14) | collective-permute-done | bytes 65568 | tf_op jit(solution)/shard_map/ppermute | solution.py:867
  112.7 7.7 %collective-permute-start.16 = (f32[9,128,128]{2,1,0:T(8,128)S(1)}, f32[9,128,128]{2,1,0:T(8,128)S(1)}, u32[]{:S(2)}, u32[]{:S(2)}) collective-permute-start(f32[9,128,128]{2,1,0:T(8,128)S(1)} %get-tuple-element.138.source), channel_id=1, source_target_pairs={{4,8},{8,4},{12,16},{16,12},{20,24},{24,20},{28,32},{32,28},{36,40... | collective-permute-start | bytes 1769480 | tf_op jit(solution)/shard_map/ppermute | solution.py:864
  120.4 3.9 %own_terms.3 = (f32[7,8,144,128]{3,2,1,0:T(8,128)S(1)}, f32[3,128,128]{2,1,0:T(8,128)S(1)}) custom-call(f32[9,128,128]{2,1,0:T(8,128)S(1)} %get-tuple-element.138.source, f32[128,128]{1,0:T(8,128)S(1)} %get-tuple-element.139.far, bf16[512,1024]{1,0:T(8,128)(2,1)S(1)} %copy-done.2), custom_call_target="tpu_custom_call" | custom-call | flops 1000000000 | bytes 12000000 | tf_op jit(solution)/shard_map/own_terms/pallas_call | solution.py:793
  124.3 3.5 %collective-permute-done.17.paired = f32[9,128,128]{2,1,0:T(8,128)S(1)} collective-permute-done((f32[9,128,128]{2,1,0:T(8,128)S(1)}, f32[9,128,128]{2,1,0:T(8,128)S(1)}, u32[]{:S(2)}, u32[]{:S(2)}) %collective-permute-start.17) | collective-permute-done | bytes 589856 | tf_op jit(solution)/shard_map/ppermute | solution.py:864
  129.5 4.7 %first_sweeps.3 = (f32[10,144,128]{2,1,0:T(8,128)S(1)}, f32[3,128,128]{2,1,0:T(8,128)S(1)}) custom-call(s32[3]{0:T(128)S(1)} %copy-done.9, f32[7,8,144,128]{3,2,1,0:T(8,128)S(1)} %get-tuple-element.140.given_U, f32[7,7,144,128]{3,2,1,0:T(8,128)S(1)} %get-tuple-element.142.given_side, f32[3,128,128]{2,1,0:T(8,128)S(1)} %get-tuple-element.143.given_E), custom_call_target="tpu_custom_call" | custom-call | flops 10000000 | bytes 14000000 | tf_op jit(solution)/shard_map/first_sweeps/pallas_call | solution.py:823
  135.4 6.0 %solve.3 = (f32[3,8,128,128]{3,2,1,0:T(8,128)}, f32[8,128,128]{2,1,0:T(8,128)}) custom-call(s32[3]{0:T(128)S(1)} %copy-done.9, f32[3,8,128,128]{3,2,1,0:T(8,128)S(1)} %get-tuple-element.116.refs_7_.refs_1_, f32[3,1,128,128]{3,2,1,0:T(8,128)S(1)} %get-tuple-element.126.refs_2_, f32[3,1,128,128]{3,2,1,0:T(8,128)S(1)} %get-tuple-element.133.refs_3_, ...), custom_call_target="tpu_custom_call" | custom-call | tf_op jit(solution)/shard_map/solve/pallas_call | solution.py:839
  (55 shorter events, 26.3 us)
Async XLA Ops:
  1.3 19.2 %copy-start = (f32[3,8,128,128]{3,2,1,0:T(8,128)S(1)}, f32[3,8,128,128]{3,2,1,0:T(8,128)}, u32[]{:S(2)}) copy-start(f32[3,8,128,128]{3,2,1,0:T(8,128)} %vel.1) | copy-start | bytes 4718596
  1.3 19.2 %copy-start.1 = (f32[2,128,128]{2,1,0:T(8,128)S(1)}, f32[2,128,128]{2,1,0:T(8,128)}, u32[]{:S(2)}) copy-start(f32[2,128,128]{2,1,0:T(8,128)} %constant.28.clone.moments) | copy-start | bytes 393220
  1.3 19.2 %copy-start.4 = (f32[8,128,128]{2,1,0:T(8,128)S(1)}, f32[8,128,128]{2,1,0:T(8,128)}, u32[]{:S(2)}) copy-start(f32[8,128,128]{2,1,0:T(8,128)} %frac.1) | copy-start | bytes 1572868
  5.6 4.7 %collective-permute-start.1 = (f32[128,128]{1,0:T(8,128)}, f32[128,128]{1,0:T(8,128)S(1)}, u32[]{:S(2)}, u32[]{:S(2)}) collective-permute-start(f32[128,128]{1,0:T(8,128)} %get-tuple-element.77), channel_id=1, source_target_pairs={{1,0},{2,1},{3,2},{0,3},{5,4},{6,5},{7,6},{4,7},{9,8},{10,9},{11,1... | collective-permute-start | bytes 196616 | tf_op jit(solution)/shard_map/ppermute | solution.py:867
  6.3 4.0 %collective-permute-start = (f32[128,128]{1,0:T(8,128)}, f32[128,128]{1,0:T(8,128)S(1)}, u32[]{:S(2)}, u32[]{:S(2)}) collective-permute-start(f32[128,128]{1,0:T(8,128)} %get-tuple-element.77), channel_id=1, source_target_pairs={{3,0},{0,1},{1,2},{2,3},{7,4},{4,5},{5,6},{6,7},{11,8},{8,9},{9,10... | collective-permute-start | bytes 196616 | tf_op jit(solution)/shard_map/ppermute | solution.py:867
  11.0 14.9 %copy-start.10 = (f32[2,128]{1,0:T(2,128)S(1)}, f32[2,128]{1,0:T(2,128)}, u32[]{:S(2)}) copy-start(f32[2,128]{1,0:T(2,128)} %param.12) | copy-start | bytes 3076
  11.1 15.0 %copy-start.9 = (s32[3]{0:T(128)S(1)}, s32[3]{0:T(128)}, u32[]{:S(2)}) copy-start(s32[3]{0:T(128)} %add_convert_fusion.flags.refs_0_) | copy-start | bytes 40
  11.1 14.9 %collective-permute-start.2 = (f32[9,128,128]{2,1,0:T(8,128)}, f32[9,128,128]{2,1,0:T(8,128)S(1)}, u32[]{:S(2)}, u32[]{:S(2)}) collective-permute-start(f32[9,128,128]{2,1,0:T(8,128)} %get-tuple-element.82), channel_id=1, source_target_pairs={{0,4},{4,0},{8,12},{12,8},{16,20},{20,16},{24,28},{28,24},{32,36},... | collective-permute-start | bytes 1769480 | tf_op jit(solution)/shard_map/ppermute | solution.py:864
  12.8 21.7 %collective-permute-start.3 = (f32[9,128,128]{2,1,0:T(8,128)}, f32[9,128,128]{2,1,0:T(8,128)S(1)}, u32[]{:S(2)}, u32[]{:S(2)}) collective-permute-start(f32[9,128,128]{2,1,0:T(8,128)} %get-tuple-element.92), channel_id=1, source_target_pairs={{4,8},{8,4},{12,16},{16,12},{20,24},{24,20},{28,32},{32,28},{36,40... | collective-permute-start | bytes 1769480 | tf_op jit(solution)/shard_map/ppermute | solution.py:864
  34.5 18.8 %copy-start.2 = (bf16[512,1024]{1,0:T(8,128)(2,1)S(1)}, bf16[512,1024]{1,0:T(8,128)(2,1)}, u32[]{:S(2)}) copy-start(bf16[512,1024]{1,0:T(8,128)(2,1)} %constant.30.clone.table.refs_7_) | copy-start | bytes 3145732
  37.9 3.4 %collective-permute-start.6 = (f32[128,128]{1,0:T(8,128)S(1)}, f32[128,128]{1,0:T(8,128)S(1)}, u32[]{:S(2)}, u32[]{:S(2)}) collective-permute-start(f32[128,128]{1,0:T(8,128)S(1)} %get-tuple-element.100.a), channel_id=1, source_target_pairs={{3,0},{0,1},{1,2},{2,3},{7,4},{4,5},{5,6},{6,7},{11,8},{8,9},{9,10... | collective-permute-start | bytes 196616 | tf_op jit(solution)/shard_map/ppermute | solution.py:867
  39.9 4.5 %collective-permute-start.5 = (f32[128,128]{1,0:T(8,128)S(1)}, f32[128,128]{1,0:T(8,128)S(1)}, u32[]{:S(2)}, u32[]{:S(2)}) collective-permute-start(f32[128,128]{1,0:T(8,128)S(1)} %get-tuple-element.100.a), channel_id=1, source_target_pairs={{2,0},{3,1},{0,2},{1,3},{6,4},{7,5},{4,6},{5,7},{10,8},{11,9},{8,1... | collective-permute-start | bytes 196616 | tf_op jit(solution)/shard_map/ppermute | solution.py:867
  41.1 3.8 %collective-permute-start.4 = (f32[128,128]{1,0:T(8,128)S(1)}, f32[128,128]{1,0:T(8,128)S(1)}, u32[]{:S(2)}, u32[]{:S(2)}) collective-permute-start(f32[128,128]{1,0:T(8,128)S(1)} %get-tuple-element.100.a), channel_id=1, source_target_pairs={{1,0},{2,1},{3,2},{0,3},{5,4},{6,5},{7,6},{4,7},{9,8},{10,9},{11,1... | collective-permute-start | bytes 196616 | tf_op jit(solution)/shard_map/ppermute | solution.py:867
  45.4 15.2 %collective-permute-start.8 = (f32[9,128,128]{2,1,0:T(8,128)S(1)}, f32[9,128,128]{2,1,0:T(8,128)S(1)}, u32[]{:S(2)}, u32[]{:S(2)}) collective-permute-start(f32[9,128,128]{2,1,0:T(8,128)S(1)} %get-tuple-element.102.source), channel_id=1, source_target_pairs={{0,4},{4,0},{8,12},{12,8},{16,20},{20,16},{24,28},{28,24},{32,36},... | collective-permute-start | bytes 1769480 | tf_op jit(solution)/shard_map/ppermute | solution.py:864
  45.5 22.7 %collective-permute-start.7 = (f32[9,128,128]{2,1,0:T(8,128)S(1)}, f32[9,128,128]{2,1,0:T(8,128)S(1)}, u32[]{:S(2)}, u32[]{:S(2)}) collective-permute-start(f32[9,128,128]{2,1,0:T(8,128)S(1)} %get-tuple-element.102.source), channel_id=1, source_target_pairs={{4,8},{8,4},{12,16},{16,12},{20,24},{24,20},{28,32},{32,28},{36,40... | collective-permute-start | bytes 1769480 | tf_op jit(solution)/shard_map/ppermute | solution.py:864
  74.4 4.7 %collective-permute-start.10 = (f32[128,128]{1,0:T(8,128)S(1)}, f32[128,128]{1,0:T(8,128)S(1)}, u32[]{:S(2)}, u32[]{:S(2)}) collective-permute-start(f32[128,128]{1,0:T(8,128)S(1)} %get-tuple-element.112), channel_id=1, source_target_pairs={{1,0},{2,1},{3,2},{0,3},{5,4},{6,5},{7,6},{4,7},{9,8},{10,9},{11,1... | collective-permute-start | bytes 196616 | tf_op jit(solution)/shard_map/ppermute | solution.py:867
  75.1 4.0 %collective-permute-start.9 = (f32[128,128]{1,0:T(8,128)S(1)}, f32[128,128]{1,0:T(8,128)S(1)}, u32[]{:S(2)}, u32[]{:S(2)}) collective-permute-start(f32[128,128]{1,0:T(8,128)S(1)} %get-tuple-element.112), channel_id=1, source_target_pairs={{3,0},{0,1},{1,2},{2,3},{7,4},{4,5},{5,6},{6,7},{11,8},{8,9},{9,10... | collective-permute-start | bytes 196616 | tf_op jit(solution)/shard_map/ppermute | solution.py:867
  79.3 14.6 %collective-permute-start.11 = (f32[9,128,128]{2,1,0:T(8,128)S(1)}, f32[9,128,128]{2,1,0:T(8,128)S(1)}, u32[]{:S(2)}, u32[]{:S(2)}) collective-permute-start(f32[9,128,128]{2,1,0:T(8,128)S(1)} %get-tuple-element.117), channel_id=1, source_target_pairs={{0,4},{4,0},{8,12},{12,8},{16,20},{20,16},{24,28},{28,24},{32,36},... | collective-permute-start | bytes 1769480 | tf_op jit(solution)/shard_map/ppermute | solution.py:864
  79.4 22.1 %collective-permute-start.12 = (f32[9,128,128]{2,1,0:T(8,128)S(1)}, f32[9,128,128]{2,1,0:T(8,128)S(1)}, u32[]{:S(2)}, u32[]{:S(2)}) collective-permute-start(f32[9,128,128]{2,1,0:T(8,128)S(1)} %get-tuple-element.127), channel_id=1, source_target_pairs={{4,8},{8,4},{12,16},{16,12},{20,24},{24,20},{28,32},{32,28},{36,40... | collective-permute-start | bytes 1769480 | tf_op jit(solution)/shard_map/ppermute | solution.py:864
  105.7 2.7 %collective-permute-start.15 = (f32[128,128]{1,0:T(8,128)S(1)}, f32[128,128]{1,0:T(8,128)S(1)}, u32[]{:S(2)}, u32[]{:S(2)}) collective-permute-start(f32[128,128]{1,0:T(8,128)S(1)} %get-tuple-element.136.a), channel_id=1, source_target_pairs={{3,0},{0,1},{1,2},{2,3},{7,4},{4,5},{5,6},{6,7},{11,8},{8,9},{9,10... | collective-permute-start | bytes 196616 | tf_op jit(solution)/shard_map/ppermute | solution.py:867
  106.2 5.4 %collective-permute-start.14 = (f32[128,128]{1,0:T(8,128)S(1)}, f32[128,128]{1,0:T(8,128)S(1)}, u32[]{:S(2)}, u32[]{:S(2)}) collective-permute-start(f32[128,128]{1,0:T(8,128)S(1)} %get-tuple-element.136.a), channel_id=1, source_target_pairs={{2,0},{3,1},{0,2},{1,3},{6,4},{7,5},{4,6},{5,7},{10,8},{11,9},{8,1... | collective-permute-start | bytes 196616 | tf_op jit(solution)/shard_map/ppermute | solution.py:867
  108.4 3.8 %collective-permute-start.13 = (f32[128,128]{1,0:T(8,128)S(1)}, f32[128,128]{1,0:T(8,128)S(1)}, u32[]{:S(2)}, u32[]{:S(2)}) collective-permute-start(f32[128,128]{1,0:T(8,128)S(1)} %get-tuple-element.136.a), channel_id=1, source_target_pairs={{1,0},{2,1},{3,2},{0,3},{5,4},{6,5},{7,6},{4,7},{9,8},{10,9},{11,1... | collective-permute-start | bytes 196616 | tf_op jit(solution)/shard_map/ppermute | solution.py:867
  112.6 15.2 %collective-permute-start.17 = (f32[9,128,128]{2,1,0:T(8,128)S(1)}, f32[9,128,128]{2,1,0:T(8,128)S(1)}, u32[]{:S(2)}, u32[]{:S(2)}) collective-permute-start(f32[9,128,128]{2,1,0:T(8,128)S(1)} %get-tuple-element.138.source), channel_id=1, source_target_pairs={{0,4},{4,0},{8,12},{12,8},{16,20},{20,16},{24,28},{28,24},{32,36},... | collective-permute-start | bytes 1769480 | tf_op jit(solution)/shard_map/ppermute | solution.py:864
  112.7 22.7 %collective-permute-start.16 = (f32[9,128,128]{2,1,0:T(8,128)S(1)}, f32[9,128,128]{2,1,0:T(8,128)S(1)}, u32[]{:S(2)}, u32[]{:S(2)}) collective-permute-start(f32[9,128,128]{2,1,0:T(8,128)S(1)} %get-tuple-element.138.source), channel_id=1, source_target_pairs={{4,8},{8,4},{12,16},{16,12},{20,24},{24,20},{28,32},{32,28},{36,40... | collective-permute-start | bytes 1769480 | tf_op jit(solution)/shard_map/ppermute | solution.py:864
  (5 other events, 43.0 us)

commit v6 on v5

--- a/solution.py
+++ b/solution.py
@@ -387,16 +387,19 @@
 def other_body(flags, message, sides, profile, moments, *refs):
     given, (given_mid, given_frac, given_source) = refs[:7], refs[7:10]
     paired_frac, paired_source, given_pack = refs[10:13]
-    mid, frac_new, source, pack = refs[13:17]
-    scratch, keep_sem = refs[17:-1], refs[-1]
+    mid, frac_new, source, to_paired, to_other, pack = refs[13:19]
+    scratch, keep_sem = refs[19:-1], refs[-1]
     even = flags[2] == 1
     middle = pl.ds(1, NX - 2)
     kept = [
         (given_frac.at[middle], frac_new.at[middle]),
         (paired_frac, frac_new.at[jnp.where(even, NX - 1, 0)]),
-        (given_source.at[pl.ds(2, NX - 4)], source.at[pl.ds(2, NX - 4)]),
         (paired_source, source.at[pl.ds(jnp.where(even, NX - 2, 0), 2)]),
+        (paired_source, to_paired.at[pl.ds(jnp.where(even, NX - 3, 0), 2)]),
+        (paired_source.at[jnp.where(even, 0, 1)], to_other.at[jnp.where(even, NX - 2, 0)]),
     ]
+    for out, place in ((source, 2), (to_paired, jnp.where(even, 1, 2)), (to_other, jnp.where(even, 2, 1))):
+        kept.append((given_source.at[pl.ds(2, NX - 4)], out.at[pl.ds(place, NX - 4)]))
     kept = start_copies(kept, keep_sem)
     pack[...] = given_pack[...]
     for up in (True, False):
@@ -414,18 +417,21 @@
                 scratch,
             )
 
+    place = jnp.where(even, 0, NX - 2)
+    for k in range(2):
+        to_other[jnp.where(even, 0, NX - 3) + k] = source[place + k]
+    to_paired[place] = source[jnp.where(even, 1, NX - 2)]
     for copy in kept:
         copy.wait()
 
 
-def combine_body(a, b, c, d, table, _, message, out, sem):
+def combine_body(a, b, c, d, table, _, __, to_paired, to_other, out, sem):
     total = 0.0
     for k, ref in enumerate((a, b, c, d)):
         total = total + jnp.dot(ref[...], table[k], precision=HIGHEST, preferred_element_type=F32)
     out[...] = total
-    copy = pltpu.make_async_copy(out, message.at[NX], sem)
-    copy.start()
-    copy.wait()
+    for copy in start_copies([(out, message.at[NX - 1]) for message in (to_paired, to_other)], sem):
+        copy.wait()
 
 
 def merge_body(before, after, _, __, right, left, out, sem):
@@ -493,10 +499,10 @@
     E[...] = given_E[...]
     for k in range(1, HALO + 1):
         x = jnp.where(even, k - 1, NX - k)
-        moments = pltpu.roll(paired[NX], (128 - 16 * x) % 128, 1)
+        moments = pltpu.roll(paired[NX - 1], (128 - 16 * x) % 128, 1)
         plane = jnp.where(even, HALO + NX - 1 + k, HALO - k)
         place = jnp.where(even, k - 1, HALO - k)
-        terms(table, U, E, lhs, place, plane, paired[x], moments, k - 1)
+        terms(table, U, E, lhs, place, plane, paired[place], moments, k - 1)
 
 
 def domain(flags):
@@ -612,9 +618,10 @@
     E[...] = jnp.zeros((2, NY, 128), F32)
     for k in range(1, HALO + 1):
         x = jnp.where(even, NX - k, k - 1)
-        moments = pltpu.roll(other[NX], (128 - 16 * x) % 128, 1)
+        moments = pltpu.roll(other[NX - 1], (128 - 16 * x) % 128, 1)
         plane = halo_plane(k)
-        terms(table, U, E, lhs, plane, plane, other[x], moments, k - 1, first_group)
+        place = jnp.where(even, HALO - k, k - 1)
+        terms(table, U, E, lhs, plane, plane, other[place], moments, k - 1, first_group)
     for m in range(top, -1, -1):
         for depth in (top - m, top + 1 - m):
             U[m, own_plane(depth)] = jnp.zeros((ROWS, NZ), F32)
@@ -708,7 +715,7 @@
 PREDICTED = tuple(shape(*PADDED) for _ in range(7)) + (
     shape(3, *BLOCK),
     shape(*BLOCK),
-    shape(*MESSAGE),
+    shape(*BLOCK),
     shape(NY, 128),
 )
 
@@ -751,26 +758,26 @@
     *buffers, mid, inner_frac, inner_source, _ = inner
     return pl.pallas_call(
         other_body,
-        out_shape=(shape(3, 1, NY, NZ), shape(*BLOCK), shape(*MESSAGE), shape(NY, 128)),
+        out_shape=(shape(3, 1, NY, NZ), *[shape(*BLOCK)] * 4, shape(NY, 128)),
         in_specs=[IN_SMEM] + [ANYWHERE] + [IN_VMEM] * 11 + [ANYWHERE] * 4 + [IN_VMEM],
-        out_specs=(IN_VMEM,) * 4,
-        scratch_shapes=SIDE_SCRATCH + [pltpu.SemaphoreType.DMA((4,))],
+        out_specs=(IN_VMEM,) * 6,
+        scratch_shapes=SIDE_SCRATCH + [pltpu.SemaphoreType.DMA((8,))],
         compiler_params=pltpu.CompilerParams(vmem_limit_bytes=12 * MIB),
         name="other_side",
     )(flags, message, sides, profile, moments, *buffers, mid, inner_frac, inner_source, frac, source, pack)
 
 
-def combine_call(packs, table, message):
+def combine_call(packs, table, to_paired, to_other):
     return pl.pallas_call(
         combine_body,
-        out_shape=(shape(*MESSAGE), shape(NY, 128)),
-        in_specs=[IN_VMEM] * 5 + [ANYWHERE],
-        out_specs=(ANYWHERE, IN_VMEM),
-        scratch_shapes=[pltpu.SemaphoreType.DMA],
-        input_output_aliases={5: 0},
+        out_shape=(shape(*BLOCK), shape(*BLOCK), shape(NY, 128)),
+        in_specs=[IN_VMEM] * 5 + [ANYWHERE] * 2,
+        out_specs=(ANYWHERE, ANYWHERE, IN_VMEM),
+        scratch_shapes=[pltpu.SemaphoreType.DMA((2,))],
+        input_output_aliases={5: 0, 6: 1},
         compiler_params=pltpu.CompilerParams(vmem_limit_bytes=4 * MIB),
         name="combine",
-    )(*packs, table, message)
+    )(*packs, table, to_paired, to_other)
 
 
 def merge_call(before, after, right, left):
@@ -882,12 +889,13 @@
         paired = exchange(paired, True)
         inner = inner_call(velocity, fraction, guess, sides, moments)
         mid_paired, frac, source, pack = paired_call(flags, paired, sides, profile, moments, inner)
-        mid_other, fraction, source, pack = other_call(
+        mid_other, fraction, source, to_paired, to_other, pack = other_call(
             flags, other, sides, profile, moments, inner, frac, source, pack
         )
-        source, far = combine_call([pack] + [around(pack, o) for o in (1, 2, 3)], combine, source)
-        other = exchange(source, False)
-        paired = exchange(source, True)
+        packs = [pack] + [around(pack, o) for o in (1, 2, 3)]
+        to_paired, to_other, far = combine_call(packs, combine, to_paired, to_other)
+        other = exchange(to_other, False)
+        paired = exchange(to_paired, True)
         own, ends = own_terms_call(source, far, table)
         side, ends = side_terms_call(flags, paired, ends, table)
         part, ends = first_sweeps_call(flags, own, side, ends)

time: 142 us -> 140 us (0.986)
  waiting for transfers between devices: 35.2 us -> 32.3 us
    ppermute x8, waiting for transfers between devices: 21.9 us -> 19 us  [exchange(): return lax.ppermute(block, 'stream', pairs if with_pair else others)]
where the time goes in v6:
time: 140 us; the launch traced here: 139 us
  Pallas kernels  63.1 us (45%)
  starting transfers between devices  42.3 us (30%)
  waiting for transfers between devices  32.3 us (23%)
    ppermute x8, starting transfers between devices, exchange(): return lax.ppermute(block, 'stream', pairs if with_pair else others)  32.8 us
    ppermute x8, waiting for transfers between devices, exchange(): return lax.ppermute(block, 'stream', pairs if with_pair else others)  19 us
    ppermute x10, waiting for transfers between devices, around(): lax.ppermute(block, 'span', [((i + offset) % BLOCKS, i) for i in range(BL...  13.3 us
    pallas_call x2, Pallas kernels, solve_call(): pl.pallas_call(functools.partial(solve_body, more), out_shape=tuple(outs)...  12.2 us
    pallas_call x2, Pallas kernels, inner_call(): pl.pallas_call(inner_body, out_shape=PREDICTED, in_specs=[ANYWHERE] * 3 +...  9.96 us
    ppermute x10, starting transfers between devices, around(): lax.ppermute(block, 'span', [((i + offset) % BLOCKS, i) for i in range(BL...  9.47 us
    pallas_call x2, Pallas kernels, first_sweeps_call(): pl.pallas_call(first_sweeps_body, out_shape=(shape(*SUM), shape(3, NY, 12...  9.41 us
    pallas_call x2, Pallas kernels, other_call(): pl.pallas_call(other_body, out_shape=(shape(3, 1, NY, NZ), *[shape(*BLOCK...  8.19 us
  transfers between devices with their start and end apart: 18, of which 15 were waited for; matrix products, arithmetic and copies ran while one was open for 0% of the time, Pallas kernels for 26%

profile of v6, /device:TPU:7, one launch (start us, length us, event | category | flops | bytes accessed | tf_op | source)
XLA Modules:
  0.0 139.4 jit_solution(7133356724523081397)
XLA Ops:
  1.3 4.3 %pack.1 = (f32[9,128,128]{2,1,0:T(8,128)}, f32[9,128,128]{2,1,0:T(8,128)}, f32[128,128]{1,0:T(8,128)}, f32[8,128,128]{2,1,0:T(8,128)}) custom-call(s32[3]{0:T(128)} %add_convert_fusion.flags.refs_0_, f32[3,8,128,128]{3,2,1,0:T(8,128)} %vel.1, f32[8,128,128]{2,1,0:T(8,128)} %frac.1, f32[8,128,128]{2,1,0:T(8,128)} %refs_5_.1, f32[8,128,128]{2,1,0:T(8,128)} %old_far.1), custom_call_target="tpu_custom_call" | custom-call | tf_op jit(solution)/shard_map/pack/pallas_call | solution.py:701
  7.4 2.9 %collective-permute-done.1.after = f32[128,128]{1,0:T(8,128)S(1)} collective-permute-done((f32[128,128]{1,0:T(8,128)}, f32[128,128]{1,0:T(8,128)S(1)}, u32[]{:S(2)}, u32[]{:S(2)}) %collective-permute-start.1) | collective-permute-done | bytes 65568 | tf_op jit(solution)/shard_map/ppermute | solution.py:874
  12.8 7.6 %collective-permute-start.3 = (f32[9,128,128]{2,1,0:T(8,128)}, f32[9,128,128]{2,1,0:T(8,128)S(1)}, u32[]{:S(2)}, u32[]{:S(2)}) collective-permute-start(f32[9,128,128]{2,1,0:T(8,128)} %get-tuple-element.98), channel_id=1, source_target_pairs={{4,8},{8,4},{12,16},{16,12},{20,24},{24,20},{28,32},{32,28},{36,40... | collective-permute-start | bytes 1769480 | tf_op jit(solution)/shard_map/ppermute | solution.py:871
  20.4 5.0 %inner.2 = (f32[8,144,128]{2,1,0:T(8,128)S(1)}, f32[8,144,128]{2,1,0:T(8,128)S(1)}, f32[8,144,128]{2,1,0:T(8,128)S(1)}, f32[8,144,128]{2,1,0:T(8,128)S(1)}, f32[...) custom-call(f32[3,8,128,128]{3,2,1,0:T(8,128)S(1)} %copy-done, ...), custom_call_target="tpu_custom_call" | custom-call | flops 20000000 | bytes 16000000 | tf_op jit(solution)/shard_map/inner/pallas_call | solution.py:724
  26.1 2.8 %paired_side.2 = (f32[3,1,128,128]{3,2,1,0:T(8,128)S(1)}, f32[128,128]{1,0:T(8,128)S(1)}, f32[2,128,128]{2,1,0:T(8,128)S(1)}, f32[128,128]{1,0:T(8,128)S(1)}) custom-call(s32[3]{0:T(128)S(1)} %copy-done.9, f32[9,128,128]{2,1,0:T(8,128)S(1)} %collective-permute-done.2.message, f32[128,128]{1,0:T(8,128)S(1)} %get-tuple-element.86.sides, ...), custom_call_target="tpu_custom_call" | custom-call | flops 6000000 | bytes 6000000 | tf_op jit(solution)/shard_map/paired_side/pallas_call | solution.py:745
  28.9 5.6 %collective-permute-done.3.message = f32[9,128,128]{2,1,0:T(8,128)S(1)} collective-permute-done((f32[9,128,128]{2,1,0:T(8,128)}, f32[9,128,128]{2,1,0:T(8,128)S(1)}, u32[]{:S(2)}, u32[]{:S(2)}) %collective-permute-start.3) | collective-permute-done | bytes 589856 | tf_op jit(solution)/shard_map/ppermute | solution.py:871
  34.5 3.7 %other_side.2 = (f32[3,1,128,128]{3,2,1,0:T(8,128)S(1)}, f32[8,128,128]{2,1,0:T(8,128)S(1)}, f32[8,128,128]{2,1,0:T(8,128)S(1)}, f32[8,128,128]{2,1,0:T(8,128)S(...) custom-call(s32[3]{0:T(128)S(1)} %copy-done.9, f32[9,128,128]{2,1,0:T(8,128)S(1)} %collective-permute-done.3.message, ...), custom_call_target="tpu_custom_call" | custom-call | tf_op jit(solution)/shard_map/other_side/pallas_call | solution.py:759
  41.6 3.2 %collective-permute-done.5.c = f32[128,128]{1,0:T(8,128)S(1)} collective-permute-done((f32[128,128]{1,0:T(8,128)S(1)}, f32[128,128]{1,0:T(8,128)S(1)}, u32[]{:S(2)}, u32[]{:S(2)}) %collective-permute-start.5) | collective-permute-done | bytes 65568 | tf_op jit(solution)/shard_map/ppermute | solution.py:874
  45.9 7.9 %collective-permute-start.7 = (f32[8,128,128]{2,1,0:T(8,128)S(1)}, f32[8,128,128]{2,1,0:T(8,128)S(1)}, u32[]{:S(2)}, u32[]{:S(2)}) collective-permute-start(f32[8,128,128]{2,1,0:T(8,128)S(1)} %get-tuple-element.109), channel_id=1, source_target_pairs={{4,8},{8,4},{12,16},{16,12},{20,24},{24,20},{28,32},{32,28},{36,40... | collective-permute-start | bytes 1572872 | tf_op jit(solution)/shard_map/ppermute | solution.py:871
  53.8 3.9 %own_terms.2 = (f32[7,8,144,128]{3,2,1,0:T(8,128)S(1)}, f32[3,128,128]{2,1,0:T(8,128)S(1)}) custom-call(f32[8,128,128]{2,1,0:T(8,128)S(1)} %get-tuple-element.110.source, f32[128,128]{1,0:T(8,128)S(1)} %get-tuple-element.111.far, bf16[512,1024]{1,0:T(8,128)(2,1)S(1)} %copy-done.2), custom_call_target="tpu_custom_call" | custom-call | flops 1000000000 | bytes 12000000 | tf_op jit(solution)/shard_map/own_terms/pallas_call | solution.py:800
  61.3 4.7 %first_sweeps.2 = (f32[10,144,128]{2,1,0:T(8,128)S(1)}, f32[3,128,128]{2,1,0:T(8,128)S(1)}) custom-call(s32[3]{0:T(128)S(1)} %copy-done.9, f32[7,8,144,128]{3,2,1,0:T(8,128)S(1)} %get-tuple-element.112.given_U, f32[7,7,144,128]{3,2,1,0:T(8,128)S(1)} %get-tuple-element.115.given_side, f32[3,128,128]{2,1,0:T(8,128)S(1)} %get-tuple-element.116.given_E), custom_call_target="tpu_custom_call" | custom-call | flops 10000000 | bytes 14000000 | tf_op jit(solution)/shard_map/first_sweeps/pallas_call | solution.py:830
  67.2 6.2 %solve.2 = (f32[3,8,128,128]{3,2,1,0:T(8,128)S(1)}, f32[8,128,128]{2,1,0:T(8,128)}, f32[9,128,128]{2,1,0:T(8,128)S(1)}, f32[9,128,128]{2,1,0:T(8,128)S(1)}, f32[...) custom-call(s32[3]{0:T(128)S(1)} %copy-done.9, f32[3,8,128,128]{3,2,1,0:T(8,128)S(1)} %get-tuple-element.87.refs_7_.refs_1_, ...), custom_call_target="tpu_custom_call" | custom-call | tf_op jit(solution)/shard_map/solve/pallas_call | solution.py:846
  75.2 2.9 %collective-permute-done.10.after = f32[128,128]{1,0:T(8,128)S(1)} collective-permute-done((f32[128,128]{1,0:T(8,128)S(1)}, f32[128,128]{1,0:T(8,128)S(1)}, u32[]{:S(2)}, u32[]{:S(2)}) %collective-permute-start.10) | collective-permute-done | bytes 65568 | tf_op jit(solution)/shard_map/ppermute | solution.py:874
  78.4 7.7 %collective-permute-start.12 = (f32[9,128,128]{2,1,0:T(8,128)S(1)}, f32[9,128,128]{2,1,0:T(8,128)S(1)}, u32[]{:S(2)}, u32[]{:S(2)}) collective-permute-start(f32[9,128,128]{2,1,0:T(8,128)S(1)} %get-tuple-element.136), channel_id=1, source_target_pairs={{4,8},{8,4},{12,16},{16,12},{20,24},{24,20},{28,32},{32,28},{36,40... | collective-permute-start | bytes 1769480 | tf_op jit(solution)/shard_map/ppermute | solution.py:871
  86.1 5.0 %inner.3 = (f32[8,144,128]{2,1,0:T(8,128)S(1)}, f32[8,144,128]{2,1,0:T(8,128)S(1)}, f32[8,144,128]{2,1,0:T(8,128)S(1)}, f32[8,144,128]{2,1,0:T(8,128)S(1)}, f32[...) custom-call(f32[3,8,128,128]{3,2,1,0:T(8,128)S(1)} %get-tuple-elemen, ...), custom_call_target="tpu_custom_call" | custom-call | flops 20000000 | bytes 16000000 | tf_op jit(solution)/shard_map/inner/pallas_call | solution.py:724
  92.9 2.8 %paired_side.3 = (f32[3,1,128,128]{3,2,1,0:T(8,128)S(1)}, f32[128,128]{1,0:T(8,128)S(1)}, f32[2,128,128]{2,1,0:T(8,128)S(1)}, f32[128,128]{1,0:T(8,128)S(1)}) custom-call(s32[3]{0:T(128)S(1)} %copy-done.9, f32[9,128,128]{2,1,0:T(8,128)S(1)} %collective-permute-done.11.message, f32[128,128]{1,0:T(8,128)S(1)} %get-tuple-element.124.sides, ...), custom_call_target="tpu_custom_call" | custom-call | flops 6000000 | bytes 6000000 | tf_op jit(solution)/shard_map/paired_side/pallas_call | solution.py:745
  95.8 4.8 %collective-permute-done.12.message = f32[9,128,128]{2,1,0:T(8,128)S(1)} collective-permute-done((f32[9,128,128]{2,1,0:T(8,128)S(1)}, f32[9,128,128]{2,1,0:T(8,128)S(1)}, u32[]{:S(2)}, u32[]{:S(2)}) %collective-permute-start.12) | collective-permute-done | bytes 589856 | tf_op jit(solution)/shard_map/ppermute | solution.py:871
  100.6 4.5 %other_side.3 = (f32[3,1,128,128]{3,2,1,0:T(8,128)S(1)}, f32[8,128,128]{2,1,0:T(8,128)}, f32[8,128,128]{2,1,0:T(8,128)S(1)}, f32[8,128,128]{2,1,0:T(8,128)S(1)},...) custom-call(s32[3]{0:T(128)S(1)} %copy-done.9, f32[9,128,128]{2,1,0:T(8,128)S(1)} %collective-permute-done.12.message, ...), custom_call_target="tpu_custom_call" | custom-call | tf_op jit(solution)/shard_map/other_side/pallas_call | solution.py:759
  105.6 2.1 %collective-permute-start.14 = (f32[128,128]{1,0:T(8,128)S(1)}, f32[128,128]{1,0:T(8,128)S(1)}, u32[]{:S(2)}, u32[]{:S(2)}) collective-permute-start(f32[128,128]{1,0:T(8,128)S(1)} %get-tuple-element.145.a), channel_id=1, source_target_pairs={{2,0},{3,1},{0,2},{1,3},{6,4},{7,5},{4,6},{5,7},{10,8},{11,9},{8,1... | collective-permute-start | bytes 196616 | tf_op jit(solution)/shard_map/ppermute | solution.py:874
  107.7 3.2 %collective-permute-done.14.c = f32[128,128]{1,0:T(8,128)S(1)} collective-permute-done((f32[128,128]{1,0:T(8,128)S(1)}, f32[128,128]{1,0:T(8,128)S(1)}, u32[]{:S(2)}, u32[]{:S(2)}) %collective-permute-start.14) | collective-permute-done | bytes 65568 | tf_op jit(solution)/shard_map/ppermute | solution.py:874
  112.2 7.7 %collective-permute-start.16 = (f32[8,128,128]{2,1,0:T(8,128)S(1)}, f32[8,128,128]{2,1,0:T(8,128)S(1)}, u32[]{:S(2)}, u32[]{:S(2)}) collective-permute-start(f32[8,128,128]{2,1,0:T(8,128)S(1)} %get-tuple-element.148), channel_id=1, source_target_pairs={{4,8},{8,4},{12,16},{16,12},{20,24},{24,20},{28,32},{32,28},{36,40... | collective-permute-start | bytes 1572872 | tf_op jit(solution)/shard_map/ppermute | solution.py:871
  119.9 3.9 %own_terms.3 = (f32[7,8,144,128]{3,2,1,0:T(8,128)S(1)}, f32[3,128,128]{2,1,0:T(8,128)S(1)}) custom-call(f32[8,128,128]{2,1,0:T(8,128)S(1)} %get-tuple-element.149.source, f32[128,128]{1,0:T(8,128)S(1)} %get-tuple-element.150.far, bf16[512,1024]{1,0:T(8,128)(2,1)S(1)} %copy-done.2), custom_call_target="tpu_custom_call" | custom-call | flops 1000000000 | bytes 12000000 | tf_op jit(solution)/shard_map/own_terms/pallas_call | solution.py:800
  127.5 4.7 %first_sweeps.3 = (f32[10,144,128]{2,1,0:T(8,128)S(1)}, f32[3,128,128]{2,1,0:T(8,128)S(1)}) custom-call(s32[3]{0:T(128)S(1)} %copy-done.9, f32[7,8,144,128]{3,2,1,0:T(8,128)S(1)} %get-tuple-element.151.given_U, f32[7,7,144,128]{3,2,1,0:T(8,128)S(1)} %get-tuple-element.154.given_side, f32[3,128,128]{2,1,0:T(8,128)S(1)} %get-tuple-element.155.given_E), custom_call_target="tpu_custom_call" | custom-call | flops 10000000 | bytes 14000000 | tf_op jit(solution)/shard_map/first_sweeps/pallas_call | solution.py:830
  133.3 6.0 %solve.3 = (f32[3,8,128,128]{3,2,1,0:T(8,128)}, f32[8,128,128]{2,1,0:T(8,128)}) custom-call(s32[3]{0:T(128)S(1)} %copy-done.9, f32[3,8,128,128]{3,2,1,0:T(8,128)S(1)} %get-tuple-element.125.refs_7_.refs_1_, f32[3,1,128,128]{3,2,1,0:T(8,128)S(1)} %get-tuple-element.135.refs_2_, f32[3,1,128,128]{3,2,1,0:T(8,128)S(1)} %get-tuple-element.142.refs_3_, ...), custom_call_target="tpu_custom_call" | custom-call | tf_op jit(solution)/shard_map/solve/pallas_call | solution.py:846
  (55 shorter events, 25.4 us)
Async XLA Ops:
  1.3 19.2 %copy-start = (f32[3,8,128,128]{3,2,1,0:T(8,128)S(1)}, f32[3,8,128,128]{3,2,1,0:T(8,128)}, u32[]{:S(2)}) copy-start(f32[3,8,128,128]{3,2,1,0:T(8,128)} %vel.1) | copy-start | bytes 4718596
  1.3 19.2 %copy-start.1 = (f32[2,128,128]{2,1,0:T(8,128)S(1)}, f32[2,128,128]{2,1,0:T(8,128)}, u32[]{:S(2)}) copy-start(f32[2,128,128]{2,1,0:T(8,128)} %constant.28.clone.moments) | copy-start | bytes 393220
  1.3 19.2 %copy-start.3 = (f32[8,128,128]{2,1,0:T(8,128)S(1)}, f32[8,128,128]{2,1,0:T(8,128)}, u32[]{:S(2)}) copy-start(f32[8,128,128]{2,1,0:T(8,128)} %frac.1) | copy-start | bytes 1572868
  5.6 4.7 %collective-permute-start.1 = (f32[128,128]{1,0:T(8,128)}, f32[128,128]{1,0:T(8,128)S(1)}, u32[]{:S(2)}, u32[]{:S(2)}) collective-permute-start(f32[128,128]{1,0:T(8,128)} %get-tuple-element.83), channel_id=1, source_target_pairs={{1,0},{2,1},{3,2},{0,3},{5,4},{6,5},{7,6},{4,7},{9,8},{10,9},{11,1... | collective-permute-start | bytes 196616 | tf_op jit(solution)/shard_map/ppermute | solution.py:874
  6.3 4.0 %collective-permute-start = (f32[128,128]{1,0:T(8,128)}, f32[128,128]{1,0:T(8,128)S(1)}, u32[]{:S(2)}, u32[]{:S(2)}) collective-permute-start(f32[128,128]{1,0:T(8,128)} %get-tuple-element.83), channel_id=1, source_target_pairs={{3,0},{0,1},{1,2},{2,3},{7,4},{4,5},{5,6},{6,7},{11,8},{8,9},{9,10... | collective-permute-start | bytes 196616 | tf_op jit(solution)/shard_map/ppermute | solution.py:874
  11.0 14.9 %copy-start.10 = (f32[2,128]{1,0:T(2,128)S(1)}, f32[2,128]{1,0:T(2,128)}, u32[]{:S(2)}) copy-start(f32[2,128]{1,0:T(2,128)} %param.12) | copy-start | bytes 3076
  11.1 15.0 %copy-start.9 = (s32[3]{0:T(128)S(1)}, s32[3]{0:T(128)}, u32[]{:S(2)}) copy-start(s32[3]{0:T(128)} %add_convert_fusion.flags.refs_0_) | copy-start | bytes 40
  11.1 14.9 %collective-permute-start.2 = (f32[9,128,128]{2,1,0:T(8,128)}, f32[9,128,128]{2,1,0:T(8,128)S(1)}, u32[]{:S(2)}, u32[]{:S(2)}) collective-permute-start(f32[9,128,128]{2,1,0:T(8,128)} %get-tuple-element.88), channel_id=1, source_target_pairs={{0,4},{4,0},{8,12},{12,8},{16,20},{20,16},{24,28},{28,24},{32,36},... | collective-permute-start | bytes 1769480 | tf_op jit(solution)/shard_map/ppermute | solution.py:871
  12.8 21.7 %collective-permute-start.3 = (f32[9,128,128]{2,1,0:T(8,128)}, f32[9,128,128]{2,1,0:T(8,128)S(1)}, u32[]{:S(2)}, u32[]{:S(2)}) collective-permute-start(f32[9,128,128]{2,1,0:T(8,128)} %get-tuple-element.98), channel_id=1, source_target_pairs={{4,8},{8,4},{12,16},{16,12},{20,24},{24,20},{28,32},{32,28},{36,40... | collective-permute-start | bytes 1769480 | tf_op jit(solution)/shard_map/ppermute | solution.py:871
  38.2 15.6 %copy-start.2 = (bf16[512,1024]{1,0:T(8,128)(2,1)S(1)}, bf16[512,1024]{1,0:T(8,128)(2,1)}, u32[]{:S(2)}) copy-start(bf16[512,1024]{1,0:T(8,128)(2,1)} %constant.30.clone.table.refs_7_) | copy-start | bytes 3145732
  38.2 3.4 %collective-permute-start.6 = (f32[128,128]{1,0:T(8,128)S(1)}, f32[128,128]{1,0:T(8,128)S(1)}, u32[]{:S(2)}, u32[]{:S(2)}) collective-permute-start(f32[128,128]{1,0:T(8,128)S(1)} %get-tuple-element.106.a), channel_id=1, source_target_pairs={{3,0},{0,1},{1,2},{2,3},{7,4},{4,5},{5,6},{6,7},{11,8},{8,9},{9,10... | collective-permute-start | bytes 196616 | tf_op jit(solution)/shard_map/ppermute | solution.py:874
  40.2 4.5 %collective-permute-start.5 = (f32[128,128]{1,0:T(8,128)S(1)}, f32[128,128]{1,0:T(8,128)S(1)}, u32[]{:S(2)}, u32[]{:S(2)}) collective-permute-start(f32[128,128]{1,0:T(8,128)S(1)} %get-tuple-element.106.a), channel_id=1, source_target_pairs={{2,0},{3,1},{0,2},{1,3},{6,4},{7,5},{4,6},{5,7},{10,8},{11,9},{8,1... | collective-permute-start | bytes 196616 | tf_op jit(solution)/shard_map/ppermute | solution.py:874
  41.5 3.8 %collective-permute-start.4 = (f32[128,128]{1,0:T(8,128)S(1)}, f32[128,128]{1,0:T(8,128)S(1)}, u32[]{:S(2)}, u32[]{:S(2)}) collective-permute-start(f32[128,128]{1,0:T(8,128)S(1)} %get-tuple-element.106.a), channel_id=1, source_target_pairs={{1,0},{2,1},{3,2},{0,3},{5,4},{6,5},{7,6},{4,7},{9,8},{10,9},{11,1... | collective-permute-start | bytes 196616 | tf_op jit(solution)/shard_map/ppermute | solution.py:874
  45.8 13.8 %collective-permute-start.8 = (f32[8,128,128]{2,1,0:T(8,128)S(1)}, f32[8,128,128]{2,1,0:T(8,128)S(1)}, u32[]{:S(2)}, u32[]{:S(2)}) collective-permute-start(f32[8,128,128]{2,1,0:T(8,128)S(1)} %get-tuple-element.113), channel_id=1, source_target_pairs={{0,4},{4,0},{8,12},{12,8},{16,20},{20,16},{24,28},{28,24},{32,36},... | collective-permute-start | bytes 1572872 | tf_op jit(solution)/shard_map/ppermute | solution.py:871
  45.9 21.3 %collective-permute-start.7 = (f32[8,128,128]{2,1,0:T(8,128)S(1)}, f32[8,128,128]{2,1,0:T(8,128)S(1)}, u32[]{:S(2)}, u32[]{:S(2)}) collective-permute-start(f32[8,128,128]{2,1,0:T(8,128)S(1)} %get-tuple-element.109), channel_id=1, source_target_pairs={{4,8},{8,4},{12,16},{16,12},{20,24},{24,20},{28,32},{32,28},{36,40... | collective-permute-start | bytes 1572872 | tf_op jit(solution)/shard_map/ppermute | solution.py:871
  73.4 4.6 %collective-permute-start.10 = (f32[128,128]{1,0:T(8,128)S(1)}, f32[128,128]{1,0:T(8,128)S(1)}, u32[]{:S(2)}, u32[]{:S(2)}) collective-permute-start(f32[128,128]{1,0:T(8,128)S(1)} %get-tuple-element.121), channel_id=1, source_target_pairs={{1,0},{2,1},{3,2},{0,3},{5,4},{6,5},{7,6},{4,7},{9,8},{10,9},{11,1... | collective-permute-start | bytes 196616 | tf_op jit(solution)/shard_map/ppermute | solution.py:874
  74.1 4.0 %collective-permute-start.9 = (f32[128,128]{1,0:T(8,128)S(1)}, f32[128,128]{1,0:T(8,128)S(1)}, u32[]{:S(2)}, u32[]{:S(2)}) collective-permute-start(f32[128,128]{1,0:T(8,128)S(1)} %get-tuple-element.121), channel_id=1, source_target_pairs={{3,0},{0,1},{1,2},{2,3},{7,4},{4,5},{5,6},{6,7},{11,8},{8,9},{9,10... | collective-permute-start | bytes 196616 | tf_op jit(solution)/shard_map/ppermute | solution.py:874
  78.4 14.6 %collective-permute-start.11 = (f32[9,128,128]{2,1,0:T(8,128)S(1)}, f32[9,128,128]{2,1,0:T(8,128)S(1)}, u32[]{:S(2)}, u32[]{:S(2)}) collective-permute-start(f32[9,128,128]{2,1,0:T(8,128)S(1)} %get-tuple-element.126), channel_id=1, source_target_pairs={{0,4},{4,0},{8,12},{12,8},{16,20},{20,16},{24,28},{28,24},{32,36},... | collective-permute-start | bytes 1769480 | tf_op jit(solution)/shard_map/ppermute | solution.py:871
  78.4 22.1 %collective-permute-start.12 = (f32[9,128,128]{2,1,0:T(8,128)S(1)}, f32[9,128,128]{2,1,0:T(8,128)S(1)}, u32[]{:S(2)}, u32[]{:S(2)}) collective-permute-start(f32[9,128,128]{2,1,0:T(8,128)S(1)} %get-tuple-element.136), channel_id=1, source_target_pairs={{4,8},{8,4},{12,16},{16,12},{20,24},{24,20},{28,32},{32,28},{36,40... | collective-permute-start | bytes 1769480 | tf_op jit(solution)/shard_map/ppermute | solution.py:871
  105.1 2.7 %collective-permute-start.15 = (f32[128,128]{1,0:T(8,128)S(1)}, f32[128,128]{1,0:T(8,128)S(1)}, u32[]{:S(2)}, u32[]{:S(2)}) collective-permute-start(f32[128,128]{1,0:T(8,128)S(1)} %get-tuple-element.145.a), channel_id=1, source_target_pairs={{3,0},{0,1},{1,2},{2,3},{7,4},{4,5},{5,6},{6,7},{11,8},{8,9},{9,10... | collective-permute-start | bytes 196616 | tf_op jit(solution)/shard_map/ppermute | solution.py:874
  105.6 5.3 %collective-permute-start.14 = (f32[128,128]{1,0:T(8,128)S(1)}, f32[128,128]{1,0:T(8,128)S(1)}, u32[]{:S(2)}, u32[]{:S(2)}) collective-permute-start(f32[128,128]{1,0:T(8,128)S(1)} %get-tuple-element.145.a), channel_id=1, source_target_pairs={{2,0},{3,1},{0,2},{1,3},{6,4},{7,5},{4,6},{5,7},{10,8},{11,9},{8,1... | collective-permute-start | bytes 196616 | tf_op jit(solution)/shard_map/ppermute | solution.py:874
  107.7 3.8 %collective-permute-start.13 = (f32[128,128]{1,0:T(8,128)S(1)}, f32[128,128]{1,0:T(8,128)S(1)}, u32[]{:S(2)}, u32[]{:S(2)}) collective-permute-start(f32[128,128]{1,0:T(8,128)S(1)} %get-tuple-element.145.a), channel_id=1, source_target_pairs={{1,0},{2,1},{3,2},{0,3},{5,4},{6,5},{7,6},{4,7},{9,8},{10,9},{11,1... | collective-permute-start | bytes 196616 | tf_op jit(solution)/shard_map/ppermute | solution.py:874
  112.1 13.6 %collective-permute-start.17 = (f32[8,128,128]{2,1,0:T(8,128)S(1)}, f32[8,128,128]{2,1,0:T(8,128)S(1)}, u32[]{:S(2)}, u32[]{:S(2)}) collective-permute-start(f32[8,128,128]{2,1,0:T(8,128)S(1)} %get-tuple-element.152), channel_id=1, source_target_pairs={{0,4},{4,0},{8,12},{12,8},{16,20},{20,16},{24,28},{28,24},{32,36},... | collective-permute-start | bytes 1572872 | tf_op jit(solution)/shard_map/ppermute | solution.py:871
  112.2 21.2 %collective-permute-start.16 = (f32[8,128,128]{2,1,0:T(8,128)S(1)}, f32[8,128,128]{2,1,0:T(8,128)S(1)}, u32[]{:S(2)}, u32[]{:S(2)}) collective-permute-start(f32[8,128,128]{2,1,0:T(8,128)S(1)} %get-tuple-element.148), channel_id=1, source_target_pairs={{4,8},{8,4},{12,16},{16,12},{20,24},{24,20},{28,32},{32,28},{36,40... | collective-permute-start | bytes 1572872 | tf_op jit(solution)/shard_map/ppermute | solution.py:871
  (5 other events, 43.3 us)

commit v7 on v6

--- a/solution.py
+++ b/solution.py
@@ -362,7 +362,7 @@
         (end_mid[rows],) = cells(*outside, Z, 10 if up else 1, y, (0,))
         return carry
 
-    lax.fori_loop(0, 16, block, 0, unroll=2)
+    lax.fori_loop(0, 16, block, 0, unroll=4)
     if up:
         source[0] = source_plane(6, given_mid[0, 5], mid[0], given_mid[1, 6], given_mid[2, 6], moments, pack)
         source[1] = source_plane(7, given_mid[0, 6], end_mid[...], mid[1], mid[2], moments, pack)
@@ -491,7 +491,7 @@
         terms(table, U, E, lhs, x, x + HALO, source[x], moments, 0)
         return carry
 
-    lax.fori_loop(0, NX, own_plane, 0)
+    lax.fori_loop(0, NX, own_plane, 0, unroll=2)
 
 
 def side_terms_body(flags, paired, given_E, table, U, E, lhs):
@@ -588,7 +588,7 @@
                 )
             return carry
 
-        lax.fori_loop(0, m + 1, sweep, 0)
+        lax.fori_loop(0, m + 1, sweep, 0, unroll=2 if m % 2 == 1 else 1)
         lax.fori_loop(0, NX, sweep_own, 0, unroll=2)
 
     def emit(j, carry):
@@ -642,8 +642,8 @@
                 put(U, m, plane, y, beside(U, m + 1, plane, y))
             return carry
 
-        lax.fori_loop(0, m + 1, sweep, 0)
-        lax.fori_loop(0, top - m, sweep_own, 0)
+        lax.fori_loop(0, m + 1, sweep, 0, unroll=2 if m % 2 == 1 else 1)
+        lax.fori_loop(0, top - m, sweep_own, 0, unroll=2 if (top - m) % 2 == 0 else 1)
 
     for j in range(NX + 2):
         T[j] = given_sum[j] + U[0, HALO - 1 + j]

time: 140 us -> 140 us (level)
  Pallas kernels: 63.1 us -> 60.1 us
  waiting for transfers between devices: 32.3 us -> 35.2 us
    ppermute x8, waiting for transfers between devices: 19 us -> 21.9 us  [exchange(): return lax.ppermute(block, 'stream', pairs if with_pair else others)]
    pallas_call x2, Pallas kernels: 7.73 us -> 5.07 us  [own_terms_call(): pl.pallas_call(own_terms_body, out_shape=(shape(*OWN_TERMS), shape(3, NY,...]
  transfers between devices with their start and end apart: 18 -> 18, of which waited for: 15 -> 15; matrix products, arithmetic and copies ran while one was open for 0% -> 0% of each run, Pallas kernels for 26% -> 24%
where the time goes in v7:
time: 140 us; the launch traced here: 139 us
  Pallas kernels  60.1 us (43%)
  starting transfers between devices  42.3 us (30%)
  waiting for transfers between devices  35.2 us (25%)
    ppermute x8, starting transfers between devices, exchange(): return lax.ppermute(block, 'stream', pairs if with_pair else others)  32.8 us
    ppermute x8, waiting for transfers between devices, exchange(): return lax.ppermute(block, 'stream', pairs if with_pair else others)  21.9 us
    ppermute x10, waiting for transfers between devices, around(): lax.ppermute(block, 'span', [((i + offset) % BLOCKS, i) for i in range(BL...  13.3 us
    pallas_call x2, Pallas kernels, solve_call(): pl.pallas_call(functools.partial(solve_body, more), out_shape=tuple(outs)...  12.3 us
    pallas_call x2, Pallas kernels, inner_call(): pl.pallas_call(inner_body, out_shape=PREDICTED, in_specs=[ANYWHERE] * 3 +...  9.96 us
    pallas_call x2, Pallas kernels, first_sweeps_call(): pl.pallas_call(first_sweeps_body, out_shape=(shape(*SUM), shape(3, NY, 12...  9.61 us
    ppermute x10, starting transfers between devices, around(): lax.ppermute(block, 'span', [((i + offset) % BLOCKS, i) for i in range(BL...  9.48 us
    pallas_call x2, Pallas kernels, other_call(): pl.pallas_call(other_body, out_shape=(shape(3, 1, NY, NZ), *[shape(*BLOCK...  8.03 us
  transfers between devices with their start and end apart: 18, of which 15 were waited for; matrix products, arithmetic and copies ran while one was open for 0% of the time, Pallas kernels for 24%

profile of v7, /device:TPU:7, one launch (start us, length us, event | category | flops | bytes accessed | tf_op | source)
XLA Modules:
  0.0 139.3 jit_solution(15375888513824864434)
XLA Ops:
  1.3 4.3 %pack.1 = (f32[9,128,128]{2,1,0:T(8,128)}, f32[9,128,128]{2,1,0:T(8,128)}, f32[128,128]{1,0:T(8,128)}, f32[8,128,128]{2,1,0:T(8,128)}) custom-call(s32[3]{0:T(128)} %add_convert_fusion.flags.refs_0_, f32[3,8,128,128]{3,2,1,0:T(8,128)} %vel.1, f32[8,128,128]{2,1,0:T(8,128)} %frac.1, f32[8,128,128]{2,1,0:T(8,128)} %refs_5_.1, f32[8,128,128]{2,1,0:T(8,128)} %old_far.1), custom_call_target="tpu_custom_call" | custom-call | tf_op jit(solution)/shard_map/pack/pallas_call | solution.py:701
  7.4 2.9 %collective-permute-done.1.after = f32[128,128]{1,0:T(8,128)S(1)} collective-permute-done((f32[128,128]{1,0:T(8,128)}, f32[128,128]{1,0:T(8,128)S(1)}, u32[]{:S(2)}, u32[]{:S(2)}) %collective-permute-start.1) | collective-permute-done | bytes 65568 | tf_op jit(solution)/shard_map/ppermute | solution.py:874
  12.8 7.6 %collective-permute-start.3 = (f32[9,128,128]{2,1,0:T(8,128)}, f32[9,128,128]{2,1,0:T(8,128)S(1)}, u32[]{:S(2)}, u32[]{:S(2)}) collective-permute-start(f32[9,128,128]{2,1,0:T(8,128)} %get-tuple-element.98), channel_id=1, source_target_pairs={{4,8},{8,4},{12,16},{16,12},{20,24},{24,20},{28,32},{32,28},{36,40... | collective-permute-start | bytes 1769480 | tf_op jit(solution)/shard_map/ppermute | solution.py:871
  20.4 5.0 %inner.2 = (f32[8,144,128]{2,1,0:T(8,128)S(1)}, f32[8,144,128]{2,1,0:T(8,128)S(1)}, f32[8,144,128]{2,1,0:T(8,128)S(1)}, f32[8,144,128]{2,1,0:T(8,128)S(1)}, f32[...) custom-call(f32[3,8,128,128]{3,2,1,0:T(8,128)S(1)} %copy-done, ...), custom_call_target="tpu_custom_call" | custom-call | flops 20000000 | bytes 16000000 | tf_op jit(solution)/shard_map/inner/pallas_call | solution.py:724
  26.1 2.6 %paired_side.2 = (f32[3,1,128,128]{3,2,1,0:T(8,128)S(1)}, f32[128,128]{1,0:T(8,128)S(1)}, f32[2,128,128]{2,1,0:T(8,128)S(1)}, f32[128,128]{1,0:T(8,128)S(1)}) custom-call(s32[3]{0:T(128)S(1)} %copy-done.9, f32[9,128,128]{2,1,0:T(8,128)S(1)} %collective-permute-done.2.message, f32[128,128]{1,0:T(8,128)S(1)} %get-tuple-element.86.sides, ...), custom_call_target="tpu_custom_call" | custom-call | flops 6000000 | bytes 6000000 | tf_op jit(solution)/shard_map/paired_side/pallas_call | solution.py:745
  28.7 5.8 %collective-permute-done.3.message = f32[9,128,128]{2,1,0:T(8,128)S(1)} collective-permute-done((f32[9,128,128]{2,1,0:T(8,128)}, f32[9,128,128]{2,1,0:T(8,128)S(1)}, u32[]{:S(2)}, u32[]{:S(2)}) %collective-permute-start.3) | collective-permute-done | bytes 589856 | tf_op jit(solution)/shard_map/ppermute | solution.py:871
  34.5 3.5 %other_side.2 = (f32[3,1,128,128]{3,2,1,0:T(8,128)S(1)}, f32[8,128,128]{2,1,0:T(8,128)S(1)}, f32[8,128,128]{2,1,0:T(8,128)S(1)}, f32[8,128,128]{2,1,0:T(8,128)S(...) custom-call(s32[3]{0:T(128)S(1)} %copy-done.9, f32[9,128,128]{2,1,0:T(8,128)S(1)} %collective-permute-done.3.message, ...), custom_call_target="tpu_custom_call" | custom-call | tf_op jit(solution)/shard_map/other_side/pallas_call | solution.py:759
  41.4 3.2 %collective-permute-done.5.c = f32[128,128]{1,0:T(8,128)S(1)} collective-permute-done((f32[128,128]{1,0:T(8,128)S(1)}, f32[128,128]{1,0:T(8,128)S(1)}, u32[]{:S(2)}, u32[]{:S(2)}) %collective-permute-start.5) | collective-permute-done | bytes 65568 | tf_op jit(solution)/shard_map/ppermute | solution.py:874
  45.7 7.9 %collective-permute-start.7 = (f32[8,128,128]{2,1,0:T(8,128)S(1)}, f32[8,128,128]{2,1,0:T(8,128)S(1)}, u32[]{:S(2)}, u32[]{:S(2)}) collective-permute-start(f32[8,128,128]{2,1,0:T(8,128)S(1)} %get-tuple-element.109), channel_id=1, source_target_pairs={{4,8},{8,4},{12,16},{16,12},{20,24},{24,20},{28,32},{32,28},{36,40... | collective-permute-start | bytes 1572872 | tf_op jit(solution)/shard_map/ppermute | solution.py:871
  56.1 3.2 %collective-permute-done.8.paired = f32[8,128,128]{2,1,0:T(8,128)S(1)} collective-permute-done((f32[8,128,128]{2,1,0:T(8,128)S(1)}, f32[8,128,128]{2,1,0:T(8,128)S(1)}, u32[]{:S(2)}, u32[]{:S(2)}) %collective-permute-start.8) | collective-permute-done | bytes 524320 | tf_op jit(solution)/shard_map/ppermute | solution.py:871
  61.1 4.8 %first_sweeps.2 = (f32[10,144,128]{2,1,0:T(8,128)S(1)}, f32[3,128,128]{2,1,0:T(8,128)S(1)}) custom-call(s32[3]{0:T(128)S(1)} %copy-done.9, f32[7,8,144,128]{3,2,1,0:T(8,128)S(1)} %get-tuple-element.112.given_U, f32[7,7,144,128]{3,2,1,0:T(8,128)S(1)} %get-tuple-element.115.given_side, f32[3,128,128]{2,1,0:T(8,128)S(1)} %get-tuple-element.116.given_E), custom_call_target="tpu_custom_call" | custom-call | flops 10000000 | bytes 14000000 | tf_op jit(solution)/shard_map/first_sweeps/pallas_call | solution.py:830
  67.0 6.2 %solve.2 = (f32[3,8,128,128]{3,2,1,0:T(8,128)S(1)}, f32[8,128,128]{2,1,0:T(8,128)}, f32[9,128,128]{2,1,0:T(8,128)S(1)}, f32[9,128,128]{2,1,0:T(8,128)S(1)}, f32[...) custom-call(s32[3]{0:T(128)S(1)} %copy-done.9, f32[3,8,128,128]{3,2,1,0:T(8,128)S(1)} %get-tuple-element.87.refs_7_.refs_1_, ...), custom_call_target="tpu_custom_call" | custom-call | tf_op jit(solution)/shard_map/solve/pallas_call | solution.py:846
  75.0 2.9 %collective-permute-done.10.after = f32[128,128]{1,0:T(8,128)S(1)} collective-permute-done((f32[128,128]{1,0:T(8,128)S(1)}, f32[128,128]{1,0:T(8,128)S(1)}, u32[]{:S(2)}, u32[]{:S(2)}) %collective-permute-start.10) | collective-permute-done | bytes 65568 | tf_op jit(solution)/shard_map/ppermute | solution.py:874
  78.3 7.7 %collective-permute-start.12 = (f32[9,128,128]{2,1,0:T(8,128)S(1)}, f32[9,128,128]{2,1,0:T(8,128)S(1)}, u32[]{:S(2)}, u32[]{:S(2)}) collective-permute-start(f32[9,128,128]{2,1,0:T(8,128)S(1)} %get-tuple-element.136), channel_id=1, source_target_pairs={{4,8},{8,4},{12,16},{16,12},{20,24},{24,20},{28,32},{32,28},{36,40... | collective-permute-start | bytes 1769480 | tf_op jit(solution)/shard_map/ppermute | solution.py:871
  86.0 5.0 %inner.3 = (f32[8,144,128]{2,1,0:T(8,128)S(1)}, f32[8,144,128]{2,1,0:T(8,128)S(1)}, f32[8,144,128]{2,1,0:T(8,128)S(1)}, f32[8,144,128]{2,1,0:T(8,128)S(1)}, f32[...) custom-call(f32[3,8,128,128]{3,2,1,0:T(8,128)S(1)} %get-tuple-elemen, ...), custom_call_target="tpu_custom_call" | custom-call | flops 20000000 | bytes 16000000 | tf_op jit(solution)/shard_map/inner/pallas_call | solution.py:724
  92.8 2.6 %paired_side.3 = (f32[3,1,128,128]{3,2,1,0:T(8,128)S(1)}, f32[128,128]{1,0:T(8,128)S(1)}, f32[2,128,128]{2,1,0:T(8,128)S(1)}, f32[128,128]{1,0:T(8,128)S(1)}) custom-call(s32[3]{0:T(128)S(1)} %copy-done.9, f32[9,128,128]{2,1,0:T(8,128)S(1)} %collective-permute-done.11.message, f32[128,128]{1,0:T(8,128)S(1)} %get-tuple-element.124.sides, ...), custom_call_target="tpu_custom_call" | custom-call | flops 6000000 | bytes 6000000 | tf_op jit(solution)/shard_map/paired_side/pallas_call | solution.py:745
  95.4 5.0 %collective-permute-done.12.message = f32[9,128,128]{2,1,0:T(8,128)S(1)} collective-permute-done((f32[9,128,128]{2,1,0:T(8,128)S(1)}, f32[9,128,128]{2,1,0:T(8,128)S(1)}, u32[]{:S(2)}, u32[]{:S(2)}) %collective-permute-start.12) | collective-permute-done | bytes 589856 | tf_op jit(solution)/shard_map/ppermute | solution.py:871
  100.4 4.5 %other_side.3 = (f32[3,1,128,128]{3,2,1,0:T(8,128)S(1)}, f32[8,128,128]{2,1,0:T(8,128)}, f32[8,128,128]{2,1,0:T(8,128)S(1)}, f32[8,128,128]{2,1,0:T(8,128)S(1)},...) custom-call(s32[3]{0:T(128)S(1)} %copy-done.9, f32[9,128,128]{2,1,0:T(8,128)S(1)} %collective-permute-done.12.message, ...), custom_call_target="tpu_custom_call" | custom-call | tf_op jit(solution)/shard_map/other_side/pallas_call | solution.py:759
  107.6 3.3 %collective-permute-done.14.c = f32[128,128]{1,0:T(8,128)S(1)} collective-permute-done((f32[128,128]{1,0:T(8,128)S(1)}, f32[128,128]{1,0:T(8,128)S(1)}, u32[]{:S(2)}, u32[]{:S(2)}) %collective-permute-start.14) | collective-permute-done | bytes 65568 | tf_op jit(solution)/shard_map/ppermute | solution.py:874
  112.0 7.7 %collective-permute-start.16 = (f32[8,128,128]{2,1,0:T(8,128)S(1)}, f32[8,128,128]{2,1,0:T(8,128)S(1)}, u32[]{:S(2)}, u32[]{:S(2)}) collective-permute-start(f32[8,128,128]{2,1,0:T(8,128)S(1)} %get-tuple-element.148), channel_id=1, source_target_pairs={{4,8},{8,4},{12,16},{16,12},{20,24},{24,20},{28,32},{32,28},{36,40... | collective-permute-start | bytes 1572872 | tf_op jit(solution)/shard_map/ppermute | solution.py:871
  119.8 2.5 %own_terms.3 = (f32[7,8,144,128]{3,2,1,0:T(8,128)S(1)}, f32[3,128,128]{2,1,0:T(8,128)S(1)}) custom-call(f32[8,128,128]{2,1,0:T(8,128)S(1)} %get-tuple-element.149.source, f32[128,128]{1,0:T(8,128)S(1)} %get-tuple-element.150.far, bf16[512,1024]{1,0:T(8,128)(2,1)S(1)} %copy-done.2), custom_call_target="tpu_custom_call" | custom-call | flops 1000000000 | bytes 12000000 | tf_op jit(solution)/shard_map/own_terms/pallas_call | solution.py:800
  122.3 3.4 %collective-permute-done.17.paired = f32[8,128,128]{2,1,0:T(8,128)S(1)} collective-permute-done((f32[8,128,128]{2,1,0:T(8,128)S(1)}, f32[8,128,128]{2,1,0:T(8,128)S(1)}, u32[]{:S(2)}, u32[]{:S(2)}) %collective-permute-start.17) | collective-permute-done | bytes 524320 | tf_op jit(solution)/shard_map/ppermute | solution.py:871
  127.4 4.8 %first_sweeps.3 = (f32[10,144,128]{2,1,0:T(8,128)S(1)}, f32[3,128,128]{2,1,0:T(8,128)S(1)}) custom-call(s32[3]{0:T(128)S(1)} %copy-done.9, f32[7,8,144,128]{3,2,1,0:T(8,128)S(1)} %get-tuple-element.151.given_U, f32[7,7,144,128]{3,2,1,0:T(8,128)S(1)} %get-tuple-element.154.given_side, f32[3,128,128]{2,1,0:T(8,128)S(1)} %get-tuple-element.155.given_E), custom_call_target="tpu_custom_call" | custom-call | flops 10000000 | bytes 14000000 | tf_op jit(solution)/shard_map/first_sweeps/pallas_call | solution.py:830
  133.3 6.0 %solve.3 = (f32[3,8,128,128]{3,2,1,0:T(8,128)}, f32[8,128,128]{2,1,0:T(8,128)}) custom-call(s32[3]{0:T(128)S(1)} %copy-done.9, f32[3,8,128,128]{3,2,1,0:T(8,128)S(1)} %get-tuple-element.125.refs_7_.refs_1_, f32[3,1,128,128]{3,2,1,0:T(8,128)S(1)} %get-tuple-element.135.refs_2_, f32[3,1,128,128]{3,2,1,0:T(8,128)S(1)} %get-tuple-element.142.refs_3_, ...), custom_call_target="tpu_custom_call" | custom-call | tf_op jit(solution)/shard_map/solve/pallas_call | solution.py:846
  (55 shorter events, 25.9 us)
Async XLA Ops:
  1.3 19.2 %copy-start = (f32[3,8,128,128]{3,2,1,0:T(8,128)S(1)}, f32[3,8,128,128]{3,2,1,0:T(8,128)}, u32[]{:S(2)}) copy-start(f32[3,8,128,128]{3,2,1,0:T(8,128)} %vel.1) | copy-start | bytes 4718596
  1.3 19.2 %copy-start.1 = (f32[2,128,128]{2,1,0:T(8,128)S(1)}, f32[2,128,128]{2,1,0:T(8,128)}, u32[]{:S(2)}) copy-start(f32[2,128,128]{2,1,0:T(8,128)} %constant.28.clone.moments) | copy-start | bytes 393220
  1.3 19.2 %copy-start.3 = (f32[8,128,128]{2,1,0:T(8,128)S(1)}, f32[8,128,128]{2,1,0:T(8,128)}, u32[]{:S(2)}) copy-start(f32[8,128,128]{2,1,0:T(8,128)} %frac.1) | copy-start | bytes 1572868
  5.6 4.7 %collective-permute-start.1 = (f32[128,128]{1,0:T(8,128)}, f32[128,128]{1,0:T(8,128)S(1)}, u32[]{:S(2)}, u32[]{:S(2)}) collective-permute-start(f32[128,128]{1,0:T(8,128)} %get-tuple-element.83), channel_id=1, source_target_pairs={{1,0},{2,1},{3,2},{0,3},{5,4},{6,5},{7,6},{4,7},{9,8},{10,9},{11,1... | collective-permute-start | bytes 196616 | tf_op jit(solution)/shard_map/ppermute | solution.py:874
  6.3 4.0 %collective-permute-start = (f32[128,128]{1,0:T(8,128)}, f32[128,128]{1,0:T(8,128)S(1)}, u32[]{:S(2)}, u32[]{:S(2)}) collective-permute-start(f32[128,128]{1,0:T(8,128)} %get-tuple-element.83), channel_id=1, source_target_pairs={{3,0},{0,1},{1,2},{2,3},{7,4},{4,5},{5,6},{6,7},{11,8},{8,9},{9,10... | collective-permute-start | bytes 196616 | tf_op jit(solution)/shard_map/ppermute | solution.py:874
  11.0 14.9 %copy-start.10 = (f32[2,128]{1,0:T(2,128)S(1)}, f32[2,128]{1,0:T(2,128)}, u32[]{:S(2)}) copy-start(f32[2,128]{1,0:T(2,128)} %param.12) | copy-start | bytes 3076
  11.1 15.0 %copy-start.9 = (s32[3]{0:T(128)S(1)}, s32[3]{0:T(128)}, u32[]{:S(2)}) copy-start(s32[3]{0:T(128)} %add_convert_fusion.flags.refs_0_) | copy-start | bytes 40
  11.1 14.9 %collective-permute-start.2 = (f32[9,128,128]{2,1,0:T(8,128)}, f32[9,128,128]{2,1,0:T(8,128)S(1)}, u32[]{:S(2)}, u32[]{:S(2)}) collective-permute-start(f32[9,128,128]{2,1,0:T(8,128)} %get-tuple-element.88), channel_id=1, source_target_pairs={{0,4},{4,0},{8,12},{12,8},{16,20},{20,16},{24,28},{28,24},{32,36},... | collective-permute-start | bytes 1769480 | tf_op jit(solution)/shard_map/ppermute | solution.py:871
  12.8 21.7 %collective-permute-start.3 = (f32[9,128,128]{2,1,0:T(8,128)}, f32[9,128,128]{2,1,0:T(8,128)S(1)}, u32[]{:S(2)}, u32[]{:S(2)}) collective-permute-start(f32[9,128,128]{2,1,0:T(8,128)} %get-tuple-element.98), channel_id=1, source_target_pairs={{4,8},{8,4},{12,16},{16,12},{20,24},{24,20},{28,32},{32,28},{36,40... | collective-permute-start | bytes 1769480 | tf_op jit(solution)/shard_map/ppermute | solution.py:871
  38.0 15.6 %copy-start.2 = (bf16[512,1024]{1,0:T(8,128)(2,1)S(1)}, bf16[512,1024]{1,0:T(8,128)(2,1)}, u32[]{:S(2)}) copy-start(bf16[512,1024]{1,0:T(8,128)(2,1)} %constant.30.clone.table.refs_7_) | copy-start | bytes 3145732
  38.0 3.4 %collective-permute-start.6 = (f32[128,128]{1,0:T(8,128)S(1)}, f32[128,128]{1,0:T(8,128)S(1)}, u32[]{:S(2)}, u32[]{:S(2)}) collective-permute-start(f32[128,128]{1,0:T(8,128)S(1)} %get-tuple-element.106.a), channel_id=1, source_target_pairs={{3,0},{0,1},{1,2},{2,3},{7,4},{4,5},{5,6},{6,7},{11,8},{8,9},{9,10... | collective-permute-start | bytes 196616 | tf_op jit(solution)/shard_map/ppermute | solution.py:874
  40.1 4.5 %collective-permute-start.5 = (f32[128,128]{1,0:T(8,128)S(1)}, f32[128,128]{1,0:T(8,128)S(1)}, u32[]{:S(2)}, u32[]{:S(2)}) collective-permute-start(f32[128,128]{1,0:T(8,128)S(1)} %get-tuple-element.106.a), channel_id=1, source_target_pairs={{2,0},{3,1},{0,2},{1,3},{6,4},{7,5},{4,6},{5,7},{10,8},{11,9},{8,1... | collective-permute-start | bytes 196616 | tf_op jit(solution)/shard_map/ppermute | solution.py:874
  41.3 3.8 %collective-permute-start.4 = (f32[128,128]{1,0:T(8,128)S(1)}, f32[128,128]{1,0:T(8,128)S(1)}, u32[]{:S(2)}, u32[]{:S(2)}) collective-permute-start(f32[128,128]{1,0:T(8,128)S(1)} %get-tuple-element.106.a), channel_id=1, source_target_pairs={{1,0},{2,1},{3,2},{0,3},{5,4},{6,5},{7,6},{4,7},{9,8},{10,9},{11,1... | collective-permute-start | bytes 196616 | tf_op jit(solution)/shard_map/ppermute | solution.py:874
  45.6 13.8 %collective-permute-start.8 = (f32[8,128,128]{2,1,0:T(8,128)S(1)}, f32[8,128,128]{2,1,0:T(8,128)S(1)}, u32[]{:S(2)}, u32[]{:S(2)}) collective-permute-start(f32[8,128,128]{2,1,0:T(8,128)S(1)} %get-tuple-element.113), channel_id=1, source_target_pairs={{0,4},{4,0},{8,12},{12,8},{16,20},{20,16},{24,28},{28,24},{32,36},... | collective-permute-start | bytes 1572872 | tf_op jit(solution)/shard_map/ppermute | solution.py:871
  45.7 21.3 %collective-permute-start.7 = (f32[8,128,128]{2,1,0:T(8,128)S(1)}, f32[8,128,128]{2,1,0:T(8,128)S(1)}, u32[]{:S(2)}, u32[]{:S(2)}) collective-permute-start(f32[8,128,128]{2,1,0:T(8,128)S(1)} %get-tuple-element.109), channel_id=1, source_target_pairs={{4,8},{8,4},{12,16},{16,12},{20,24},{24,20},{28,32},{32,28},{36,40... | collective-permute-start | bytes 1572872 | tf_op jit(solution)/shard_map/ppermute | solution.py:871
  73.3 4.6 %collective-permute-start.10 = (f32[128,128]{1,0:T(8,128)S(1)}, f32[128,128]{1,0:T(8,128)S(1)}, u32[]{:S(2)}, u32[]{:S(2)}) collective-permute-start(f32[128,128]{1,0:T(8,128)S(1)} %get-tuple-element.121), channel_id=1, source_target_pairs={{1,0},{2,1},{3,2},{0,3},{5,4},{6,5},{7,6},{4,7},{9,8},{10,9},{11,1... | collective-permute-start | bytes 196616 | tf_op jit(solution)/shard_map/ppermute | solution.py:874
  73.9 4.0 %collective-permute-start.9 = (f32[128,128]{1,0:T(8,128)S(1)}, f32[128,128]{1,0:T(8,128)S(1)}, u32[]{:S(2)}, u32[]{:S(2)}) collective-permute-start(f32[128,128]{1,0:T(8,128)S(1)} %get-tuple-element.121), channel_id=1, source_target_pairs={{3,0},{0,1},{1,2},{2,3},{7,4},{4,5},{5,6},{6,7},{11,8},{8,9},{9,10... | collective-permute-start | bytes 196616 | tf_op jit(solution)/shard_map/ppermute | solution.py:874
  78.2 14.6 %collective-permute-start.11 = (f32[9,128,128]{2,1,0:T(8,128)S(1)}, f32[9,128,128]{2,1,0:T(8,128)S(1)}, u32[]{:S(2)}, u32[]{:S(2)}) collective-permute-start(f32[9,128,128]{2,1,0:T(8,128)S(1)} %get-tuple-element.126), channel_id=1, source_target_pairs={{0,4},{4,0},{8,12},{12,8},{16,20},{20,16},{24,28},{28,24},{32,36},... | collective-permute-start | bytes 1769480 | tf_op jit(solution)/shard_map/ppermute | solution.py:871
  78.3 22.1 %collective-permute-start.12 = (f32[9,128,128]{2,1,0:T(8,128)S(1)}, f32[9,128,128]{2,1,0:T(8,128)S(1)}, u32[]{:S(2)}, u32[]{:S(2)}) collective-permute-start(f32[9,128,128]{2,1,0:T(8,128)S(1)} %get-tuple-element.136), channel_id=1, source_target_pairs={{4,8},{8,4},{12,16},{16,12},{20,24},{24,20},{28,32},{32,28},{36,40... | collective-permute-start | bytes 1769480 | tf_op jit(solution)/shard_map/ppermute | solution.py:871
  104.9 2.7 %collective-permute-start.15 = (f32[128,128]{1,0:T(8,128)S(1)}, f32[128,128]{1,0:T(8,128)S(1)}, u32[]{:S(2)}, u32[]{:S(2)}) collective-permute-start(f32[128,128]{1,0:T(8,128)S(1)} %get-tuple-element.145.a), channel_id=1, source_target_pairs={{3,0},{0,1},{1,2},{2,3},{7,4},{4,5},{5,6},{6,7},{11,8},{8,9},{9,10... | collective-permute-start | bytes 196616 | tf_op jit(solution)/shard_map/ppermute | solution.py:874
  105.4 5.4 %collective-permute-start.14 = (f32[128,128]{1,0:T(8,128)S(1)}, f32[128,128]{1,0:T(8,128)S(1)}, u32[]{:S(2)}, u32[]{:S(2)}) collective-permute-start(f32[128,128]{1,0:T(8,128)S(1)} %get-tuple-element.145.a), channel_id=1, source_target_pairs={{2,0},{3,1},{0,2},{1,3},{6,4},{7,5},{4,6},{5,7},{10,8},{11,9},{8,1... | collective-permute-start | bytes 196616 | tf_op jit(solution)/shard_map/ppermute | solution.py:874
  107.6 3.8 %collective-permute-start.13 = (f32[128,128]{1,0:T(8,128)S(1)}, f32[128,128]{1,0:T(8,128)S(1)}, u32[]{:S(2)}, u32[]{:S(2)}) collective-permute-start(f32[128,128]{1,0:T(8,128)S(1)} %get-tuple-element.145.a), channel_id=1, source_target_pairs={{1,0},{2,1},{3,2},{0,3},{5,4},{6,5},{7,6},{4,7},{9,8},{10,9},{11,1... | collective-permute-start | bytes 196616 | tf_op jit(solution)/shard_map/ppermute | solution.py:874
  111.9 13.8 %collective-permute-start.17 = (f32[8,128,128]{2,1,0:T(8,128)S(1)}, f32[8,128,128]{2,1,0:T(8,128)S(1)}, u32[]{:S(2)}, u32[]{:S(2)}) collective-permute-start(f32[8,128,128]{2,1,0:T(8,128)S(1)} %get-tuple-element.152), channel_id=1, source_target_pairs={{0,4},{4,0},{8,12},{12,8},{16,20},{20,16},{24,28},{28,24},{32,36},... | collective-permute-start | bytes 1572872 | tf_op jit(solution)/shard_map/ppermute | solution.py:871
  112.0 21.3 %collective-permute-start.16 = (f32[8,128,128]{2,1,0:T(8,128)S(1)}, f32[8,128,128]{2,1,0:T(8,128)S(1)}, u32[]{:S(2)}, u32[]{:S(2)}) collective-permute-start(f32[8,128,128]{2,1,0:T(8,128)S(1)} %get-tuple-element.148), channel_id=1, source_target_pairs={{4,8},{8,4},{12,16},{16,12},{20,24},{24,20},{28,32},{32,28},{36,40... | collective-permute-start | bytes 1572872 | tf_op jit(solution)/shard_map/ppermute | solution.py:871
  (5 other events, 43.1 us)
